TPU v7x, 256 devices: a whole 4x4x8 slice. The times are simulated.
256 devices in a mesh: det: 4 (over x_hi, core), tm: 64 (over y, z, x_lo).
Axes of the slice: x: 4 (x_hi: 2, x_lo: 2; x = x_hi * 2 + x_lo), y: 4, z: 8, core: 2. Of those that a mesh axis runs over, the one named last changes fastest.
Arguments:
- sky_map: bfloat16 [128, 3, 128, 128], P('tm', None, 'det'), may hold values from -6 to 6
- tile_home: int32 [128], replicated, may hold values from 0 to 127, as said below
- piece_tiles: int32 [4, 64, 32], P('det', 'tm'), may hold values from 0 to 127, as said below
- run_slot: int32 [32, 1024], P('det', 'tm'), may hold values from 0 to 31
- hit_row: int32 [32, 131072], P('det', 'tm'), may hold values from 0 to 126
- hit_col: int32 [32, 131072], P('det', 'tm'), may hold values from 0 to 126
- frac_row: bfloat16 [32, 131072], P('det', 'tm'), may hold values from 0 to 1
- frac_col: bfloat16 [32, 131072], P('det', 'tm'), may hold values from 0 to 1
- angle: float32 [32, 131072], P('det', 'tm'), may hold values from -3.140625 to 3.140625
- noise_coef: float32 [32, 1025], P('det'), may hold values from -0.3 to 0.3
Outputs:
- normal_map: float32 [128, 3, 128, 128], P('tm', None, 'det')
Inputs may be any that keep to these rules, and one draw needn't show every extreme that they name: A permutation: tile g lies in row tile_home[g] of sky_map. `piece_tiles`: the 32 tiles listed by one piece are distinct, and at most 1 of them lie in rows of one index of tm (rows o * 2 to o * 2 + 1 of sky_map); every piece has exactly 1 tile in each index of tm that it reads from.
All inputs are finite; a program needn't handle non-finite values.
Results may differ from a plain program's by a relative error of at most 0.0048.
Values may be sent and summed in bfloat16 or wider, within the bound.
A program may use at most 128 MiB of HBM per device.

v0:
```python
import math

import jax
import jax.numpy as jnp
from jax import lax
from jax.sharding import PartitionSpec as P

LISTED = 32


block_cols = 128
group_runs = 32


def extended_2(cells, sides, width):
    for axis, dim in sides:
        count = lax.axis_size(axis)
        ends = count - 1
        head = lax.slice_in_dim(cells, 0, width, axis=dim)
        tail = lax.slice_in_dim(cells, cells.shape[dim] - width, cells.shape[dim], axis=dim)
        cells = jnp.concatenate(
            [
                lax.ppermute(tail, axis, [(i, (i + 1) % count) for i in range(ends)]),
                cells,
                lax.ppermute(head, axis, [((i + 1) % count, i) for i in range(ends)]),
            ],
            axis=dim,
        )
    return cells


def joined_along(parts, dim):
    shape = list(parts.shape[1:])
    shape[dim] *= parts.shape[0]
    return jnp.moveaxis(parts, 0, dim).reshape(shape)


def sent_to_all(x, axis):
    peers = lax.axis_size(axis)
    return lax.all_to_all(jnp.broadcast_to(x[None], (peers, *x.shape)), axis, 0, 0, tiled=True)


def gathered_copies(x, axis, dim):
    return joined_along(sent_to_all(x, axis), dim)


def cut_along(x, dim, peers):
    before, after = (x.shape[:dim], x.shape[dim + 1 :])
    return jnp.moveaxis(x.reshape(*before, peers, -1, *after), dim, 0)


def summed_on_arrival(x, axis, dim):
    peers = lax.axis_size(axis)
    parts = lax.all_to_all(cut_along(x, dim, peers), axis, 0, 0, tiled=True)
    return jnp.sum(parts, axis=0)


def positions_of(piece_list, tile_home):
    table_rows = jnp.arange(tile_home.shape[0], dtype=jnp.int32)
    matched = piece_list[:, None] == table_rows[None, :]
    return jnp.sum(jnp.where(matched, tile_home[None, :], 0), axis=1)


def run_weights(pixel_index, upper_frac, side_len):
    lower_weight = (1.0 - upper_frac.astype(jnp.float32)).astype(jnp.bfloat16)
    pixels = lax.broadcasted_iota(jnp.int32, pixel_index.shape + (side_len,), pixel_index.ndim)
    zero_value = jnp.zeros((), jnp.bfloat16)
    low_part = jnp.where(pixels == pixel_index[..., None], lower_weight[..., None], zero_value)
    high_part = jnp.where(pixels == pixel_index[..., None] + 1, upper_frac[..., None], zero_value)
    return low_part + high_part


def responses(angles):
    twice = 2.0 * angles
    return jnp.stack([jnp.ones_like(twice), jnp.cos(twice), jnp.sin(twice)], axis=1)


def banded(signal, noise_coef):
    det_count = signal.shape[0]
    half_band = noise_coef.shape[1] - 1
    reach_blocks = half_band // block_cols
    span_cols = (2 * reach_blocks + 1) * block_cols
    weights = jnp.concatenate([noise_coef[:, :1] + 1.0, noise_coef[:, 1:]], axis=1)
    zero_pad = jnp.zeros((det_count, block_cols - 1), jnp.float32)
    kernel_row = jnp.concatenate(
        [
            zero_pad,
            weights[:, ::-1],
            weights[:, 1:],
            zero_pad,
            jnp.zeros((det_count, 1), jnp.float32),
        ],
        axis=1,
    )
    period = span_cols + block_cols
    tiled_rows = jnp.tile(kernel_row, (1, block_cols))[:, : block_cols * (period - 1)]
    tiled_rows = tiled_rows.reshape(det_count, block_cols, period - 1)
    matrix = tiled_rows[:, :, block_cols - 1 : block_cols - 1 + span_cols]
    matrix = matrix.reshape(det_count, block_cols, 2 * reach_blocks + 1, block_cols)
    extended = extended_2(signal, (("tm", 1),), half_band)
    block_count = signal.shape[1] // block_cols
    blocks = extended.reshape(det_count, block_count + 2 * reach_blocks, block_cols)
    stacked = jnp.stack(
        [blocks[:, offset : offset + block_count] for offset in range(2 * reach_blocks + 1)], axis=1
    )
    result = jnp.einsum(
        "diml,dmnl->dni",
        matrix,
        stacked,
        precision=lax.Precision.HIGHEST,
        preferred_element_type=jnp.float32,
    )
    return result.reshape(det_count, block_count * block_cols)


def body(
    sky_map,
    tile_home,
    piece_tiles,
    run_slot,
    hit_row,
    hit_col,
    frac_row,
    frac_col,
    angle,
    noise_coef,
):
    owner_total = lax.axis_size("tm")
    tile_dev = sky_map.shape[0]
    side_len = sky_map.shape[3]
    per_owner = max(1, LISTED // owner_total)
    slot_total = owner_total * per_owner
    owned_tiles = gathered_copies(sky_map, "det", 2)
    position = positions_of(piece_tiles[0, 0], tile_home)
    owner_of = position // tile_dev
    local_slot = position % tile_dev
    listing = jnp.arange(LISTED, dtype=jnp.int32)
    earlier_same = (owner_of[:, None] == owner_of[None, :]) & (listing[:, None] > listing[None, :])
    rank_within = jnp.sum(earlier_same.astype(jnp.int32), axis=1)
    outbox_row = owner_of * per_owner + rank_within
    slot_rows = jnp.arange(slot_total, dtype=jnp.int32)
    asked_slot = (
        jnp.sum(
            jnp.where(slot_rows[:, None] == outbox_row[None, :], local_slot[None, :] + 1, 0), axis=1
        )
        - 1
    )
    served_slot = lax.all_to_all(asked_slot, "tm", split_axis=0, concat_axis=0, tiled=True)
    answer = jnp.take(owned_tiles, jnp.maximum(served_slot, 0), axis=0)
    answer = jnp.where((served_slot >= 0)[:, None, None, None], answer, jnp.zeros((), jnp.bfloat16))
    returned = lax.all_to_all(answer, "tm", split_axis=0, concat_axis=0, tiled=True)
    listed = jnp.take(returned, outbox_row, axis=0)
    det_local, time_local = hit_row.shape
    run_length = time_local // run_slot.shape[1]
    run_total = det_local * run_slot.shape[1]
    per_group = math.gcd(run_total, group_runs)
    group_total = run_total // per_group

    def grouped(values):
        return values.reshape(group_total, per_group, run_length)

    run_items = (
        run_slot.reshape(group_total, per_group),
        grouped(hit_row),
        grouped(hit_col),
        grouped(frac_row),
        grouped(frac_col),
        grouped(angle),
    )

    def project(items):
        slots, rows_at, cols_at, frac_rows, frac_cols, angles = items
        tiles = jnp.take(listed, slots, axis=0)
        row_weight = run_weights(rows_at, frac_rows, side_len).astype(jnp.float32)
        col_weight = run_weights(cols_at, frac_cols, side_len)
        partial_rows = jnp.einsum(
            "bpij,bsj->bpsi", tiles, col_weight, preferred_element_type=jnp.float32
        )
        values = jnp.sum(partial_rows * row_weight[:, None], axis=3)
        return jnp.sum(values * responses(angles), axis=1)

    signal = lax.map(project, run_items).reshape(det_local, time_local)
    filtered = banded(signal, noise_coef)

    def back_project(carry, items):
        slots, rows_at, cols_at, frac_rows, frac_cols, angles, filt_runs = items
        row_weight = run_weights(rows_at, frac_rows, side_len).astype(jnp.float32)
        col_weight = run_weights(cols_at, frac_cols, side_len)
        scaled = responses(angles) * filt_runs[:, None]
        weighted = (scaled[..., None] * row_weight[:, None]).astype(jnp.bfloat16)
        tile_terms = jnp.einsum(
            "bpsi,bsj->bpij", weighted, col_weight, preferred_element_type=jnp.float32
        )
        return (carry.at[slots].add(tile_terms), None)

    initial = jnp.zeros((LISTED, 3, side_len, side_len), jnp.float32)
    contrib, _ = lax.scan(back_project, initial, run_items + (grouped(filtered),))
    outbox = jnp.zeros((slot_total, 3, side_len, side_len), jnp.float32).at[outbox_row].set(contrib)
    arrived = lax.all_to_all(outbox, "tm", split_axis=0, concat_axis=0, tiled=True)
    summed = jnp.stack(
        [
            jnp.sum(jnp.where((served_slot == slot_id)[:, None, None, None], arrived, 0.0), axis=0)
            for slot_id in range(tile_dev)
        ]
    )
    return summed_on_arrival(summed, "det", 2)


def solution(mesh):
    placed = (
        P("tm", None, "det", None),
        P(),
        P("det", "tm", None),
        P("det", "tm"),
        P("det", "tm"),
        P("det", "tm"),
        P("det", "tm"),
        P("det", "tm"),
        P("det", "tm"),
        P("det", None),
    )
    return jax.shard_map(
        body, mesh=mesh, in_specs=placed, out_specs=P("tm", None, "det", None), check_vma=False
    )
```

profile of v0, /device:TPU:1, one launch (start us, length us, event | category | flops | bytes accessed | tf_op | source)
XLA Modules:
  0.0 764.5 jit_solution(1321152402810989350)
XLA Ops:
  0.0 0.8 select_reduce_fusion.3
  1.3 22.6 %all_to_all.26 = s32[64,1,1]{2,1,0:T(1,128)S(1)} all-to-all(s32[64,1,1]{2,1,0:T(1,128)S(1)} %copy.104), channel_id=1, replica_groups=mesh['det'=4,'tm'=64] {'tm'}, dimensions={0} | all-to-all | bytes 512 | tf_op jit(solution)/shard_map/all_to_all | solution.py:148
  23.9 1.5 broadcast_in_dim.205
  25.4 6.1 all-to-all-start.1
  31.5 1.2 maximum_reduce_fusion
  32.7 5.0 compare_reduce_fusion.3
  37.7 4.0 gather_fusion.1
  41.7 6.2 select_select_fusion
  48.0 6.0 all-to-all-start.2
  54.4 137.5 %all-to-all-done.2 = bf16[64,3,128,128]{3,2,1,0:T(8,128)(2,1)} async-done(((bf16[64,3,128,128]{3,2,1,0:T(8,128)(2,1)}), bf16[64,3,128,128]{3,2,1,0:T(8,128)(2,1)}, u32[]{:S(2)}, u32[]{:S(2)}) %all-to-all-start.2) | async-done | bytes 6291488 | tf_op jit(solution)/shard_map/all_to_all | solution.py:151
  191.9 3.9 gather_fusion.2
  195.9 2.0 broadcast_select_fusion
  197.9 59.7 %while.20 = (s32[]{:T(128)}, f32[4,32,128]{2,1,0:T(8,128)}, s32[4,32,128]{2,1,0:T(8,128)S(1)}, bf16[4,32,128]{2,1,0:T(8,128)(2,1)S(1)}, s32[4,32]{1,0:T(4,128)S(...) while((s32[]{:T(128)}, f32[4,32,128]{2,1,0:T(8,128)}, ...), condition=%wide.region_6.7_spmd, body=%wide.region_3.6_spmd.sunk | while | flops 415831328 | bytes 18305908 | solution.py:182
  198.1 2.3 fusion.85
  200.4 1.9 copy.135
  202.3 3.0 gather_fusion
  205.3 6.8 multiply_reduce_fusion.2
  212.2 0.6 bitcast_dynamic-update-slice_fusion.2
  213.0 2.3 fusion.85
  215.3 1.9 copy.135
  217.2 3.0 gather_fusion
  220.3 6.7 multiply_reduce_fusion.2
  227.9 2.3 fusion.85
  230.3 1.9 copy.135
  232.1 3.0 gather_fusion
  235.2 6.7 multiply_reduce_fusion.2
  242.9 2.3 fusion.85
  245.2 1.9 copy.135
  247.1 3.0 gather_fusion
  250.1 6.7 multiply_reduce_fusion.2
  257.6 0.9 reshape.439
  258.5 3.2 collective-permute-start
  261.7 1.3 collective-permute-start.1
  263.1 0.6 reverse
  264.5 3.9 slice.117
  268.4 8.5 %reshape.494 = f32[2358272]{0:T(1024)} reshape(f32[8,294784]{1,0:T(8,128)} %slice.117) | data formatting | bytes 18866176
  276.9 15.6 %reshape.441 = f32[8,128,2303]{2,1,0:T(8,128)} reshape(f32[2358272]{0:T(1024)} %reshape.494) | data formatting | bytes 18866176 | tf_op jit(solution)/shard_map/reshape | solution.py:97
  292.5 9.5 %slice.118 = f32[8,128,2176]{2,1,0:T(8,128)} slice(f32[8,128,2303]{2,1,0:T(8,128)} %reshape.441), slice={[0:8], [0:128], [127:2303]} | slice | bytes 17825792 | tf_op jit(solution)/shard_map/slice | solution.py:98
  302.0 9.2 %copy.122 = f32[8,128,2176]{1,2,0:T(8,128)} copy(f32[8,128,2176]{2,1,0:T(8,128)} %slice.118) | data formatting | bytes 17825792 | tf_op jit(solution)/shard_map/slice | solution.py:98
  311.6 7.3 fusion.69
  318.9 3.4 broadcast_in_dim.200
  322.3 116.8 %while.21 = (s32[]{:T(128)}, f32[32,3,128,128]{3,2,1,0:T(8,128)}, s32[4,32]{1,0:T(4,128)S(1)}, f32[4,32,128]{2,1,0:T(8,128)S(1)}, f32[4,32,128]{2,1,0:T(8,128)S(...) while((s32[]{:T(128)}, f32[32,3,128,128]{3,2,1,0:T(8,128)}, ...), condition=%wide.region_9.10_spmd, body=%wide.region_7.9_spmd.sunk | while | flops 415834208 | bytes 34128432 | solution.py:197
  322.6 4.6 fusion.90
  327.2 1.9 copy.136
  329.1 6.3 fusion.91
  335.4 16.1 %scatter_fusion = f32[32,3,128,128]{3,2,1,0:T(8,128)} fusion(f32[32,3,128,128]{3,2,1,0:T(8,128)} %get-tuple-element.376, s32[32]{0:T(128)S(1)} %fusion.89, f32[32,3,128,128]{3,2,1,0:T(8,128)} %fusion.91), kind=kCustom, calls=%fused_computation.3.clone.1 | custom fusion | flops 1572864 | bytes 18874496 | tf_op jit(solution)/shard_map/while/body/eval_jaxpr/scatter-add | solution.py:194
  351.8 4.6 fusion.90
  356.3 1.9 copy.136
  358.3 6.3 fusion.91
  364.6 16.1 %scatter_fusion = f32[32,3,128,128]{3,2,1,0:T(8,128)} fusion(f32[32,3,128,128]{3,2,1,0:T(8,128)} %get-tuple-element.376, s32[32]{0:T(128)S(1)} %fusion.89, f32[32,3,128,128]{3,2,1,0:T(8,128)} %fusion.91), kind=kCustom, calls=%fused_computation.3.clone.1 | custom fusion | flops 1572864 | bytes 18874496 | tf_op jit(solution)/shard_map/while/body/eval_jaxpr/scatter-add | solution.py:194
  381.0 4.6 fusion.90
  385.6 1.9 copy.136
  387.5 6.3 fusion.91
  393.8 16.1 %scatter_fusion = f32[32,3,128,128]{3,2,1,0:T(8,128)} fusion(f32[32,3,128,128]{3,2,1,0:T(8,128)} %get-tuple-element.376, s32[32]{0:T(128)S(1)} %fusion.89, f32[32,3,128,128]{3,2,1,0:T(8,128)} %fusion.91), kind=kCustom, calls=%fused_computation.3.clone.1 | custom fusion | flops 1572864 | bytes 18874496 | tf_op jit(solution)/shard_map/while/body/eval_jaxpr/scatter-add | solution.py:194
  410.2 4.6 fusion.90
  414.8 1.9 copy.136
  416.7 6.3 fusion.91
  423.0 16.1 %scatter_fusion = f32[32,3,128,128]{3,2,1,0:T(8,128)} fusion(f32[32,3,128,128]{3,2,1,0:T(8,128)} %get-tuple-element.376, s32[32]{0:T(128)S(1)} %fusion.89, f32[32,3,128,128]{3,2,1,0:T(8,128)} %fusion.91), kind=kCustom, calls=%fused_computation.3.clone.1 | custom fusion | flops 1572864 | bytes 18874496 | tf_op jit(solution)/shard_map/while/body/eval_jaxpr/scatter-add | solution.py:194
  439.1 6.2 broadcast_in_dim.199
  445.3 13.7 %scatter_fusion.1 = f32[64,3,128,128]{3,2,1,0:T(8,128)} fusion(f32[64,3,128,128]{3,2,1,0:T(8,128)} %broadcast_in_dim.199, s32[32]{0:T(128)S(1)} %fusion.67, f32[32,3,128,128]{3,2,1,0:T(8,128)} %get-tuple-element.100), kind=kCustom, calls=%fused_computation.4 | custom fusion | bytes 18874496 | tf_op jit(solution)/shard_map/scatter | solution.py:198
  458.9 286.6 %all_to_all.27 = f32[64,3,128,128]{3,2,1,0:T(8,128)S(1)} all-to-all(f32[64,3,128,128]{3,2,1,0:T(8,128)} %scatter_fusion.1), channel_id=1, replica_groups=mesh['det'=4,'tm'=64] {'tm'}, dimensions={0} | all-to-all | bytes 25165824 | tf_op jit(solution)/shard_map/all_to_all | solution.py:199
  745.5 2.8 select_reduce_fusion.1
  748.4 15.5 %all_to_all.28 = f32[4,2,3,32,128]{4,3,2,1,0:T(8,128)S(1)} all-to-all(f32[4,2,3,32,128]{4,3,2,1,0:T(8,128)S(1)} %copy.124), channel_id=1, replica_groups=mesh['det'=4,'tm'=64] {'det'}, dimensions={0} | all-to-all | bytes 786432 | tf_op jit(solution)/shard_map/all_to_all | solution.py:54
  763.8 0.7 reduce_sum.85
  (135 shorter events, 5.7 us)
Async XLA Ops:
  25.4 12.4 %all-to-all-start.1 = ((bf16[4,2,3,32,128]{4,3,2,1,0:T(8,128)(2,1)}), bf16[4,2,3,32,128]{4,3,2,1,0:T(8,128)(2,1)S(1)}, u32[]{:S(2)}, u32[]{:S(2)}) async-start(bf16[4,2,3,32,128]{4,3,2,1,0:T(8,128)(2,1)} %broadcast_in_dim.205), calls=%async_computation.1 | async-start | bytes 393216 | tf_op jit(solution)/shard_map/all_to_all | solution.py:40
  48.0 6.1 copy-start.6
  48.0 6.2 copy-start.4
  48.0 6.2 copy-start.5
  48.0 6.2 copy-start.3
  48.0 6.3 copy-start
  48.0 6.3 copy-start.1
  48.0 6.3 copy-start.2
  48.0 143.9 %all-to-all-start.2 = ((bf16[64,3,128,128]{3,2,1,0:T(8,128)(2,1)}), bf16[64,3,128,128]{3,2,1,0:T(8,128)(2,1)}, u32[]{:S(2)}, u32[]{:S(2)}) async-start(bf16[64,3,128,128]{3,2,1,0:T(8,128)(2,1)} %select_select_fusion), calls=%async_computation.2 | async-start | bytes 12582912 | tf_op jit(solution)/shard_map/all_to_all | solution.py:151
  258.5 52.8 %collective-permute-start = (f32[8,1024]{1,0:T(8,128)S(1)}, f32[8,1024]{1,0:T(8,128)S(1)}, u32[]{:S(2)}, u32[]{:S(2)}) collective-permute-start(f32[8,1024]{1,0:T(8,128)S(1)} %get-tuple-element.173), channel_id=1, source_target_pairs={{0,1},{1,2},{2,3},{3,4},{4,5},{5,6},{6,7},{7,8},{8,9},{9,10},{10,1... | collective-permute-start | bytes 98312 | tf_op jit(solution)/shard_map/ppermute | solution.py:23
  261.7 49.5 %collective-permute-start.1 = (f32[8,1024]{1,0:T(8,128)S(1)}, f32[8,1024]{1,0:T(8,128)S(1)}, u32[]{:S(2)}, u32[]{:S(2)}) collective-permute-start(f32[8,1024]{1,0:T(8,128)S(1)} %get-tuple-element.174), channel_id=1, source_target_pairs={{1,0},{2,1},{3,2},{4,3},{5,4},{6,5},{7,6},{8,7},{9,8},{10,9},{11,1... | collective-permute-start | bytes 98312 | tf_op jit(solution)/shard_map/ppermute | solution.py:25
  458.9 286.6 %copy-start.7 = (pred[64]{0:T(512)(128)(4,1)S(1)}, pred[64]{0:T(512)(128)(4,1)}, u32[]{:S(2)}) copy-start(pred[64]{0:T(512)(128)(4,1)} %get-tuple-element.103) | copy-start | bytes 196
  458.9 286.6 %copy-start.8 = (pred[64]{0:T(512)(128)(4,1)S(1)}, pred[64]{0:T(512)(128)(4,1)}, u32[]{:S(2)}) copy-start(pred[64]{0:T(512)(128)(4,1)} %get-tuple-element.104) | copy-start | bytes 196
where the time goes:
time: 766 us; the launch traced here: 764 us
  blocking collectives  325 us (42%)
  waiting for transfers between devices  138 us (18%)
  other arithmetic  113 us (15%)
  local copies, waits for them, and re-layouts  112 us (15%)
  matrix products  59.5 us (8%)
  starting transfers between devices  16.6 us (2%)
    all_to_all x1, blocking collectives, body(): lax.all_to_all(outbox, 'tm', split_axis=0, concat_axis=0, tiled=True)  287 us
    all_to_all x1, waiting for transfers between devices, body(): lax.all_to_all(answer, 'tm', split_axis=0, concat_axis=0, tiled=True)  137 us
    scatter-add x4, other arithmetic, back_project(): return (carry.at[slots].add(tile_terms), None)  64.5 us
    dot_general x4, matrix products, project(): jnp.einsum('bpij,bsj->bpsi', tiles, col_weight, preferred_element_type=jn...  27 us
    dot_general x4, matrix products, back_project(): jnp.einsum('bpsi,bsj->bpij', weighted, col_weight, preferred_element_type...  25.2 us
    all_to_all x1, blocking collectives, body(): lax.all_to_all(asked_slot, 'tm', split_axis=0, concat_axis=0, tiled=True)  22.6 us
    slice x2, local copies, waits for them, and re-layouts, banded(): matrix = tiled_rows[:, :, block_cols - 1:block_cols - 1 + span_cols]  18.7 us
    convert_element_type x4, other arithmetic, back_project(): row_weight = run_weights(rows_at, frac_rows, side_len).astype(jnp.float32)  18.3 us
  transfers between devices with their start and end apart: 4, of which 1 were waited for; matrix products, arithmetic and copies ran while one was open for 7% of the time, Pallas kernels for 0%

commit v1 on v0

v1 whole, which is shorter than its diff:
```python
import functools

import jax
import jax.numpy as jnp
from jax import lax
from jax.experimental import pallas as pl
from jax.experimental.pallas import tpu as pltpu
from jax.sharding import PartitionSpec as P

MESH = pl.DeviceIdType.MESH
NY, NZ, NX = 4, 8, 2
NB = NY * NX
DET, RUNS, LANE = 8, 16, 128
PIX = 128
STRIP = 32
LISTED = 32
REACH = 8
UNROLL = 4
PIECE_RUNS = DET * RUNS
ALL_RUNS = NZ * PIECE_RUNS
ANY = pl.BlockSpec(memory_space=pl.ANY)
VM = pl.BlockSpec(memory_space=pltpu.VMEM)
SM = pl.BlockSpec(memory_space=pltpu.SMEM)
DMA = pltpu.SemaphoreType.DMA
PEERS = [(dy, dx) for dy in range(NY) for dx in range(NX) if (dy, dx) != (0, 0)]


def place():
    det, tm = lax.axis_index("det"), lax.axis_index("tm")
    y, z, x = tm // (NZ * NX), (tm // NX) % NZ, tm % NX
    return det, tm, y, z, x


def tm_of(y, z, x):
    return (y * NZ + z) * NX + x


def core_of(det):
    return det + 1 - 2 * (det % 2)


def hi_of(det):
    return (det + 2) % 4


def greet(peers):
    barrier = pltpu.get_barrier_semaphore()
    for peer in peers:
        pl.semaphore_signal(barrier, inc=1, device_id=peer, device_id_type=MESH)
    pl.semaphore_wait(barrier, len(peers))


def remote(src, dst, send, recv, peer):
    return pltpu.make_async_remote_copy(
        src_ref=src, dst_ref=dst, send_sem=send, recv_sem=recv, device_id=peer, device_id_type=MESH
    )


def gather_kernel(
    q_ref, f_ref, w_ref, p_ref, tiles_ref, fo_ref, wo_ref, po_ref,
    q_own, f_own, w_own, p_own, load_sem, store_sem,
    ring_send, ring_recv, tile_send, tile_recv, core_send, core_recv, hi_send, hi_recv,
):
    det, tm, y, z, x = place()
    mine = y * NX + x
    partner, across = core_of(det), hi_of(det)
    right, left = tm_of(y, (z + 1) % NZ, x), tm_of(y, (z + NZ - 1) % NZ, x)

    def strip(slot, d):
        return tiles_ref.at[slot, :, :, pl.ds(d * STRIP, STRIP), :]

    def peer_slot(dy, dx, sign):
        return ((y + sign * dy + NY) % NY), ((x + dx) % NX)

    ins = (f_ref, w_ref, p_ref)
    outs = (fo_ref, wo_ref, po_ref)
    owns = (f_own, w_own, p_own)
    loads = [pltpu.make_async_copy(a, b, load_sem.at[i]) for i, (a, b) in enumerate(zip(ins + (q_ref,), owns + (q_own,)))]
    for copy in loads:
        copy.start()

    far = [tm_of(*(lambda s: (s[0], z, s[1]))(peer_slot(dy, dx, 1))) for dy, dx in PEERS]
    greet(
        [(det, right), (det, left), (partner, tm), (across, tm)]
        + [(det, t) for t in far]
    )

    reach = (NZ // 2, NZ // 2 - 1)

    def ring(direction, step, part):
        slot = (z + NZ - step) % NZ if direction == 0 else (z + step) % NZ
        src = ins[part] if step == 0 else outs[part].at[slot]
        return remote(
            src, outs[part].at[slot], ring_send.at[direction, step, part], ring_recv.at[direction, step, part],
            (det, right if direction == 0 else left),
        )

    def ring_in(direction, step, part):
        slot = (z + NZ - step - 1) % NZ if direction == 0 else (z + step + 1) % NZ
        return remote(
            ins[part], outs[part].at[slot], ring_send.at[direction, step, part], ring_recv.at[direction, step, part],
            (det, right if direction == 0 else left),
        )

    started = []

    def start(copy):
        copy.start()
        started.append(copy)

    start(remote(q_ref, strip(mine, det), hi_send, hi_recv, (across, tm)))
    for direction in (0, 1):
        for part in range(3):
            start(ring(direction, 0, part))
    for k, (dy, dx) in enumerate(PEERS):
        start(remote(q_ref, strip(mine, det), tile_send.at[0, k], tile_recv.at[0, k], (det, far[k])))
    start(remote(q_ref, strip(mine, det), core_send.at[0, NB - 1], core_recv.at[0, NB - 1], (partner, tm)))
    stores = []
    for i, copy in enumerate(loads):
        copy.wait()
        dst = outs[i].at[z] if i < 3 else strip(mine, det)
        store = pltpu.make_async_copy((owns + (q_own,))[i], dst, store_sem.at[i])
        store.start()
        stores.append(store)

    remote(q_ref, strip(mine, across), hi_send, hi_recv, (across, tm)).wait_recv()
    for k, (dy, dx) in enumerate(PEERS):
        start(remote(strip(mine, across), strip(mine, across), tile_send.at[1, k], tile_recv.at[1, k], (det, far[k])))
    start(
        remote(strip(mine, across), strip(mine, across), core_send.at[1, NB - 1], core_recv.at[1, NB - 1], (partner, tm))
    )

    def ring_step(step):
        for part in range(3):
            for direction in (0, 1):
                if step < reach[direction]:
                    ring_in(direction, step, part).wait_recv()
                    if step + 1 < reach[direction]:
                        start(ring(direction, step + 1, part))

    def tile_step(half):
        d = det if half == 0 else across
        for k, (dy, dx) in enumerate(PEERS):
            yy, xx = peer_slot(dy, dx, -1)
            slot = yy * NX + xx
            remote(q_ref, strip(slot, d), tile_send.at[half, k], tile_recv.at[half, k], (det, far[k])).wait_recv()
            start(remote(strip(slot, d), strip(slot, d), core_send.at[half, k], core_recv.at[half, k], (partner, tm)))

    ring_step(0)
    tile_step(0)
    ring_step(1)
    tile_step(1)
    ring_step(2)
    ring_step(3)
    for half in (0, 1):
        d = partner if half == 0 else hi_of(partner)
        for k in range(NB):
            if k < NB - 1:
                yy, xx = peer_slot(*PEERS[k], -1)
                slot = yy * NX + xx
            else:
                slot = mine
            remote(q_ref, strip(slot, d), core_send.at[half, k], core_recv.at[half, k], (partner, tm)).wait_recv()
    for store in stores:
        store.wait()
    for copy in started:
        copy.wait_send()


def gather_all(quarter, floats, fracs, positions):
    bf, f32, i32 = jnp.bfloat16, jnp.float32, jnp.int32
    half = (2, 3, STRIP, PIX)
    return pl.pallas_call(
        gather_kernel,
        out_shape=(
            jax.ShapeDtypeStruct((NB, 2, 3, PIX, PIX), bf),
            jax.ShapeDtypeStruct((NZ, *floats.shape), f32),
            jax.ShapeDtypeStruct((NZ, *fracs.shape), bf),
            jax.ShapeDtypeStruct((NZ, *positions.shape), i32),
        ),
        in_specs=[ANY] * 4,
        out_specs=(ANY,) * 4,
        scratch_shapes=[
            pltpu.VMEM(half, bf),
            pltpu.VMEM(floats.shape, f32),
            pltpu.VMEM(fracs.shape, bf),
            pltpu.VMEM(positions.shape, i32),
            DMA((4,)),
            DMA((4,)),
            DMA((2, 4, 3)),
            DMA((2, 4, 3)),
            DMA((2, NB)),
            DMA((2, NB)),
            DMA((2, NB)),
            DMA((2, NB)),
            DMA,
            DMA,
        ],
        compiler_params=pltpu.CompilerParams(collective_id=0, has_side_effects=True),
        name="gather_all",
    )(quarter, floats, fracs, positions)


def sin_cos(v):
    quarter = jnp.round(v * 0.6366197723675814)
    u = v - quarter * 1.5703125
    u = u - quarter * 4.837512969970703e-4
    u = u - quarter * 7.549789948768648e-8
    u2 = u * u
    s = u + u * u2 * (-1.6666654611e-1 + u2 * (8.3321608736e-3 + u2 * -1.9515295891e-4))
    c = 1.0 - 0.5 * u2 + u2 * u2 * (4.166664568298827e-2 + u2 * (-1.388731625493765e-3 + u2 * 2.443315711809948e-5))
    q = quarter.astype(jnp.int32) & 3
    odd = (q & 1) == 1
    sin = jnp.where(odd, c, s)
    cos = jnp.where(odd, s, c)
    sin = jnp.where(q >= 2, -sin, sin)
    cos = jnp.where((q == 1) | (q == 2), -cos, cos)
    return sin, cos


def low_of(high):
    return (1.0 - high).astype(jnp.bfloat16).astype(jnp.float32)


def run_of(entry):
    run = entry % ALL_RUNS
    return entry // ALL_RUNS, run // PIECE_RUNS, (run // RUNS) % DET, run % RUNS


def line(ref, at):
    z, d, r = at
    return ref[z, d, pl.ds(r, 1), :]


def spread(index, low, high, rows):
    return jnp.where(rows == index, low, jnp.where(rows == index + 1, high, 0.0))


def forward_kernel(cnt_ref, list_ref, tiles_ref, f_ref, w_ref, sig_ref, cs_ref, hit_ref, frac_ref):
    def prepare(z, _):
        code = f_ref[z, 0].astype(jnp.int32)
        hit_ref[z, 0] = code // PIX
        hit_ref[z, 1] = code % PIX
        sin, cos = sin_cos(2.0 * f_ref[z, 1])
        cs_ref[z, 0] = cos
        cs_ref[z, 1] = sin
        frac_ref[z, 0] = w_ref[z, 0].astype(jnp.float32)
        frac_ref[z, 1] = w_ref[z, 1].astype(jnp.float32)
        sig_ref[z] = jnp.zeros_like(sig_ref[z])
        return 0

    lax.fori_loop(0, NZ, prepare, 0)
    count = cnt_ref[0]
    rows = lax.broadcasted_iota(jnp.int32, (PIX, LANE), 0)

    def body(step, _):
        for u in range(UNROLL):
            k = step * UNROLL + u
            tile, z, d, r = run_of(list_ref[k])
            at = (d, pl.ds(r, 1), slice(None))
            col_high = frac_ref[z, 1, *at]
            row_high = frac_ref[z, 0, *at]
            col_weight = spread(hit_ref[z, 1, *at], low_of(col_high), col_high, rows).astype(jnp.bfloat16)
            row_weight = spread(hit_ref[z, 0, *at], low_of(row_high), row_high, rows)
            partial = jnp.dot(tiles_ref[tile], col_weight, preferred_element_type=jnp.float32)
            value = [
                jnp.sum(partial[p * PIX : (p + 1) * PIX] * row_weight, axis=0, keepdims=True) for p in range(3)
            ]
            total = value[0] + cs_ref[z, 0, *at] * value[1] + cs_ref[z, 1, *at] * value[2]
            sig_ref[z, *at] = jnp.where(k < count, total, 0.0)
        return 0

    lax.fori_loop(0, (count + UNROLL - 1) // UNROLL, body, 0)


def forward(count, order, tiles, floats, fracs):
    f32 = jnp.float32
    block = (NZ, DET, RUNS, LANE)
    pair = (NZ, 2, DET, RUNS, LANE)
    return pl.pallas_call(
        forward_kernel,
        out_shape=(jax.ShapeDtypeStruct(block, f32), jax.ShapeDtypeStruct(pair, f32)),
        in_specs=[SM, SM, VM, VM, VM],
        out_specs=(VM, VM),
        scratch_shapes=[pltpu.VMEM(pair, jnp.int32), pltpu.VMEM(pair, f32)],
        name="forward",
    )(count, order, tiles, floats, fracs)


def backward_kernel(cnt_ref, list_ref, f_ref, w_ref, cs_ref, filt_ref, acc_ref, hit_ref, frac_ref):
    def prepare(z, _):
        code = f_ref[z, 0].astype(jnp.int32)
        hit_ref[z, 0] = code // PIX
        hit_ref[z, 1] = code % PIX
        frac_ref[z, 0] = w_ref[z, 0].astype(jnp.float32)
        frac_ref[z, 1] = w_ref[z, 1].astype(jnp.float32)
        return 0

    lax.fori_loop(0, NZ, prepare, 0)

    def clear(t, _):
        acc_ref[t] = jnp.zeros_like(acc_ref[t])
        return 0

    lax.fori_loop(0, 2 * NB, clear, 0)
    count = cnt_ref[0]
    rows = lax.broadcasted_iota(jnp.int32, (PIX, LANE), 0)

    def body(step, _):
        for u in range(UNROLL):
            k = step * UNROLL + u
            tile, z, d, r = run_of(list_ref[k])
            at = (d, pl.ds(r, 1), slice(None))
            col_high = frac_ref[z, 1, *at]
            row_high = frac_ref[z, 0, *at]
            row_low = low_of(row_high)
            col_weight = spread(hit_ref[z, 1, *at], low_of(col_high), col_high, rows).astype(jnp.bfloat16)
            filt = jnp.where(k < count, filt_ref[z, *at], 0.0)
            hit = hit_ref[z, 0, *at]
            parts = []
            for p in range(3):
                scaled = filt if p == 0 else cs_ref[z, p - 1, *at] * filt
                parts.append(spread(hit, scaled * row_low, scaled * row_high, rows).astype(jnp.bfloat16))
            weighted = jnp.concatenate(parts, axis=0)
            acc_ref[tile] += lax.dot_general(
                weighted, col_weight, (((1,), (1,)), ((), ())), preferred_element_type=jnp.float32
            )
        return 0

    lax.fori_loop(0, (count + UNROLL - 1) // UNROLL, body, 0)


def backward(count, order, floats, fracs, turns, filtered):
    f32 = jnp.float32
    pair = (NZ, 2, DET, RUNS, LANE)
    return pl.pallas_call(
        backward_kernel,
        out_shape=jax.ShapeDtypeStruct((2 * NB, 3 * PIX, PIX), f32),
        in_specs=[SM, SM, VM, VM, VM, VM],
        out_specs=VM,
        scratch_shapes=[pltpu.VMEM(pair, jnp.int32), pltpu.VMEM(pair, f32)],
        name="backward",
    )(count, order, floats, fracs, turns, filtered)


def toeplitz_kernel(w_ref, hi_ref, lo_ref):
    lanes = lax.broadcasted_iota(jnp.int32, (LANE, LANE), 1)
    rows = lax.broadcasted_iota(jnp.int32, (LANE, LANE), 0)
    upper = lanes >= rows

    def rolled(block):
        return pltpu.roll(
            jnp.broadcast_to(w_ref[0, pl.ds(block, 1), :], (LANE, LANE)), 0, 1, stride=1, stride_axis=0
        )

    before = rolled(0)
    for block in range(1, 2 * REACH + 2):
        after = rolled(block)
        m = 2 * REACH + 1 - block
        matrix = jnp.where(upper, after, before)
        high = matrix.astype(jnp.bfloat16)
        hi_ref[0, m] = high
        lo_ref[0, m] = (matrix - high.astype(jnp.float32)).astype(jnp.bfloat16)
        before = after


def toeplitz(noise_coef):
    count = noise_coef.shape[1] - 1
    weights = jnp.concatenate([noise_coef[:, :1] + 1.0, noise_coef[:, 1:]], axis=1)
    edge = jnp.zeros((DET, LANE), jnp.float32)
    line_all = jnp.concatenate([edge, weights[:, :0:-1], weights, edge[:, 1:]], axis=1)
    blocks = line_all.reshape(DET, 2 * REACH + 2, LANE)
    shape = jax.ShapeDtypeStruct((DET, 2 * REACH + 1, LANE, LANE), jnp.bfloat16)
    out = pl.BlockSpec((1, 2 * REACH + 1, LANE, LANE), lambda d: (d, 0, 0, 0))
    return pl.pallas_call(
        toeplitz_kernel,
        grid=(DET,),
        out_shape=(shape, shape),
        in_specs=[pl.BlockSpec((1, 2 * REACH + 2, LANE), lambda d: (d, 0, 0))],
        out_specs=(out, out),
        name="toeplitz",
    )(blocks)


def filter_kernel(
    part_ref, hi_ref, lo_ref, out_ref, land, ext, filt, own_sem, send, recv, halo_send, halo_recv, back_send, back_recv
):
    det, tm, y, z, x = place()
    total_tm = NY * NZ * NX
    peers = [tm_of(y, (z + k) % NZ, x) for k in range(1, NZ)]
    prior, later = (tm + total_tm - 1) % total_tm, (tm + 1) % total_tm
    greet([(det, t) for t in peers + [prior, later]])
    own = pltpu.make_async_copy(part_ref.at[z], land.at[0], own_sem)
    own.start()
    sends = []
    for k in range(1, NZ):
        copy = remote(part_ref.at[(z + k) % NZ], land.at[k], send.at[k], recv.at[k], (det, peers[k - 1]))
        copy.start()
        sends.append(copy)
    own.wait()
    total = land[0]
    for k in range(1, NZ):
        sends[k - 1].wait_recv()
        total = total + land[k]
    ext[:, REACH : REACH + RUNS, :] = total
    to_prior = remote(
        ext.at[:, pl.ds(REACH, REACH), :], ext.at[:, pl.ds(REACH + RUNS, REACH), :],
        halo_send.at[0], halo_recv.at[0], (det, prior),
    )
    to_later = remote(
        ext.at[:, pl.ds(RUNS, REACH), :], ext.at[:, pl.ds(0, REACH), :], halo_send.at[1], halo_recv.at[1], (det, later)
    )
    to_prior.start()
    to_later.start()
    to_prior.wait_recv()
    to_later.wait_recv()
    first, last = tm == 0, tm == total_tm - 1
    for d in range(DET):
        line_all = jnp.concatenate(
            [
                jnp.where(first, 0.0, ext[d, :REACH]),
                ext[d, REACH : REACH + RUNS],
                jnp.where(last, 0.0, ext[d, REACH + RUNS :]),
            ],
            axis=0,
        )
        result = jnp.zeros((RUNS, LANE), jnp.float32)
        for m in range(2 * REACH + 1):
            window = line_all[m : m + RUNS]
            high = window.astype(jnp.bfloat16)
            low = (window - high.astype(jnp.float32)).astype(jnp.bfloat16)
            both = jnp.dot(
                jnp.concatenate([high, low], axis=0), hi_ref[d, m], preferred_element_type=jnp.float32
            )
            result += both[:RUNS] + both[RUNS:]
            result += jnp.dot(high, lo_ref[d, m], preferred_element_type=jnp.float32)
        filt[d] = result
    back = []
    for k in range(1, NZ):
        copy = remote(filt, out_ref.at[z], back_send.at[k], back_recv.at[k], (det, peers[k - 1]))
        copy.start()
        back.append(copy)
    own = pltpu.make_async_copy(filt, out_ref.at[z], own_sem)
    own.start()
    own.wait()
    for k in range(1, NZ):
        remote(filt, out_ref.at[(z + NZ - k) % NZ], back_send.at[k], back_recv.at[k], (det, peers[k - 1])).wait_recv()
    for copy in sends + back + [to_prior, to_later]:
        copy.wait_send()


def filtered_of(partial, hi, lo):
    f32 = jnp.float32
    block = (DET, RUNS, LANE)
    return pl.pallas_call(
        filter_kernel,
        out_shape=jax.ShapeDtypeStruct((NZ, *block), f32),
        in_specs=[ANY, VM, VM],
        out_specs=ANY,
        scratch_shapes=[
            pltpu.VMEM((NZ, *block), f32),
            pltpu.VMEM((DET, RUNS + 2 * REACH, LANE), f32),
            pltpu.VMEM(block, f32),
            DMA,
            DMA((NZ,)),
            DMA((NZ,)),
            DMA((2,)),
            DMA((2,)),
            DMA((NZ,)),
            DMA((NZ,)),
        ],
        compiler_params=pltpu.CompilerParams(collective_id=1, has_side_effects=True),
        name="filter",
    )(partial, hi, lo)


def collect_kernel(
    acc_ref, out_ref, own, land_core, land_far, land_hi, total,
    own_sem, core_send, core_recv, far_send, far_recv, hi_send, hi_recv,
):
    det, tm, y, z, x = place()
    mine = y * NX + x
    core, hi = det % 2, det // 2
    partner, across = core_of(det), hi_of(det)
    order = PEERS + [(0, 0)]

    def slot_of(dy, dx, sign):
        return ((y + sign * dy + NY) % NY) * NX + (x + dx) % NX

    far = [tm_of((y + dy) % NY, z, (x + dx) % NX) for dy, dx in PEERS]
    loads = []
    for k, (dy, dx) in enumerate(order):
        copy = pltpu.make_async_copy(acc_ref.at[slot_of(dy, dx, 1), :, :, :, core], own.at[k], own_sem.at[k])
        copy.start()
        loads.append(copy)
    greet([(partner, tm), (across, tm)] + [(det, t) for t in far])
    swaps = []
    for k, (dy, dx) in enumerate(order):
        copy = remote(
            acc_ref.at[slot_of(dy, dx, 1), :, :, :, 1 - core], land_core.at[k], core_send.at[k], core_recv.at[k],
            (partner, tm),
        )
        copy.start()
        swaps.append(copy)
    sends = []
    for k in range(NB):
        loads[k].wait()
        swaps[k].wait_recv()
        own[k] = own[k] + land_core[k]
        if k < NB - 1:
            copy = remote(own.at[k], land_far.at[k], far_send.at[k], far_recv.at[k], (det, far[k]))
            copy.start()
            sends.append(copy)
    total[...] = own[NB - 1]
    for k in range(NB - 1):
        sends[k].wait_recv()
        total[...] = total[...] + land_far[k]
    copy = remote(total.at[:, :, 1 - hi], land_hi, hi_send, hi_recv, (across, tm))
    copy.start()
    copy.wait_recv()
    out_ref[...] = total[:, :, pl.ds(hi, 1)].reshape(out_ref.shape) + land_hi[...]
    for other in swaps + sends + [copy]:
        other.wait_send()


def collect(acc):
    f32 = jnp.float32
    half = (2, 3, 2, STRIP, PIX)
    quarter = (2, 3, STRIP, PIX)
    return pl.pallas_call(
        collect_kernel,
        out_shape=jax.ShapeDtypeStruct(quarter, f32),
        in_specs=[ANY],
        out_specs=VM,
        scratch_shapes=[
            pltpu.VMEM((NB, *half), f32),
            pltpu.VMEM((NB, *half), f32),
            pltpu.VMEM((NB - 1, *half), f32),
            pltpu.VMEM(quarter, f32),
            pltpu.VMEM(half, f32),
            DMA((NB,)),
            DMA((NB,)),
            DMA((NB,)),
            DMA((NB,)),
            DMA((NB,)),
            DMA,
            DMA,
        ],
        compiler_params=pltpu.CompilerParams(collective_id=2, has_side_effects=True),
        name="collect",
    )(acc.reshape(NB, 2, 3, 2, 2, STRIP, PIX))


def run_positions(piece_list, tile_home, run_slot):
    table = jnp.arange(tile_home.shape[0], dtype=jnp.int32)
    position = jnp.sum(jnp.where(piece_list[:, None] == table[None, :], tile_home[None, :], 0), axis=1)
    slots = jnp.arange(LISTED, dtype=jnp.int32)
    runs = run_slot.reshape(-1)
    return jnp.sum(jnp.where(runs[None, :] == slots[:, None], position[:, None], 0), axis=0)


def ordered(positions):
    _, _, _, z, _ = place()
    flat = positions.reshape(-1)
    mine = (flat // (2 * NX)) % NZ == z
    tile = (flat // (2 * NX * NZ)) * (2 * NX) + flat % (2 * NX)
    index = jnp.arange(ALL_RUNS, dtype=jnp.int32)
    key = jnp.where(mine, tile, 2 * NB) * ALL_RUNS + index
    rank = jnp.sum((key[None, :] < key[:, None]).astype(jnp.int32), axis=1)
    entry = tile * ALL_RUNS + index
    order = jnp.sum(jnp.where(rank[:, None] == index[None, :], entry[:, None], 0), axis=0)
    return jnp.sum(mine.astype(jnp.int32)).reshape(1), order


def body(
    sky_map, tile_home, piece_tiles, run_slot, hit_row, hit_col, frac_row, frac_col, angle, noise_coef
):
    shape = (DET, RUNS, LANE)
    code = (hit_row * PIX + hit_col).astype(jnp.float32)
    floats = jnp.stack([code.reshape(shape), angle.reshape(shape)])
    fracs = jnp.stack([frac_row.reshape(shape), frac_col.reshape(shape)])
    positions = run_positions(piece_tiles[0, 0], tile_home, run_slot).reshape(1, PIECE_RUNS)
    hi, lo = toeplitz(noise_coef)
    tiles, all_floats, all_fracs, all_positions = gather_all(sky_map, floats, fracs, positions)
    count, order = ordered(all_positions)
    partial, turns = forward(count, order, tiles.reshape(2 * NB, 3 * PIX, PIX), all_floats, all_fracs)
    filtered = filtered_of(partial, hi, lo)
    acc = backward(count, order, all_floats, all_fracs, turns, filtered)
    return collect(acc)


def solution(mesh):
    placed = (
        P("tm", None, "det", None),
        P(),
        P("det", "tm", None),
        P("det", "tm"),
        P("det", "tm"),
        P("det", "tm"),
        P("det", "tm"),
        P("det", "tm"),
        P("det", "tm"),
        P("det", None),
    )
    return jax.shard_map(
        body, mesh=mesh, in_specs=placed, out_specs=P("tm", None, "det", None), check_vma=False
    )
```

time: 766 us -> 154 us (0.20)
  blocking collectives: 325 us -> 0 us
  Pallas kernels: 0 us -> 139 us
  waiting for transfers between devices: 138 us -> 0 us
  local copies, waits for them, and re-layouts: 112 us -> 6.11 us
  other arithmetic: 113 us -> 8.3 us
  matrix products: 59.5 us -> 0 us
  starting transfers between devices: 16.6 us -> 0 us
    all_to_all x3 -> x0, blocking collectives: 325 us -> none  [the longest x1 287 us: body(): lax.all_to_all(outbox, 'tm', split_axis=0, concat_axis=0, tiled=True)]
    pallas_call x0 -> x6, Pallas kernels: none -> 139 us  [the longest x1 36 us: filtered_of(): pl.pallas_call(filter_kernel, out_shape=jax.ShapeDtypeStruct((NZ, *block)...]
    all_to_all x2 -> x0, waiting for transfers between devices: 138 us -> none  [the longest x1 137 us: body(): lax.all_to_all(answer, 'tm', split_axis=0, concat_axis=0, tiled=True)]
    scatter-add x4 -> x0, other arithmetic: 64.5 us -> none  [back_project(): return (carry.at[slots].add(tile_terms), None)]
    dot_general x9 -> x0, matrix products: 59.5 us -> none  [the longest x4 27 us: project(): jnp.einsum('bpij,bsj->bpsi', tiles, col_weight, preferred_element_type=jn...]
    convert_element_type x16 -> x0, other arithmetic: 27.7 us -> none  [the longest x4 18.3 us: back_project(): row_weight = run_weights(rows_at, frac_rows, side_len).astype(jnp.float32)]
    slice x5 -> x2, local copies, waits for them, and re-layouts: 22.7 us -> 0.84 us  [the longest x1 0.84 us: toeplitz(): noise_coef[:, 1:]]
    gather x6 -> x0, local copies, waits for them, and re-layouts: 20.1 us -> none  [the longest x4 12.2 us: project(): tiles = jnp.take(listed, slots, axis=0)]
  transfers between devices with their start and end apart: 4 -> 0, of which waited for: 1 -> 0; matrix products, arithmetic and copies ran while one was open for 7% -> 0% of each run, Pallas kernels for 0% -> 0%
where the time goes in v1:
time: 154 us
  Pallas kernels  139 us (90%)
  other arithmetic  8.3 us (5%)
  local copies, waits for them, and re-layouts  6.11 us (4%)
    pallas_call x1, Pallas kernels, filtered_of(): pl.pallas_call(filter_kernel, out_shape=jax.ShapeDtypeStruct((NZ, *block)...  36 us
    pallas_call x1, Pallas kernels, collect(): pl.pallas_call(collect_kernel, out_shape=jax.ShapeDtypeStruct(quarter, f3...  30.3 us
    pallas_call x1, Pallas kernels, gather_all(): pl.pallas_call(gather_kernel, out_shape=(jax.ShapeDtypeStruct((NB, 2, 3,...  28.2 us
    pallas_call x1, Pallas kernels, backward(): pl.pallas_call(backward_kernel, out_shape=jax.ShapeDtypeStruct((2 * NB, 3...  20.4 us
    pallas_call x1, Pallas kernels, forward(): pl.pallas_call(forward_kernel, out_shape=(jax.ShapeDtypeStruct(block, f32...  17.3 us
    pallas_call x1, Pallas kernels, toeplitz(): pl.pallas_call(toeplitz_kernel, grid=(DET,), out_shape=(shape, shape), in...  6.95 us

profile of v1, /device:TPU:1, one launch (start us, length us, event | category | flops | bytes accessed | tf_op | source)
XLA Modules:
  0.0 153.6 jit_solution(13009788049482452587)
XLA Ops:
  0.0 0.8 select_reduce_fusion.2
  0.8 0.8 eq.67
  1.6 0.7 select_reduce_fusion.1
  2.3 0.7 slice_add_fusion
  3.0 0.8 slice.9
  3.8 0.6 rev.3
  4.4 0.1 concatenate.3
  4.5 0.7 copy.12.w_ref
  5.1 0.9 convert_bitcast_fusion
  6.0 0.9 copy_bitcast_fusion
  6.9 0.7 pad_maximum_fusion.f_ref
  7.5 0.8 copy_bitcast_fusion.2
  8.3 0.6 pad_maximum_fusion.1.w_ref
  9.0 28.2 %gather_all.1 = (bf16[8,2,3,128,128]{4,3,2,1,0:T(8,128)(2,1)}, f32[8,2,8,16,128]{4,3,2,1,0:T(8,128)}, bf16[8,2,8,16,128]{4,3,2,1,0:T(8,128)(2,1)}, s32[8,1,128]{2,1,0:T(1,128)}) custom-call(bf16[2,3,32,128]{3,2,1,0:T(8,128)(2,1)} %q_ref.1, f32[2,8,16,128]{3,2,1,0:T(8,128)} %pad_maximum_fusion.f_ref, bf16[2,8,16,128]{3,2,1,0:T(8,128)(2,1)} %pad_maximum_fusion.1.w_ref, ...), custom_call_target="tpu_custom_call" | custom-call | tf_op jit(solution)/shard_map/gather_all/pallas_call | solution.py:173
  37.2 1.4 fusion.8
  38.6 0.7 iota_add_fusion.1
  39.3 0.6 convert_reduce_fusion
  39.9 1.2 select_reduce_fusion.list_ref
  41.1 17.3 %forward.1 = (f32[8,8,16,128]{3,2,1,0:T(8,128)}, f32[8,2,8,16,128]{4,3,2,1,0:T(8,128)}) custom-call(s32[1]{0:T(128)} %bitcast.2.cnt_ref, s32[1024]{0:T(1024)} %select_reduce_fusion.list_ref, bf16[16,384,128]{2,1,0:T(8,128)(2,1)} %bitcast.25, f32[8,2,8,16,128]{4,3,2,1,0:T(8,128)} %get-tuple-element.14.f_ref, bf16[8,2,8,16,128]{4,3,2,1,0:T(8,128)(2,1)} %get-tuple-element.15.w_ref), custom_call_target="tpu_custom_call" | custom-call | tf_op jit(solution)/shard_map/forward/pallas_call | solution.py:280
  58.4 7.0 %toeplitz.1 = (bf16[8,17,128,128]{3,2,1,0:T(8,128)(2,1)}, bf16[8,17,128,128]{3,2,1,0:T(8,128)(2,1)}) custom-call(f32[8,18,128]{2,1,0:T(8,128)} %copy.12.w_ref), custom_call_target="tpu_custom_call" | custom-call | tf_op jit(solution)/shard_map/toeplitz/pallas_call | solution.py:375
  65.4 36.0 %filter.1.filt_ref = f32[8,8,16,128]{3,2,1,0:T(8,128)} custom-call(f32[8,8,16,128]{3,2,1,0:T(8,128)} %get-tuple-element.18.part_ref, bf16[8,17,128,128]{3,2,1,0:T(8,128)(2,1)} %get-tuple-element.19.hi_ref, bf16[8,17,128,128]{3,2,1,0:T(8,128)(2,1)} %get-tuple-element.20.lo_ref), custom_call_target="tpu_custom_call" | custom-call | tf_op jit(solution)/shard_map/filter/pallas_call | solution.py:455
  101.4 20.4 %backward.1 = f32[16,384,128]{2,1,0:T(8,128)} custom-call(s32[1]{0:T(128)} %bitcast.2.cnt_ref, s32[1024]{0:T(1024)} %select_reduce_fusion.list_ref, f32[8,2,8,16,128]{4,3,2,1,0:T(8,128)} %get-tuple-element.14.f_ref, bf16[8,2,8,16,128]{4,3,2,1,0:T(8,128)(2,1)} %get-tuple-element.15.w_ref, f32[8,2,8,16,128]{4,3,2,1,0:T(8,128)} %get-tuple-element.17.cs_ref, ...), custom_call_target="tpu_custom_call" | custom-call | tf_op jit(solution)/shard_map/backward/pallas_call | solution.py:336
  121.8 30.3 %collect.1 = f32[2,3,32,128]{3,2,1,0:T(8,128)} custom-call(f32[8,2,3,2,2,32,128]{6,5,4,3,2,1,0:T(8,128)} %bitcast.24), custom_call_target="tpu_custom_call" | custom-call | tf_op jit(solution)/shard_map/collect/pallas_call | solution.py:530
  152.1 1.5 %copy.22 = f32[2,3,32,128]{3,2,1,0:T(8,128)} copy(f32[2,3,32,128]{3,2,1,0:T(8,128)} %collect.1) | data formatting | bytes 196608
  (2 shorter events, 0.0 us)

commit v2 on v1

v2 whole, which is shorter than its diff:
```python
import functools

import jax
import jax.numpy as jnp
from jax import lax
from jax.experimental import pallas as pl
from jax.experimental.pallas import tpu as pltpu
from jax.sharding import PartitionSpec as P

MESH = pl.DeviceIdType.MESH
NY, NZ, NX = 4, 8, 2
NB = NY * NX
DET, RUNS, LANE = 8, 16, 128
PIX = 128
STRIP = 32
LISTED = 32
TILE_DEV = 2
REACH = 8
UNROLL = 4
PIECE_RUNS = DET * RUNS
ALL_RUNS = NB * PIECE_RUNS
ANY = pl.BlockSpec(memory_space=pl.ANY)
VM = pl.BlockSpec(memory_space=pltpu.VMEM)
SM = pl.BlockSpec(memory_space=pltpu.SMEM)
DMA = pltpu.SemaphoreType.DMA
PEERS = [(dy, dx) for dy in range(NY) for dx in range(NX) if (dy, dx) != (0, 0)]


def place():
    det, tm = lax.axis_index("det"), lax.axis_index("tm")
    y, z, x = tm // (NZ * NX), (tm // NX) % NZ, tm % NX
    return det, tm, y, z, x


def tm_of(y, z, x):
    return (y * NZ + z) * NX + x


def core_of(det):
    return det + 1 - 2 * (det % 2)


def hi_of(det):
    return (det + 2) % 4


def greet(peers):
    barrier = pltpu.get_barrier_semaphore()
    for peer in peers:
        pl.semaphore_signal(barrier, inc=1, device_id=peer, device_id_type=MESH)
    pl.semaphore_wait(barrier, len(peers))


def remote(src, dst, send, recv, peer):
    return pltpu.make_async_remote_copy(
        src_ref=src, dst_ref=dst, send_sem=send, recv_sem=recv, device_id=peer, device_id_type=MESH
    )


def pack_kernel(home_ref, piece_ref, slot_ref, row_ref, col_ref, low_ref, high_ref, angle_ref, float_ref, frac_ref, pos_ref):
    for r in range(RUNS):
        at = slice(r * LANE, (r + 1) * LANE)
        float_ref[0, r] = (row_ref[:, at] * PIX + col_ref[:, at]).astype(jnp.float32)
        float_ref[1, r] = angle_ref[:, at]
        frac_ref[0, r] = low_ref[:, at]
        frac_ref[1, r] = high_ref[:, at]
    slots = slot_ref[...]
    position = jnp.zeros_like(slots)
    for s in range(LISTED):
        position = jnp.where(slots == s, home_ref[piece_ref[0, s]], position)
    pos_ref[...] = position


def packed(tile_home, piece_list, run_slot, hit_row, hit_col, frac_row, frac_col, angle):
    shape = (2, RUNS, DET, LANE)
    return pl.pallas_call(
        pack_kernel,
        out_shape=(
            jax.ShapeDtypeStruct(shape, jnp.float32),
            jax.ShapeDtypeStruct(shape, jnp.bfloat16),
            jax.ShapeDtypeStruct((DET, RUNS), jnp.int32),
        ),
        in_specs=[SM, SM] + [VM] * 6,
        out_specs=(VM, VM, VM),
        name="pack",
    )(tile_home, piece_list, run_slot, hit_row, hit_col, frac_row, frac_col, angle)


def run_order(pos_ref, order_ref, y, x):
    f32, i32 = jnp.float32, jnp.int32
    lanes = lax.broadcasted_iota(i32, (RUNS, LANE), 1)
    offset = lax.broadcasted_iota(i32, (RUNS, LANE), 0)
    spot = jnp.zeros((DET, LANE), f32)
    for slot in range(NB):
        placed = (lanes == offset + slot * RUNS).astype(f32).astype(jnp.bfloat16)
        spot += jnp.dot(pos_ref[slot].astype(f32).astype(jnp.bfloat16), placed, preferred_element_type=f32)
    pos = spot.astype(i32)
    here = (pos // (TILE_DEV * NX * NZ) == y) & ((pos // TILE_DEV) % NX == x)
    tile = ((pos // (TILE_DEV * NX)) % NZ) * TILE_DEV + pos % TILE_DEV
    run = lax.broadcasted_iota(i32, (DET, LANE), 0) * LANE + lax.broadcasted_iota(i32, (DET, LANE), 1)
    key = (jnp.where(here, tile, TILE_DEV * NZ) * ALL_RUNS + run).astype(f32)
    entry_t = (tile * ALL_RUNS + run).astype(f32).T
    key_t = key.T
    square = (LANE, LANE)
    ranks = []
    for d in range(DET):
        mine = jnp.broadcast_to(key[d : d + 1], square)
        less = jnp.zeros(square, f32)
        for e in range(DET):
            less += jnp.where(jnp.broadcast_to(key_t[:, e : e + 1], square) < mine, 1.0, 0.0)
        ranks.append(jnp.sum(less, axis=0, keepdims=True))
    rank_t = jnp.concatenate(ranks, axis=0).T
    place = lax.broadcasted_iota(i32, square, 1).astype(f32)
    for d in range(DET):
        found = jnp.zeros(square, f32)
        for e in range(DET):
            at = jnp.broadcast_to(rank_t[:, e : e + 1], square) - (d * LANE)
            found += jnp.where(at == place, jnp.broadcast_to(entry_t[:, e : e + 1], square), 0.0)
        order_ref[d : d + 1, :] = jnp.sum(found, axis=0, keepdims=True).astype(i32)
    count = jnp.sum(jnp.sum(here.astype(f32), axis=1, keepdims=True), axis=0, keepdims=True)
    order_ref[DET:, :] = jnp.broadcast_to(count, (DET, LANE)).astype(i32)


def gather_kernel(
    q_ref, f_ref, w_ref, p_ref, tiles_ref, fo_ref, wo_ref, order_ref,
    q_own, f_own, w_own, pos_all, load_sem, store_sem,
    pos_send, pos_recv, block_send, block_recv, ring_send, ring_recv, core_send, core_recv, hi_send, hi_recv,
):
    det, tm, y, z, x = place()
    partner, across = core_of(det), hi_of(det)
    right, left = tm_of(y, (z + 1) % NZ, x), tm_of(y, (z + NZ - 1) % NZ, x)
    ahead, behind = (y + 1) % NY, (y + NY - 1) % NY
    facing = (y + NY // 2) % NY
    other = 1 - x
    up, down, side = (det, tm_of(ahead, z, x)), (det, tm_of(behind, z, x)), (det, tm_of(y, z, other))
    far = [(det, tm_of((y + dy) % NY, z, (x + dx) % NX)) for dy, dx in PEERS]

    def strip(slot, d):
        return tiles_ref.at[slot, :, :, pl.ds(d * STRIP, STRIP), :]

    def block(slot, part):
        return fo_ref.at[slot, part] if part < 2 else wo_ref.at[slot]

    def own_block(part):
        return f_ref.at[part] if part < 2 else w_ref

    mine = y * NX + x
    loads = [
        pltpu.make_async_copy(q_ref, q_own, load_sem.at[0]),
        pltpu.make_async_copy(f_ref, f_own, load_sem.at[1]),
        pltpu.make_async_copy(w_ref, w_own, load_sem.at[2]),
        pltpu.make_async_copy(p_ref, pos_all.at[mine], load_sem.at[3]),
    ]
    for copy in loads:
        copy.start()
    greet([(det, right), (det, left), (partner, tm), (across, tm)] + far)

    started = []

    def start(copy):
        copy.start()
        started.append(copy)

    for k, peer in enumerate(far):
        start(remote(p_ref, pos_all.at[mine], pos_send.at[k], pos_recv.at[k], peer))
    start(remote(q_ref, strip(z, det), hi_send, hi_recv, (across, tm)))

    def send_block(link, slot, part, peer, own=False):
        start(
            remote(
                own_block(part) if own else block(slot, part), block(slot, part),
                block_send.at[link, part], block_recv.at[link, part], peer,
            )
        )

    def wait_block(link, slot, part):
        remote(own_block(part), block(slot, part), block_send.at[link, part], block_recv.at[link, part], side).wait_recv()

    for part in range(3):
        send_block(1, mine, part, up, True)
        send_block(2, mine, part, down, True)
        send_block(0, mine, part, side, True)

    def reach(half, direction):
        return NZ // 2 if half == direction else NZ // 2 - 1

    owner = (det, across)

    def send_strip(half, direction, step):
        slot = (z + NZ - step) % NZ if direction == 0 else (z + step) % NZ
        src = q_ref if half == 0 and step == 0 else strip(slot, owner[half])
        start(
            remote(
                src, strip(slot, owner[half]), ring_send.at[half, direction, step], ring_recv.at[half, direction, step],
                (det, right if direction == 0 else left),
            )
        )

    def take_strip(half, step):
        for direction in (0, 1):
            if step < reach(half, direction):
                slot = (z + NZ - step - 1) % NZ if direction == 0 else (z + step + 1) % NZ
                here = strip(slot, owner[half])
                remote(q_ref, here, ring_send.at[half, direction, step], ring_recv.at[half, direction, step], side).wait_recv()
                if step + 1 < reach(half, direction):
                    send_strip(half, direction, step + 1)
                index = 1 + direction * NZ // 2 + step
                start(remote(here, here, core_send.at[half, index], core_recv.at[half, index], (partner, tm)))

    for direction in (0, 1):
        send_strip(0, direction, 0)
    start(remote(q_ref, strip(z, det), core_send.at[0, 0], core_recv.at[0, 0], (partner, tm)))
    stores = []
    for i, (src, dst) in enumerate(((q_own, strip(z, det)), (f_own, fo_ref.at[mine]), (w_own, wo_ref.at[mine]))):
        loads[i].wait()
        copy = pltpu.make_async_copy(src, dst, store_sem.at[i])
        copy.start()
        stores.append(copy)

    remote(q_ref, strip(z, across), hi_send, hi_recv, (across, tm)).wait_recv()
    for direction in (0, 1):
        send_strip(1, direction, 0)
    start(remote(strip(z, across), strip(z, across), core_send.at[1, 0], core_recv.at[1, 0], (partner, tm)))

    slot_of = {1: behind * NX + x, 2: ahead * NX + x, 0: y * NX + other, 5: facing * NX + x, 6: facing * NX + other,
               3: behind * NX + other, 4: ahead * NX + other}

    def near(part):
        for link in (1, 2, 0):
            wait_block(link, slot_of[link], part)
            if link == 1 and part != 1:
                send_block(5, slot_of[1], part, up)
            if link == 2 and part == 1:
                send_block(5, slot_of[2], part, down)
            if link == 0:
                send_block(3, slot_of[0], part, up)
                send_block(4, slot_of[0], part, down)

    def opposite(part):
        wait_block(5, slot_of[5], part)
        send_block(6, slot_of[5], part, side)

    take_strip(0, 0)
    near(0)
    take_strip(1, 0)
    near(1)
    take_strip(0, 1)
    near(2)
    take_strip(1, 1)
    opposite(0)
    opposite(1)
    take_strip(0, 2)
    opposite(2)
    take_strip(1, 2)
    take_strip(0, 3)
    take_strip(1, 3)

    loads[3].wait()
    for k, peer in enumerate(far):
        remote(p_ref, pos_all.at[mine], pos_send.at[k], pos_recv.at[k], peer).wait_recv()
    run_order(pos_all, order_ref, y, x)

    for part in range(3):
        for link in (3, 4, 6):
            wait_block(link, slot_of[link], part)
    theirs = (partner, hi_of(partner))
    for half in (0, 1):
        for direction in (0, 1):
            for step in range(-1 if direction == 0 else 0, reach(half, direction)):
                slot = (z + NZ - step - 1) % NZ if direction == 0 else (z + step + 1) % NZ
                index = 0 if step < 0 else 1 + direction * NZ // 2 + step
                remote(
                    q_ref, strip(slot, theirs[half]), core_send.at[half, index], core_recv.at[half, index], (partner, tm)
                ).wait_recv()
    for copy in stores:
        copy.wait()
    for copy in started:
        copy.wait_send()


def gather_all(quarter, floats, fracs, positions):
    bf, f32, i32 = jnp.bfloat16, jnp.float32, jnp.int32
    return pl.pallas_call(
        gather_kernel,
        out_shape=(
            jax.ShapeDtypeStruct((NZ, TILE_DEV, 3, PIX, PIX), bf),
            jax.ShapeDtypeStruct((NB, *floats.shape), f32),
            jax.ShapeDtypeStruct((NB, *fracs.shape), bf),
            jax.ShapeDtypeStruct((2 * DET, LANE), i32),
        ),
        in_specs=[ANY] * 4,
        out_specs=(ANY, ANY, ANY, VM),
        scratch_shapes=[
            pltpu.VMEM(quarter.shape, bf),
            pltpu.VMEM(floats.shape, f32),
            pltpu.VMEM(fracs.shape, bf),
            pltpu.VMEM((NB, *positions.shape), i32),
            DMA((4,)),
            DMA((3,)),
            DMA((NB,)),
            DMA((NB,)),
            DMA((7, 3)),
            DMA((7, 3)),
            DMA((2, 2, NZ // 2)),
            DMA((2, 2, NZ // 2)),
            DMA((2, NZ + 1)),
            DMA((2, NZ + 1)),
            DMA,
            DMA,
        ],
        compiler_params=pltpu.CompilerParams(collective_id=0, has_side_effects=True),
        name="gather_all",
    )(quarter, floats, fracs, positions)


def sin_cos(v):
    quarter = jnp.round(v * 0.6366197723675814)
    u = v - quarter * 1.5703125
    u = u - quarter * 4.837512969970703e-4
    u = u - quarter * 7.549789948768648e-8
    u2 = u * u
    s = u + u * u2 * (-1.6666654611e-1 + u2 * (8.3321608736e-3 + u2 * -1.9515295891e-4))
    c = 1.0 - 0.5 * u2 + u2 * u2 * (4.166664568298827e-2 + u2 * (-1.388731625493765e-3 + u2 * 2.443315711809948e-5))
    q = quarter.astype(jnp.int32) & 3
    odd = (q & 1) == 1
    sin = jnp.where(odd, c, s)
    cos = jnp.where(odd, s, c)
    sin = jnp.where(q >= 2, -sin, sin)
    cos = jnp.where((q == 1) | (q == 2), -cos, cos)
    return sin, cos


def low_of(high):
    return (1.0 - high).astype(jnp.bfloat16).astype(jnp.float32)


def run_of(entry):
    run = entry & (ALL_RUNS - 1)
    return entry >> 10, (run >> 4) & (NB - 1), run >> 7, run & (RUNS - 1)


def spread(index, low, high, rows):
    return jnp.where(rows == index, low, jnp.where(rows == index + 1, high, 0.0))


def forward_kernel(list_ref, tiles_ref, f_ref, w_ref, sig_ref, cs_ref, hit_ref, frac_ref):
    def prepare(z, _):
        code = f_ref[z, 0].astype(jnp.int32)
        hit_ref[z, 0] = code // PIX
        hit_ref[z, 1] = code % PIX
        sin, cos = sin_cos(2.0 * f_ref[z, 1])
        cs_ref[z, 0] = cos
        cs_ref[z, 1] = sin
        frac_ref[z, 0] = w_ref[z, 0].astype(jnp.float32)
        frac_ref[z, 1] = w_ref[z, 1].astype(jnp.float32)
        sig_ref[z] = jnp.zeros_like(sig_ref[z])
        return 0

    lax.fori_loop(0, NB, prepare, 0)
    count = list_ref[DET, 0]
    rows = lax.broadcasted_iota(jnp.int32, (PIX, LANE), 0)

    def body(step, _):
        for u in range(UNROLL):
            k = step * UNROLL + u
            tile, z, d, r = run_of(list_ref[k >> 7, k & (LANE - 1)])
            at = (r, pl.ds(d, 1), slice(None))
            col_high = frac_ref[z, 1, *at]
            row_high = frac_ref[z, 0, *at]
            col_weight = spread(hit_ref[z, 1, *at], low_of(col_high), col_high, rows).astype(jnp.bfloat16)
            row_weight = spread(hit_ref[z, 0, *at], low_of(row_high), row_high, rows)
            partial = jnp.dot(tiles_ref[tile], col_weight, preferred_element_type=jnp.float32)
            value = [
                jnp.sum(partial[p * PIX : (p + 1) * PIX] * row_weight, axis=0, keepdims=True) for p in range(3)
            ]
            total = value[0] + cs_ref[z, 0, *at] * value[1] + cs_ref[z, 1, *at] * value[2]
            sig_ref[z, d, pl.ds(r, 1), :] = jnp.where(k < count, total, 0.0)
        return 0

    lax.fori_loop(0, (count + UNROLL - 1) // UNROLL, body, 0)


def forward(order, tiles, floats, fracs):
    f32 = jnp.float32
    block = (NB, DET, RUNS, LANE)
    pair = (NB, 2, RUNS, DET, LANE)
    return pl.pallas_call(
        forward_kernel,
        out_shape=(jax.ShapeDtypeStruct(block, f32), jax.ShapeDtypeStruct(pair, f32)),
        in_specs=[SM, VM, VM, VM],
        out_specs=(VM, VM),
        scratch_shapes=[pltpu.VMEM(pair, jnp.int32), pltpu.VMEM(pair, f32)],
        name="forward",
    )(order, tiles, floats, fracs)


def backward_kernel(list_ref, f_ref, w_ref, cs_ref, filt_ref, acc_ref, hit_ref, frac_ref):
    def prepare(z, _):
        code = f_ref[z, 0].astype(jnp.int32)
        hit_ref[z, 0] = code // PIX
        hit_ref[z, 1] = code % PIX
        frac_ref[z, 0] = w_ref[z, 0].astype(jnp.float32)
        frac_ref[z, 1] = w_ref[z, 1].astype(jnp.float32)
        return 0

    lax.fori_loop(0, NB, prepare, 0)

    def clear(t, _):
        acc_ref[t] = jnp.zeros_like(acc_ref[t])
        return 0

    lax.fori_loop(0, TILE_DEV * NZ, clear, 0)
    count = list_ref[DET, 0]
    rows = lax.broadcasted_iota(jnp.int32, (PIX, LANE), 0)

    def body(step, _):
        for u in range(UNROLL):
            k = step * UNROLL + u
            tile, z, d, r = run_of(list_ref[k >> 7, k & (LANE - 1)])
            at = (r, pl.ds(d, 1), slice(None))
            col_high = frac_ref[z, 1, *at]
            row_high = frac_ref[z, 0, *at]
            row_low = low_of(row_high)
            col_weight = spread(hit_ref[z, 1, *at], low_of(col_high), col_high, rows).astype(jnp.bfloat16)
            filt = jnp.where(k < count, filt_ref[z, d, pl.ds(r, 1), :], 0.0)
            hit = hit_ref[z, 0, *at]
            parts = []
            for p in range(3):
                scaled = filt if p == 0 else cs_ref[z, p - 1, *at] * filt
                parts.append(spread(hit, scaled * row_low, scaled * row_high, rows).astype(jnp.bfloat16))
            weighted = jnp.concatenate(parts, axis=0)
            acc_ref[tile] += lax.dot_general(
                weighted, col_weight, (((1,), (1,)), ((), ())), preferred_element_type=jnp.float32
            )
        return 0

    lax.fori_loop(0, (count + UNROLL - 1) // UNROLL, body, 0)


def backward(order, floats, fracs, turns, filtered):
    f32 = jnp.float32
    pair = (NB, 2, RUNS, DET, LANE)
    return pl.pallas_call(
        backward_kernel,
        out_shape=jax.ShapeDtypeStruct((TILE_DEV * NZ, 3 * PIX, PIX), f32),
        in_specs=[SM, VM, VM, VM, VM],
        out_specs=VM,
        scratch_shapes=[pltpu.VMEM(pair, jnp.int32), pltpu.VMEM(pair, f32)],
        name="backward",
    )(order, floats, fracs, turns, filtered)


def toeplitz(noise_ref, line_ref, hi_ref, lo_ref):
    square = (LANE, LANE)
    lanes = lax.broadcasted_iota(jnp.int32, square, 1)
    rows = lax.broadcasted_iota(jnp.int32, square, 0)
    first = lax.broadcasted_iota(jnp.int32, (DET, LANE), 1) == 0
    for q in range(REACH):
        lags = noise_ref[:, q * LANE : (q + 1) * LANE]
        line_ref[q] = jnp.where(first, lags + 1.0, lags) if q == 0 else lags
    line_ref[REACH] = jnp.where(first, jnp.broadcast_to(noise_ref[:, REACH * LANE :], (DET, LANE)), 0.0)

    def one(d, _):
        def put(q, matrix):
            high = matrix.astype(jnp.bfloat16)
            hi_ref[d, q] = high
            lo_ref[d, q] = (matrix - high.astype(jnp.float32)).astype(jnp.bfloat16)

        before = None
        for q in range(REACH + 1):
            lags = line_ref[q, pl.ds(d, 1), :]
            after = pltpu.roll(jnp.broadcast_to(lags, square), 0, 1, stride=1, stride_axis=0)
            if q == 0:
                put(0, jnp.where(lanes >= rows, after, 0.0))
                put(REACH + 1, jnp.where(lanes > rows, after, 0.0))
            else:
                put(q, jnp.where(lanes >= rows, after, before))
            before = after
        return 0

    lax.fori_loop(0, DET, one, 0)


STRAIGHT = (((1,), (0,)), ((), ()))
CROSSED = (((1,), (1,)), ((), ()))


def filter_kernel(
    part_ref, noise_ref, out_ref, land, ext, filt, lags, t_hi, t_lo,
    own_sem, send, recv, halo_send, halo_recv, back_send, back_recv,
):
    det, tm, y, z, x = place()
    total_tm = NY * NZ * NX
    mine = y * NX + x
    prior, later = (tm + total_tm - 1) % total_tm, (tm + 1) % total_tm

    def slot(k, sign):
        dy, dx = PEERS[k]
        return ((y + sign * dy + NY) % NY) * NX + (x + dx) % NX

    peers = [(det, tm_of((y + dy) % NY, z, (x + dx) % NX)) for dy, dx in PEERS]
    greet(peers + [(det, later), (det, prior)])
    own = pltpu.make_async_copy(part_ref.at[mine], land.at[NB - 1], own_sem)
    own.start()
    sends = []
    for k, peer in enumerate(peers):
        copy = remote(part_ref.at[slot(k, 1)], land.at[k], send.at[k], recv.at[k], peer)
        copy.start()
        sends.append(copy)
    toeplitz(noise_ref, lags, t_hi, t_lo)
    own.wait()
    total = land[NB - 1]
    for k in range(NB - 1):
        sends[k].wait_recv()
        total = total + land[k]
    ext[:, REACH : REACH + RUNS, :] = total
    to_prior = remote(
        ext.at[:, pl.ds(REACH, REACH), :], ext.at[:, pl.ds(REACH + RUNS, REACH), :],
        halo_send.at[0], halo_recv.at[0], (det, prior),
    )
    to_later = remote(
        ext.at[:, pl.ds(RUNS, REACH), :], ext.at[:, pl.ds(0, REACH), :], halo_send.at[1], halo_recv.at[1], (det, later)
    )
    to_prior.start()
    to_later.start()
    to_prior.wait_recv()
    to_later.wait_recv()
    first, last = tm == 0, tm == total_tm - 1

    def product(left, right, crossed):
        return lax.dot_general(left, right, CROSSED if crossed else STRAIGHT, preferred_element_type=jnp.float32)

    for d in range(DET):
        line_all = jnp.concatenate(
            [
                jnp.where(first, 0.0, ext[d, :REACH]),
                ext[d, REACH : REACH + RUNS],
                jnp.where(last, 0.0, ext[d, REACH + RUNS :]),
            ],
            axis=0,
        )
        result = jnp.zeros((RUNS, LANE), jnp.float32)
        for m in range(2 * REACH + 1):
            window = line_all[m : m + RUNS]
            high = window.astype(jnp.bfloat16)
            low = (window - high.astype(jnp.float32)).astype(jnp.bfloat16)
            stack = jnp.concatenate([high, low], axis=0)
            q = REACH - m
            for index, crossed in [(q, False)] if q > 0 else [(-q, True)] if q < 0 else [(0, False), (REACH + 1, True)]:
                both = product(stack, t_hi[d, index], crossed)
                result += both[:RUNS] + both[RUNS:] + product(high, t_lo[d, index], crossed)
        filt[d] = result
    back = []
    for k, peer in enumerate(peers):
        copy = remote(filt, out_ref.at[mine], back_send.at[k], back_recv.at[k], peer)
        copy.start()
        back.append(copy)
    own = pltpu.make_async_copy(filt, out_ref.at[mine], own_sem)
    own.start()
    own.wait()
    for k, peer in enumerate(peers):
        remote(filt, out_ref.at[slot(k, -1)], back_send.at[k], back_recv.at[k], peer).wait_recv()
    for copy in sends + back + [to_prior, to_later]:
        copy.wait_send()


def filtered_of(partial, noise_coef):
    f32, bf = jnp.float32, jnp.bfloat16
    block = (DET, RUNS, LANE)
    matrices = (DET, REACH + 2, LANE, LANE)
    return pl.pallas_call(
        filter_kernel,
        out_shape=jax.ShapeDtypeStruct((NB, *block), f32),
        in_specs=[ANY, VM],
        out_specs=ANY,
        scratch_shapes=[
            pltpu.VMEM((NB, *block), f32),
            pltpu.VMEM((DET, RUNS + 2 * REACH, LANE), f32),
            pltpu.VMEM(block, f32),
            pltpu.VMEM((REACH + 1, DET, LANE), f32),
            pltpu.VMEM(matrices, bf),
            pltpu.VMEM(matrices, bf),
            DMA,
            DMA((NB,)),
            DMA((NB,)),
            DMA((2,)),
            DMA((2,)),
            DMA((NB,)),
            DMA((NB,)),
        ],
        compiler_params=pltpu.CompilerParams(collective_id=1, has_side_effects=True),
        name="filter",
    )(partial, noise_coef)


CHUNKS = [(t, p) for t in range(TILE_DEV) for p in range(3)]
HALF_Z = NZ // 2
OFFSETS = [4, 3, -3, 2, -2, 1, -1, 0]


def collect_kernel(
    acc_ref, out_ref, own, land_core, land, land_hi, total,
    own_sem, core_send, core_recv, ring_send, ring_recv, hi_send, hi_recv,
):
    det, tm, y, z, x = place()
    core, hi = det % 2, det // 2
    partner, across = core_of(det), hi_of(det)
    neighbours = ((det, tm_of(y, (z + 1) % NZ, x)), (det, tm_of(y, (z + NZ - 1) % NZ, x)))
    loads = []
    for k, offset in enumerate(OFFSETS):
        copy = pltpu.make_async_copy(acc_ref.at[(z + offset + NZ) % NZ, :, :, :, core], own.at[k], own_sem.at[k])
        copy.start()
        loads.append(copy)
    greet([(partner, tm), (across, tm), *neighbours])
    started = []

    def start(copy):
        copy.start()
        started.append(copy)

    for k, offset in enumerate(OFFSETS):
        start(
            remote(
                acc_ref.at[(z + offset + NZ) % NZ, :, :, :, 1 - core], land_core.at[k], core_send.at[k], core_recv.at[k],
                (partner, tm),
            )
        )

    def ring(direction, step, c):
        t, p = CHUNKS[c]
        sign = 1 if direction == 0 else -1
        k = OFFSETS.index(sign * (HALF_Z - step)) if step else 0
        return remote(
            own.at[k, t, p], land.at[direction, step, t, p],
            ring_send.at[direction, step, c], ring_recv.at[direction, step, c], neighbours[direction],
        )

    def swapped(k):
        loads[k].wait()
        remote(acc_ref.at[0, :, :, :, 0], land_core.at[k], core_send.at[k], core_recv.at[k], (partner, tm)).wait_recv()

    swapped(0)
    for direction in (0, 1):
        for c, (t, p) in enumerate(CHUNKS):
            if t == direction:
                own[0, t, p] = own[0, t, p] + land_core[0, t, p]
    for p in range(3):
        for direction in (0, 1):
            start(ring(direction, 0, direction * 3 + p))
    for step in range(1, HALF_Z):
        keys = [OFFSETS.index(HALF_Z - step), OFFSETS.index(step - HALF_Z)]
        for k in keys:
            swapped(k)
        for i in range(len(CHUNKS)):
            for direction in (0, 1):
                c = (i + 3 * (1 - direction)) % len(CHUNKS) if step == 1 else i
                t, p = CHUNKS[c]
                k = keys[direction]
                value = own[k, t, p] + land_core[k, t, p]
                if step > 1 or t == direction:
                    ring(direction, step - 1, c).wait_recv()
                    value = value + land[direction, step - 1, t, p]
                own[k, t, p] = value
                start(ring(direction, step, c))
    last = len(OFFSETS) - 1
    swapped(last)

    def across_copy(c):
        t, p = CHUNKS[c]
        return remote(total.at[t, p, 1 - hi], land_hi.at[t, p], hi_send.at[c], hi_recv.at[c], (across, tm))

    for c, (t, p) in enumerate(CHUNKS):
        value = own[last, t, p] + land_core[last, t, p]
        for direction in (0, 1):
            ring(direction, HALF_Z - 1, c).wait_recv()
            value = value + land[direction, HALF_Z - 1, t, p]
        total[t, p] = value
        start(across_copy(c))
    for c, (t, p) in enumerate(CHUNKS):
        across_copy(c).wait_recv()
        out_ref[t, p] = total[t, p, hi] + land_hi[t, p]
    for copy in started:
        copy.wait_send()


def collect(acc):
    f32 = jnp.float32
    half = (TILE_DEV, 3, 2, STRIP, PIX)
    quarter = (TILE_DEV, 3, STRIP, PIX)
    return pl.pallas_call(
        collect_kernel,
        out_shape=jax.ShapeDtypeStruct(quarter, f32),
        in_specs=[ANY],
        out_specs=VM,
        scratch_shapes=[
            pltpu.VMEM((NZ, *half), f32),
            pltpu.VMEM((NZ, *half), f32),
            pltpu.VMEM((2, HALF_Z, *half), f32),
            pltpu.VMEM(quarter, f32),
            pltpu.VMEM(half, f32),
            DMA((NZ,)),
            DMA((NZ,)),
            DMA((NZ,)),
            DMA((2, HALF_Z, 6)),
            DMA((2, HALF_Z, 6)),
            DMA((6,)),
            DMA((6,)),
        ],
        compiler_params=pltpu.CompilerParams(collective_id=2, has_side_effects=True),
        name="collect",
    )(acc.reshape(NZ, TILE_DEV, 3, 2, 2, STRIP, PIX))


def body(
    sky_map, tile_home, piece_tiles, run_slot, hit_row, hit_col, frac_row, frac_col, angle, noise_coef
):
    floats, fracs, positions = packed(
        tile_home, piece_tiles.reshape(1, LISTED), run_slot, hit_row, hit_col, frac_row, frac_col, angle
    )
    tiles, all_floats, all_fracs, order = gather_all(sky_map, floats, fracs, positions)
    partial, turns = forward(order, tiles.reshape(TILE_DEV * NZ, 3 * PIX, PIX), all_floats, all_fracs)
    filtered = filtered_of(partial, noise_coef)
    acc = backward(order, all_floats, all_fracs, turns, filtered)
    return collect(acc)


def solution(mesh):
    placed = (
        P("tm", None, "det", None),
        P(),
        P("det", "tm", None),
        P("det", "tm"),
        P("det", "tm"),
        P("det", "tm"),
        P("det", "tm"),
        P("det", "tm"),
        P("det", "tm"),
        P("det", None),
    )
    return jax.shard_map(
        body, mesh=mesh, in_specs=placed, out_specs=P("tm", None, "det", None), check_vma=False
    )
```

time: 154 us -> 123 us (0.80)
  Pallas kernels: 139 us -> 122 us
  other arithmetic: 8.3 us -> 0 us
  local copies, waits for them, and re-layouts: 6.11 us -> 1.54 us
    pallas_call x4, Pallas kernels: 91.6 us -> 79.4 us  [the longest x1 33.7 us: gather_all(): pl.pallas_call(gather_kernel, out_shape=(jax.ShapeDtypeStruct((NZ, TILE_D...]
    reduce_sum x5 -> x0, other arithmetic: 4.74 us -> none  [the longest x1 1.43 us: ordered(): return (jnp.sum(mine.astype(jnp.int32)).reshape(1), order)]
    pallas_call x1, Pallas kernels: 17.3 us -> 13.2 us  [forward(): pl.pallas_call(forward_kernel, out_shape=(jax.ShapeDtypeStruct(block, f32...]
    another operation x2 -> x0, local copies, waits for them, and re-layouts: 1.65 us -> none  [the longest x1 0.87 us: body(): floats = jnp.stack([code.reshape(shape), angle.reshape(shape)])]
where the time goes in v2:
time: 123 us; the launch traced here: 124 us
  Pallas kernels  122 us (99%)
  local copies, waits for them, and re-layouts  1.54 us (1%)
    pallas_call x1, Pallas kernels, gather_all(): pl.pallas_call(gather_kernel, out_shape=(jax.ShapeDtypeStruct((NZ, TILE_D...  33.7 us
    pallas_call x1, Pallas kernels, collect(): pl.pallas_call(collect_kernel, out_shape=jax.ShapeDtypeStruct(quarter, f3...  29.8 us
    pallas_call x1, Pallas kernels, filtered_of(): pl.pallas_call(filter_kernel, out_shape=jax.ShapeDtypeStruct((NB, *block)...  28.3 us
    pallas_call x1, Pallas kernels, backward(): pl.pallas_call(backward_kernel, out_shape=jax.ShapeDtypeStruct((TILE_DEV...  15.7 us
    pallas_call x1, Pallas kernels, forward(): pl.pallas_call(forward_kernel, out_shape=(jax.ShapeDtypeStruct(block, f32...  13.2 us

profile of v2, /device:TPU:1, one launch (start us, length us, event | category | flops | bytes accessed | tf_op | source)
XLA Modules:
  0.0 124.0 jit_solution(10607679368996223429)
XLA Ops:
  0.0 1.7 %pack.1 = (f32[2,16,8,128]{3,2,1,0:T(8,128)}, bf16[2,16,8,128]{3,2,1,0:T(8,128)(2,1)}, s32[8,16]{1,0:T(8,128)}) custom-call(s32[128]{0:T(128)} %home_ref.1, s32[1,32]{1,0:T(1,128)} %bitcast.5, s32[8,16]{1,0:T(8,128)} %slot_ref.1, s32[8,2048]{1,0:T(8,128)} %row_ref.1, s32[8,2048]{1,0:T(8,128)} %col_ref.1, bf16[8,2048]{1,0:T(8,128)(2,1)} %low_ref.1, ...), custom_call_target="tpu_custom_call" | custom-call | tf_op jit(solution)/shard_map/pack/pallas_call | solution.py:76
  1.7 33.7 %gather_all.1 = (bf16[8,2,3,128,128]{4,3,2,1,0:T(8,128)(2,1)}, f32[8,2,16,8,128]{4,3,2,1,0:T(8,128)}, bf16[8,2,16,8,128]{4,3,2,1,0:T(8,128)(2,1)}, s32[16,128]{1,0:T(8,128)}) custom-call(bf16[2,3,32,128]{3,2,1,0:T(8,128)(2,1)} %q_ref.1, f32[2,16,8,128]{3,2,1,0:T(8,128)} %get-tuple-element.14.f_ref, bf16[2,16,8,128]{3,2,1,0:T(8,128)(2,1)} %get-tuple-element.15.w_ref, ...), custom_call_target="tpu_custom_call" | custom-call | tf_op jit(solution)/shard_map/gather_all/pallas_call | solution.py:283
  35.4 13.2 %forward.1 = (f32[8,8,16,128]{3,2,1,0:T(8,128)}, f32[8,2,16,8,128]{4,3,2,1,0:T(8,128)}) custom-call(s32[16,128]{1,0:T(8,128)} %get-tuple-element.17.list_ref, bf16[16,384,128]{2,1,0:T(8,128)(2,1)} %bitcast.4, f32[8,2,16,8,128]{4,3,2,1,0:T(8,128)} %get-tuple-element.18.f_ref, bf16[8,2,16,8,128]{4,3,2,1,0:T(8,128)(2,1)} %get-tuple-element.19.w_ref), custom_call_target="tpu_custom_call" | custom-call | tf_op jit(solution)/shard_map/forward/pallas_call | solution.py:387
  48.6 28.3 %filter.1.filt_ref = f32[8,8,16,128]{3,2,1,0:T(8,128)} custom-call(f32[8,8,16,128]{3,2,1,0:T(8,128)} %get-tuple-element.22.part_ref, f32[8,1025]{1,0:T(8,128)} %noise_ref.1), custom_call_target="tpu_custom_call" | custom-call | tf_op jit(solution)/shard_map/filter/pallas_call | solution.py:571
  77.0 15.7 %backward.1 = f32[16,384,128]{2,1,0:T(8,128)} custom-call(s32[16,128]{1,0:T(8,128)} %get-tuple-element.17.list_ref, f32[8,2,16,8,128]{4,3,2,1,0:T(8,128)} %get-tuple-element.18.f_ref, bf16[8,2,16,8,128]{4,3,2,1,0:T(8,128)(2,1)} %get-tuple-element.19.w_ref, f32[8,2,16,8,128]{4,3,2,1,0:T(8,128)} %get-tuple-element.21.cs_ref, f32[8,8,16,128]{3,2,1,0:T(8,128)} %filter.1.filt_ref), custom_call_target="tpu_custom_call" | custom-call | tf_op jit(solution)/shard_map/backward/pallas_call | solution.py:443
  92.7 29.8 %collect.1 = f32[2,3,32,128]{3,2,1,0:T(8,128)} custom-call(f32[8,2,3,2,2,32,128]{6,5,4,3,2,1,0:T(8,128)} %bitcast.3), custom_call_target="tpu_custom_call" | custom-call | tf_op jit(solution)/shard_map/collect/pallas_call | solution.py:690
  122.5 1.5 %copy.12 = f32[2,3,32,128]{3,2,1,0:T(8,128)} copy(f32[2,3,32,128]{3,2,1,0:T(8,128)} %collect.1) | data formatting | bytes 196608

commit v3 on v2

--- a/solution.py
+++ b/solution.py
@@ -16,7 +16,8 @@
 LISTED = 32
 TILE_DEV = 2
 REACH = 8
-UNROLL = 4
+UNROLL = 16
+HALF = 16
 PIECE_RUNS = DET * RUNS
 ALL_RUNS = NB * PIECE_RUNS
 ANY = pl.BlockSpec(memory_space=pl.ANY)
@@ -340,14 +341,22 @@
 
 
 def spread(index, low, high, rows):
-    return jnp.where(rows == index, low, jnp.where(rows == index + 1, high, 0.0))
+    bf = jnp.bfloat16
+    wide = [jnp.broadcast_to(v, (HALF, LANE)).astype(bf) for v in (index, index + 1.0, low, high)]
+    zero = jnp.zeros((HALF, LANE), bf)
+    parts = []
+    for b in range(PIX // HALF):
+        row = rows[b * HALF : (b + 1) * HALF]
+        parts.append(jnp.where(row == wide[0], wide[2], jnp.where(row == wide[1], wide[3], zero)))
+    return jnp.concatenate(parts, axis=0)
 
 
 def forward_kernel(list_ref, tiles_ref, f_ref, w_ref, sig_ref, cs_ref, hit_ref, frac_ref):
     def prepare(z, _):
-        code = f_ref[z, 0].astype(jnp.int32)
-        hit_ref[z, 0] = code // PIX
-        hit_ref[z, 1] = code % PIX
+        code = f_ref[z, 0]
+        row = jnp.floor(code * (1.0 / PIX))
+        hit_ref[z, 0] = row
+        hit_ref[z, 1] = code - row * PIX
         sin, cos = sin_cos(2.0 * f_ref[z, 1])
         cs_ref[z, 0] = cos
         cs_ref[z, 1] = sin
@@ -358,7 +367,7 @@
 
     lax.fori_loop(0, NB, prepare, 0)
     count = list_ref[DET, 0]
-    rows = lax.broadcasted_iota(jnp.int32, (PIX, LANE), 0)
+    rows = lax.broadcasted_iota(jnp.int32, (PIX, LANE), 0).astype(jnp.float32).astype(jnp.bfloat16)
 
     def body(step, _):
         for u in range(UNROLL):
@@ -367,8 +376,8 @@
             at = (r, pl.ds(d, 1), slice(None))
             col_high = frac_ref[z, 1, *at]
             row_high = frac_ref[z, 0, *at]
-            col_weight = spread(hit_ref[z, 1, *at], low_of(col_high), col_high, rows).astype(jnp.bfloat16)
-            row_weight = spread(hit_ref[z, 0, *at], low_of(row_high), row_high, rows)
+            col_weight = spread(hit_ref[z, 1, *at], low_of(col_high), col_high, rows)
+            row_weight = spread(hit_ref[z, 0, *at], low_of(row_high), row_high, rows).astype(jnp.float32)
             partial = jnp.dot(tiles_ref[tile], col_weight, preferred_element_type=jnp.float32)
             value = [
                 jnp.sum(partial[p * PIX : (p + 1) * PIX] * row_weight, axis=0, keepdims=True) for p in range(3)
@@ -389,16 +398,17 @@
         out_shape=(jax.ShapeDtypeStruct(block, f32), jax.ShapeDtypeStruct(pair, f32)),
         in_specs=[SM, VM, VM, VM],
         out_specs=(VM, VM),
-        scratch_shapes=[pltpu.VMEM(pair, jnp.int32), pltpu.VMEM(pair, f32)],
+        scratch_shapes=[pltpu.VMEM(pair, f32), pltpu.VMEM(pair, f32)],
         name="forward",
     )(order, tiles, floats, fracs)
 
 
 def backward_kernel(list_ref, f_ref, w_ref, cs_ref, filt_ref, acc_ref, hit_ref, frac_ref):
     def prepare(z, _):
-        code = f_ref[z, 0].astype(jnp.int32)
-        hit_ref[z, 0] = code // PIX
-        hit_ref[z, 1] = code % PIX
+        code = f_ref[z, 0]
+        row = jnp.floor(code * (1.0 / PIX))
+        hit_ref[z, 0] = row
+        hit_ref[z, 1] = code - row * PIX
         frac_ref[z, 0] = w_ref[z, 0].astype(jnp.float32)
         frac_ref[z, 1] = w_ref[z, 1].astype(jnp.float32)
         return 0
@@ -411,7 +421,7 @@
 
     lax.fori_loop(0, TILE_DEV * NZ, clear, 0)
     count = list_ref[DET, 0]
-    rows = lax.broadcasted_iota(jnp.int32, (PIX, LANE), 0)
+    rows = lax.broadcasted_iota(jnp.int32, (PIX, LANE), 0).astype(jnp.float32).astype(jnp.bfloat16)
 
     def body(step, _):
         for u in range(UNROLL):
@@ -421,13 +431,13 @@
             col_high = frac_ref[z, 1, *at]
             row_high = frac_ref[z, 0, *at]
             row_low = low_of(row_high)
-            col_weight = spread(hit_ref[z, 1, *at], low_of(col_high), col_high, rows).astype(jnp.bfloat16)
+            col_weight = spread(hit_ref[z, 1, *at], low_of(col_high), col_high, rows)
             filt = jnp.where(k < count, filt_ref[z, d, pl.ds(r, 1), :], 0.0)
             hit = hit_ref[z, 0, *at]
             parts = []
             for p in range(3):
                 scaled = filt if p == 0 else cs_ref[z, p - 1, *at] * filt
-                parts.append(spread(hit, scaled * row_low, scaled * row_high, rows).astype(jnp.bfloat16))
+                parts.append(spread(hit, scaled * row_low, scaled * row_high, rows))
             weighted = jnp.concatenate(parts, axis=0)
             acc_ref[tile] += lax.dot_general(
                 weighted, col_weight, (((1,), (1,)), ((), ())), preferred_element_type=jnp.float32
@@ -445,7 +455,7 @@
         out_shape=jax.ShapeDtypeStruct((TILE_DEV * NZ, 3 * PIX, PIX), f32),
         in_specs=[SM, VM, VM, VM, VM],
         out_specs=VM,
-        scratch_shapes=[pltpu.VMEM(pair, jnp.int32), pltpu.VMEM(pair, f32)],
+        scratch_shapes=[pltpu.VMEM(pair, f32), pltpu.VMEM(pair, f32)],
         name="backward",
     )(order, floats, fracs, turns, filtered)
 

time: 123 us -> 109 us (0.89); the launches traced: 124 us -> 108 us
  Pallas kernels: 122 us -> 106 us
    pallas_call x1, Pallas kernels: 15.7 us -> 9.27 us  [backward(): pl.pallas_call(backward_kernel, out_shape=jax.ShapeDtypeStruct((TILE_DEV...]
    pallas_call x1, Pallas kernels: 13.2 us -> 8.68 us  [forward(): pl.pallas_call(forward_kernel, out_shape=(jax.ShapeDtypeStruct(block, f32...]
    pallas_call x1, Pallas kernels: 28.3 us -> 25.8 us  [filtered_of(): pl.pallas_call(filter_kernel, out_shape=jax.ShapeDtypeStruct((NB, *block)...]
    pallas_call x1, Pallas kernels: 29.8 us -> 27.4 us  [collect(): pl.pallas_call(collect_kernel, out_shape=jax.ShapeDtypeStruct(quarter, f3...]
where the time goes in v3:
time: 109 us; the launch traced here: 108 us
  Pallas kernels  106 us (97%)
  local copies, waits for them, and re-layouts  1.54 us (1%)
    pallas_call x1, Pallas kernels, gather_all(): pl.pallas_call(gather_kernel, out_shape=(jax.ShapeDtypeStruct((NZ, TILE_D...  33.7 us
    pallas_call x1, Pallas kernels, collect(): pl.pallas_call(collect_kernel, out_shape=jax.ShapeDtypeStruct(quarter, f3...  27.4 us
    pallas_call x1, Pallas kernels, filtered_of(): pl.pallas_call(filter_kernel, out_shape=jax.ShapeDtypeStruct((NB, *block)...  25.8 us
    pallas_call x1, Pallas kernels, backward(): pl.pallas_call(backward_kernel, out_shape=jax.ShapeDtypeStruct((TILE_DEV...  9.27 us
    pallas_call x1, Pallas kernels, forward(): pl.pallas_call(forward_kernel, out_shape=(jax.ShapeDtypeStruct(block, f32...  8.68 us

profile of v3, /device:TPU:1, one launch (start us, length us, event | category | flops | bytes accessed | tf_op | source)
XLA Modules:
  0.0 108.0 jit_solution(507499974061729130)
XLA Ops:
  0.0 1.7 %pack.1 = (f32[2,16,8,128]{3,2,1,0:T(8,128)}, bf16[2,16,8,128]{3,2,1,0:T(8,128)(2,1)}, s32[8,16]{1,0:T(8,128)}) custom-call(s32[128]{0:T(128)} %home_ref.1, s32[1,32]{1,0:T(1,128)} %bitcast.5, s32[8,16]{1,0:T(8,128)} %slot_ref.1, s32[8,2048]{1,0:T(8,128)} %row_ref.1, s32[8,2048]{1,0:T(8,128)} %col_ref.1, bf16[8,2048]{1,0:T(8,128)(2,1)} %low_ref.1, ...), custom_call_target="tpu_custom_call" | custom-call | tf_op jit(solution)/shard_map/pack/pallas_call | solution.py:77
  1.7 33.7 %gather_all.1 = (bf16[8,2,3,128,128]{4,3,2,1,0:T(8,128)(2,1)}, f32[8,2,16,8,128]{4,3,2,1,0:T(8,128)}, bf16[8,2,16,8,128]{4,3,2,1,0:T(8,128)(2,1)}, s32[16,128]{1,0:T(8,128)}) custom-call(bf16[2,3,32,128]{3,2,1,0:T(8,128)(2,1)} %q_ref.1, f32[2,16,8,128]{3,2,1,0:T(8,128)} %get-tuple-element.14.f_ref, bf16[2,16,8,128]{3,2,1,0:T(8,128)(2,1)} %get-tuple-element.15.w_ref, ...), custom_call_target="tpu_custom_call" | custom-call | tf_op jit(solution)/shard_map/gather_all/pallas_call | solution.py:284
  35.4 8.7 %forward.1 = (f32[8,8,16,128]{3,2,1,0:T(8,128)}, f32[8,2,16,8,128]{4,3,2,1,0:T(8,128)}) custom-call(s32[16,128]{1,0:T(8,128)} %get-tuple-element.17.list_ref, bf16[16,384,128]{2,1,0:T(8,128)(2,1)} %bitcast.4, f32[8,2,16,8,128]{4,3,2,1,0:T(8,128)} %get-tuple-element.18.f_ref, bf16[8,2,16,8,128]{4,3,2,1,0:T(8,128)(2,1)} %get-tuple-element.19.w_ref), custom_call_target="tpu_custom_call" | custom-call | tf_op jit(solution)/shard_map/forward/pallas_call | solution.py:396
  44.0 25.8 %filter.1.filt_ref = f32[8,8,16,128]{3,2,1,0:T(8,128)} custom-call(f32[8,8,16,128]{3,2,1,0:T(8,128)} %get-tuple-element.22.part_ref, f32[8,1025]{1,0:T(8,128)} %noise_ref.1), custom_call_target="tpu_custom_call" | custom-call | tf_op jit(solution)/shard_map/filter/pallas_call | solution.py:581
  69.8 9.3 %backward.1 = f32[16,384,128]{2,1,0:T(8,128)} custom-call(s32[16,128]{1,0:T(8,128)} %get-tuple-element.17.list_ref, f32[8,2,16,8,128]{4,3,2,1,0:T(8,128)} %get-tuple-element.18.f_ref, bf16[8,2,16,8,128]{4,3,2,1,0:T(8,128)(2,1)} %get-tuple-element.19.w_ref, f32[8,2,16,8,128]{4,3,2,1,0:T(8,128)} %get-tuple-element.21.cs_ref, f32[8,8,16,128]{3,2,1,0:T(8,128)} %filter.1.filt_ref), custom_call_target="tpu_custom_call" | custom-call | tf_op jit(solution)/shard_map/backward/pallas_call | solution.py:453
  79.1 27.4 %collect.1 = f32[2,3,32,128]{3,2,1,0:T(8,128)} custom-call(f32[8,2,3,2,2,32,128]{6,5,4,3,2,1,0:T(8,128)} %bitcast.3), custom_call_target="tpu_custom_call" | custom-call | tf_op jit(solution)/shard_map/collect/pallas_call | solution.py:700
  106.5 1.5 %copy.12 = f32[2,3,32,128]{3,2,1,0:T(8,128)} copy(f32[2,3,32,128]{3,2,1,0:T(8,128)} %collect.1) | data formatting | bytes 196608

commit v4 on v3

--- a/solution.py
+++ b/solution.py
@@ -18,6 +18,7 @@
 REACH = 8
 UNROLL = 16
 HALF = 16
+SENT = 2
 PIECE_RUNS = DET * RUNS
 ALL_RUNS = NB * PIECE_RUNS
 ANY = pl.BlockSpec(memory_space=pl.ANY)
@@ -56,35 +57,6 @@
     return pltpu.make_async_remote_copy(
         src_ref=src, dst_ref=dst, send_sem=send, recv_sem=recv, device_id=peer, device_id_type=MESH
     )
-
-
-def pack_kernel(home_ref, piece_ref, slot_ref, row_ref, col_ref, low_ref, high_ref, angle_ref, float_ref, frac_ref, pos_ref):
-    for r in range(RUNS):
-        at = slice(r * LANE, (r + 1) * LANE)
-        float_ref[0, r] = (row_ref[:, at] * PIX + col_ref[:, at]).astype(jnp.float32)
-        float_ref[1, r] = angle_ref[:, at]
-        frac_ref[0, r] = low_ref[:, at]
-        frac_ref[1, r] = high_ref[:, at]
-    slots = slot_ref[...]
-    position = jnp.zeros_like(slots)
-    for s in range(LISTED):
-        position = jnp.where(slots == s, home_ref[piece_ref[0, s]], position)
-    pos_ref[...] = position
-
-
-def packed(tile_home, piece_list, run_slot, hit_row, hit_col, frac_row, frac_col, angle):
-    shape = (2, RUNS, DET, LANE)
-    return pl.pallas_call(
-        pack_kernel,
-        out_shape=(
-            jax.ShapeDtypeStruct(shape, jnp.float32),
-            jax.ShapeDtypeStruct(shape, jnp.bfloat16),
-            jax.ShapeDtypeStruct((DET, RUNS), jnp.int32),
-        ),
-        in_specs=[SM, SM] + [VM] * 6,
-        out_specs=(VM, VM, VM),
-        name="pack",
-    )(tile_home, piece_list, run_slot, hit_row, hit_col, frac_row, frac_col, angle)
 
 
 def run_order(pos_ref, order_ref, y, x):
@@ -122,20 +94,37 @@
     order_ref[DET:, :] = jnp.broadcast_to(count, (DET, LANE)).astype(i32)
 
 
+def pack(home_ref, piece_ref, slot_ref, row_ref, col_ref, low_ref, high_ref, angle_ref, f_own, w_own, p_own):
+    for r in range(RUNS):
+        at = slice(r * LANE, (r + 1) * LANE)
+        f_own[0, r] = (row_ref[:, at] * PIX + col_ref[:, at]).astype(jnp.float32)
+        f_own[1, r] = angle_ref[:, at]
+        w_own[0, r] = low_ref[:, at]
+        w_own[1, r] = high_ref[:, at]
+    slots = slot_ref[...]
+    position = jnp.zeros_like(slots)
+    for s in range(LISTED):
+        position = jnp.where(slots == s, home_ref[piece_ref[0, s]], position)
+    p_own[...] = position
+
+
 def gather_kernel(
-    q_ref, f_ref, w_ref, p_ref, tiles_ref, fo_ref, wo_ref, order_ref,
-    q_own, f_own, w_own, pos_all, load_sem, store_sem,
-    pos_send, pos_recv, block_send, block_recv, ring_send, ring_recv, core_send, core_recv, hi_send, hi_recv,
+    home_ref, piece_ref, slot_ref, row_ref, col_ref, low_ref, high_ref, angle_ref, q_ref,
+    tiles_ref, fo_ref, wo_ref, order_ref,
+    q_own, f_own, w_own, p_own, pos_all, load_sem, store_sem,
+    pos_send, pos_recv, block_send, block_recv, strip_send, strip_recv, core_send, core_recv, hi_send, hi_recv,
 ):
     det, tm, y, z, x = place()
     partner, across = core_of(det), hi_of(det)
-    right, left = tm_of(y, (z + 1) % NZ, x), tm_of(y, (z + NZ - 1) % NZ, x)
     ahead, behind = (y + 1) % NY, (y + NY - 1) % NY
     facing = (y + NY // 2) % NY
     other = 1 - x
     up, down, side = (det, tm_of(ahead, z, x)), (det, tm_of(behind, z, x)), (det, tm_of(y, z, other))
     far = [(det, tm_of((y + dy) % NY, z, (x + dx) % NX)) for dy, dx in PEERS]
 
+    def along(direction, jump):
+        return (det, tm_of(y, (z + jump) % NZ if direction == 0 else (z + NZ - jump) % NZ, x))
+
     def strip(slot, d):
         return tiles_ref.at[slot, :, :, pl.ds(d * STRIP, STRIP), :]
 
@@ -143,18 +132,17 @@
         return fo_ref.at[slot, part] if part < 2 else wo_ref.at[slot]
 
     def own_block(part):
-        return f_ref.at[part] if part < 2 else w_ref
+        return f_own.at[part] if part < 2 else w_own
 
     mine = y * NX + x
-    loads = [
-        pltpu.make_async_copy(q_ref, q_own, load_sem.at[0]),
-        pltpu.make_async_copy(f_ref, f_own, load_sem.at[1]),
-        pltpu.make_async_copy(w_ref, w_own, load_sem.at[2]),
-        pltpu.make_async_copy(p_ref, pos_all.at[mine], load_sem.at[3]),
-    ]
-    for copy in loads:
-        copy.start()
-    greet([(det, right), (det, left), (partner, tm), (across, tm)] + far)
+    load = pltpu.make_async_copy(q_ref, q_own, load_sem)
+    load.start()
+    greeted = [along(d, j) for d in (0, 1) for j in (1, 2)] + [(partner, tm), (across, tm)] + far
+    barrier = pltpu.get_barrier_semaphore()
+    for peer in greeted:
+        pl.semaphore_signal(barrier, inc=1, device_id=peer, device_id_type=MESH)
+    pack(home_ref, piece_ref, slot_ref, row_ref, col_ref, low_ref, high_ref, angle_ref, f_own, w_own, p_own)
+    pl.semaphore_wait(barrier, len(greeted))
 
     started = []
 
@@ -162,9 +150,9 @@
         copy.start()
         started.append(copy)
 
+    start(remote(q_ref, strip(z, det), hi_send, hi_recv, (across, tm)))
     for k, peer in enumerate(far):
-        start(remote(p_ref, pos_all.at[mine], pos_send.at[k], pos_recv.at[k], peer))
-    start(remote(q_ref, strip(z, det), hi_send, hi_recv, (across, tm)))
+        start(remote(p_own, pos_all.at[mine], pos_send.at[k], pos_recv.at[k], peer))
 
     def send_block(link, slot, part, peer, own=False):
         start(
@@ -177,51 +165,67 @@
     def wait_block(link, slot, part):
         remote(own_block(part), block(slot, part), block_send.at[link, part], block_recv.at[link, part], side).wait_recv()
 
+    owner = (det, across)
+
+    def source_slot(direction, distance):
+        return (z + NZ - distance) % NZ if direction == 0 else (z + distance) % NZ
+
+    def send_strip(half, direction, distance):
+        slot = z if distance < 3 else source_slot(direction, 2)
+        here = strip(slot, owner[half])
+        start(
+            remote(
+                q_ref if half == 0 and distance < 3 else here, here,
+                strip_send.at[half, direction, distance - 1], strip_recv.at[half, direction, distance - 1],
+                along(direction, 2 - distance % 2),
+            )
+        )
+
+    def reach(half, direction):
+        return NZ // 2 if half == direction else NZ // 2 - 1
+
+    def to_partner(half, index, slot):
+        here = strip(slot, owner[half])
+        start(
+            remote(
+                q_ref if half == 0 and index == 0 else here, here, core_send.at[half, index], core_recv.at[half, index],
+                (partner, tm),
+            )
+        )
+
+    def take_strip(half, distance):
+        for direction in (0, 1):
+            if distance <= reach(half, direction):
+                slot = source_slot(direction, distance)
+                remote(
+                    q_ref, strip(slot, owner[half]),
+                    strip_send.at[half, direction, distance - 1], strip_recv.at[half, direction, distance - 1], side,
+                ).wait_recv()
+                if distance == 2:
+                    if reach(half, direction) == 4:
+                        send_strip(half, direction, 4)
+                    send_strip(half, direction, 3)
+                to_partner(half, direction * NZ // 2 + distance, slot)
+
+    def first_strips(half):
+        for distance in (2, 1):
+            for direction in (0, 1):
+                send_strip(half, direction, distance)
+        to_partner(half, 0, z)
+
+    first_strips(0)
     for part in range(3):
         send_block(1, mine, part, up, True)
         send_block(2, mine, part, down, True)
         send_block(0, mine, part, side, True)
-
-    def reach(half, direction):
-        return NZ // 2 if half == direction else NZ // 2 - 1
-
-    owner = (det, across)
-
-    def send_strip(half, direction, step):
-        slot = (z + NZ - step) % NZ if direction == 0 else (z + step) % NZ
-        src = q_ref if half == 0 and step == 0 else strip(slot, owner[half])
-        start(
-            remote(
-                src, strip(slot, owner[half]), ring_send.at[half, direction, step], ring_recv.at[half, direction, step],
-                (det, right if direction == 0 else left),
-            )
-        )
-
-    def take_strip(half, step):
-        for direction in (0, 1):
-            if step < reach(half, direction):
-                slot = (z + NZ - step - 1) % NZ if direction == 0 else (z + step + 1) % NZ
-                here = strip(slot, owner[half])
-                remote(q_ref, here, ring_send.at[half, direction, step], ring_recv.at[half, direction, step], side).wait_recv()
-                if step + 1 < reach(half, direction):
-                    send_strip(half, direction, step + 1)
-                index = 1 + direction * NZ // 2 + step
-                start(remote(here, here, core_send.at[half, index], core_recv.at[half, index], (partner, tm)))
-
-    for direction in (0, 1):
-        send_strip(0, direction, 0)
-    start(remote(q_ref, strip(z, det), core_send.at[0, 0], core_recv.at[0, 0], (partner, tm)))
+    load.wait()
     stores = []
-    for i, (src, dst) in enumerate(((q_own, strip(z, det)), (f_own, fo_ref.at[mine]), (w_own, wo_ref.at[mine]))):
-        loads[i].wait()
+    for i, (src, dst) in enumerate(
+        ((q_own, strip(z, det)), (f_own, fo_ref.at[mine]), (w_own, wo_ref.at[mine]), (p_own, pos_all.at[mine]))
+    ):
         copy = pltpu.make_async_copy(src, dst, store_sem.at[i])
         copy.start()
         stores.append(copy)
-
-    remote(q_ref, strip(z, across), hi_send, hi_recv, (across, tm)).wait_recv()
-    for direction in (0, 1):
-        send_strip(1, direction, 0)
-    start(remote(strip(z, across), strip(z, across), core_send.at[1, 0], core_recv.at[1, 0], (partner, tm)))
 
     slot_of = {1: behind * NX + x, 2: ahead * NX + x, 0: y * NX + other, 5: facing * NX + x, 6: facing * NX + other,
                3: behind * NX + other, 4: ahead * NX + other}
@@ -241,63 +245,68 @@
         wait_block(5, slot_of[5], part)
         send_block(6, slot_of[5], part, side)
 
-    take_strip(0, 0)
     near(0)
-    take_strip(1, 0)
+    remote(q_ref, strip(z, across), hi_send, hi_recv, (across, tm)).wait_recv()
+    first_strips(1)
+    take_strip(0, 2)
     near(1)
+    near(2)
     take_strip(0, 1)
-    near(2)
+    opposite(0)
+    take_strip(1, 2)
+    opposite(1)
+    opposite(2)
     take_strip(1, 1)
-    opposite(0)
-    opposite(1)
-    take_strip(0, 2)
-    opposite(2)
-    take_strip(1, 2)
     take_strip(0, 3)
+    take_strip(0, 4)
+
+    stores[3].wait()
+    for k, peer in enumerate(far):
+        remote(p_own, pos_all.at[mine], pos_send.at[k], pos_recv.at[k], peer).wait_recv()
+    run_order(pos_all, order_ref, y, x)
+
     take_strip(1, 3)
-
-    loads[3].wait()
-    for k, peer in enumerate(far):
-        remote(p_ref, pos_all.at[mine], pos_send.at[k], pos_recv.at[k], peer).wait_recv()
-    run_order(pos_all, order_ref, y, x)
-
+    take_strip(1, 4)
     for part in range(3):
         for link in (3, 4, 6):
             wait_block(link, slot_of[link], part)
     theirs = (partner, hi_of(partner))
     for half in (0, 1):
+        places = [(0, z)]
         for direction in (0, 1):
-            for step in range(-1 if direction == 0 else 0, reach(half, direction)):
-                slot = (z + NZ - step - 1) % NZ if direction == 0 else (z + step + 1) % NZ
-                index = 0 if step < 0 else 1 + direction * NZ // 2 + step
-                remote(
-                    q_ref, strip(slot, theirs[half]), core_send.at[half, index], core_recv.at[half, index], (partner, tm)
-                ).wait_recv()
-    for copy in stores:
+            for distance in range(1, reach(half, direction) + 1):
+                places.append((direction * NZ // 2 + distance, source_slot(direction, distance)))
+        for index, slot in places:
+            remote(
+                q_ref, strip(slot, theirs[half]), core_send.at[half, index], core_recv.at[half, index], (partner, tm)
+            ).wait_recv()
+    for copy in stores[:3]:
         copy.wait()
     for copy in started:
         copy.wait_send()
 
 
-def gather_all(quarter, floats, fracs, positions):
+def gather_all(tile_home, piece_list, run_slot, hit_row, hit_col, frac_row, frac_col, angle, quarter):
     bf, f32, i32 = jnp.bfloat16, jnp.float32, jnp.int32
+    samples = (2, RUNS, DET, LANE)
     return pl.pallas_call(
         gather_kernel,
         out_shape=(
             jax.ShapeDtypeStruct((NZ, TILE_DEV, 3, PIX, PIX), bf),
-            jax.ShapeDtypeStruct((NB, *floats.shape), f32),
-            jax.ShapeDtypeStruct((NB, *fracs.shape), bf),
+            jax.ShapeDtypeStruct((NB, *samples), f32),
+            jax.ShapeDtypeStruct((NB, *samples), bf),
             jax.ShapeDtypeStruct((2 * DET, LANE), i32),
         ),
-        in_specs=[ANY] * 4,
+        in_specs=[SM, SM] + [VM] * 6 + [ANY],
         out_specs=(ANY, ANY, ANY, VM),
         scratch_shapes=[
             pltpu.VMEM(quarter.shape, bf),
-            pltpu.VMEM(floats.shape, f32),
-            pltpu.VMEM(fracs.shape, bf),
-            pltpu.VMEM((NB, *positions.shape), i32),
+            pltpu.VMEM(samples, f32),
+            pltpu.VMEM(samples, bf),
+            pltpu.VMEM((DET, RUNS), i32),
+            pltpu.VMEM((NB, DET, RUNS), i32),
+            DMA,
             DMA((4,)),
-            DMA((3,)),
             DMA((NB,)),
             DMA((NB,)),
             DMA((7, 3)),
@@ -311,7 +320,7 @@
         ],
         compiler_params=pltpu.CompilerParams(collective_id=0, has_side_effects=True),
         name="gather_all",
-    )(quarter, floats, fracs, positions)
+    )(tile_home, piece_list, run_slot, hit_row, hit_col, frac_row, frac_col, angle, quarter)
 
 
 def sin_cos(v):
@@ -497,7 +506,7 @@
 
 def filter_kernel(
     part_ref, noise_ref, out_ref, land, ext, filt, lags, t_hi, t_lo,
-    own_sem, send, recv, halo_send, halo_recv, back_send, back_recv,
+    own_sem, store_sem, send, recv, halo_send, halo_recv, back_send, back_recv,
 ):
     det, tm, y, z, x = place()
     total_tm = NY * NZ * NX
@@ -540,6 +549,22 @@
     def product(left, right, crossed):
         return lax.dot_general(left, right, CROSSED if crossed else STRAIGHT, preferred_element_type=jnp.float32)
 
+    back, own_copies = [], []
+
+    def back_copy(c, k, source):
+        rows = pl.ds(c * SENT, SENT)
+        return remote(filt.at[rows], out_ref.at[source, rows], back_send.at[k, c], back_recv.at[k, c], peers[k])
+
+    def send_back(c):
+        for k in range(NB - 1):
+            copy = back_copy(c, k, mine)
+            copy.start()
+            back.append(copy)
+        rows = pl.ds(c * SENT, SENT)
+        copy = pltpu.make_async_copy(filt.at[rows], out_ref.at[mine, rows], store_sem.at[c])
+        copy.start()
+        own_copies.append(copy)
+
     for d in range(DET):
         line_all = jnp.concatenate(
             [
@@ -560,16 +585,13 @@
                 both = product(stack, t_hi[d, index], crossed)
                 result += both[:RUNS] + both[RUNS:] + product(high, t_lo[d, index], crossed)
         filt[d] = result
-    back = []
-    for k, peer in enumerate(peers):
-        copy = remote(filt, out_ref.at[mine], back_send.at[k], back_recv.at[k], peer)
-        copy.start()
-        back.append(copy)
-    own = pltpu.make_async_copy(filt, out_ref.at[mine], own_sem)
-    own.start()
-    own.wait()
-    for k, peer in enumerate(peers):
-        remote(filt, out_ref.at[slot(k, -1)], back_send.at[k], back_recv.at[k], peer).wait_recv()
+        if d % SENT == SENT - 1:
+            send_back(d // SENT)
+    for copy in own_copies:
+        copy.wait()
+    for c in range(DET // SENT):
+        for k, peer in enumerate(peers):
+            back_copy(c, k, slot(k, -1)).wait_recv()
     for copy in sends + back + [to_prior, to_later]:
         copy.wait_send()
 
@@ -591,12 +613,13 @@
             pltpu.VMEM(matrices, bf),
             pltpu.VMEM(matrices, bf),
             DMA,
+            DMA((DET // SENT,)),
             DMA((NB,)),
             DMA((NB,)),
             DMA((2,)),
             DMA((2,)),
-            DMA((NB,)),
-            DMA((NB,)),
+            DMA((NB, DET // SENT)),
+            DMA((NB, DET // SENT)),
         ],
         compiler_params=pltpu.CompilerParams(collective_id=1, has_side_effects=True),
         name="filter",
@@ -609,7 +632,7 @@
 
 
 def collect_kernel(
-    acc_ref, out_ref, own, land_core, land, land_hi, total,
+    acc_ref, out_ref, rest_ref, own, land_core, land, land_hi, total,
     own_sem, core_send, core_recv, ring_send, ring_recv, hi_send, hi_recv,
 ):
     det, tm, y, z, x = place()
@@ -686,9 +709,10 @@
             value = value + land[direction, HALF_Z - 1, t, p]
         total[t, p] = value
         start(across_copy(c))
+        out_ref[t, p] = total[t, p, hi]
     for c, (t, p) in enumerate(CHUNKS):
         across_copy(c).wait_recv()
-        out_ref[t, p] = total[t, p, hi] + land_hi[t, p]
+        rest_ref[t, p] = land_hi[t, p]
     for copy in started:
         copy.wait_send()
 
@@ -699,9 +723,9 @@
     quarter = (TILE_DEV, 3, STRIP, PIX)
     return pl.pallas_call(
         collect_kernel,
-        out_shape=jax.ShapeDtypeStruct(quarter, f32),
+        out_shape=(jax.ShapeDtypeStruct(quarter, f32),) * 2,
         in_specs=[ANY],
-        out_specs=VM,
+        out_specs=(VM, VM),
         scratch_shapes=[
             pltpu.VMEM((NZ, *half), f32),
             pltpu.VMEM((NZ, *half), f32),
@@ -724,14 +748,14 @@
 def body(
     sky_map, tile_home, piece_tiles, run_slot, hit_row, hit_col, frac_row, frac_col, angle, noise_coef
 ):
-    floats, fracs, positions = packed(
-        tile_home, piece_tiles.reshape(1, LISTED), run_slot, hit_row, hit_col, frac_row, frac_col, angle
+    tiles, all_floats, all_fracs, order = gather_all(
+        tile_home, piece_tiles.reshape(1, LISTED), run_slot, hit_row, hit_col, frac_row, frac_col, angle, sky_map
     )
-    tiles, all_floats, all_fracs, order = gather_all(sky_map, floats, fracs, positions)
     partial, turns = forward(order, tiles.reshape(TILE_DEV * NZ, 3 * PIX, PIX), all_floats, all_fracs)
     filtered = filtered_of(partial, noise_coef)
     acc = backward(order, all_floats, all_fracs, turns, filtered)
-    return collect(acc)
+    near, rest = collect(acc)
+    return near + rest
 
 
 def solution(mesh):

time: 109 us -> 104 us (0.954)
  Pallas kernels: 106 us -> 102 us
  other arithmetic: 0 us -> 1.6 us
  local copies, waits for them, and re-layouts: 1.54 us -> 0 us
    pallas_call x1, Pallas kernels: 33.7 us -> 29.1 us  [gather_all(): pl.pallas_call(gather_kernel, out_shape=(jax.ShapeDtypeStruct((NZ, TILE_D...]
    pallas_call x2 -> x1, Pallas kernels: 29.1 us -> 27.4 us  [collect(): pl.pallas_call(collect_kernel, out_shape=(jax.ShapeDtypeStruct(quarter, f...]
    add x0 -> x1, other arithmetic: none -> 1.6 us  [body(): return near + rest]
    pallas_call x1, Pallas kernels: 25.8 us -> 27.3 us  [filtered_of(): pl.pallas_call(filter_kernel, out_shape=jax.ShapeDtypeStruct((NB, *block)...]
    unnamed x1 -> x0, local copies, waits for them, and re-layouts: 1.54 us -> none
where the time goes in v4:
time: 104 us; the launch traced here: 103 us
  Pallas kernels  102 us (98%)
  other arithmetic  1.6 us (2%)
    pallas_call x1, Pallas kernels, gather_all(): pl.pallas_call(gather_kernel, out_shape=(jax.ShapeDtypeStruct((NZ, TILE_D...  29.1 us
    pallas_call x1, Pallas kernels, collect(): pl.pallas_call(collect_kernel, out_shape=(jax.ShapeDtypeStruct(quarter, f...  27.4 us
    pallas_call x1, Pallas kernels, filtered_of(): pl.pallas_call(filter_kernel, out_shape=jax.ShapeDtypeStruct((NB, *block)...  27.3 us
    pallas_call x1, Pallas kernels, backward(): pl.pallas_call(backward_kernel, out_shape=jax.ShapeDtypeStruct((TILE_DEV...  9.26 us
    pallas_call x1, Pallas kernels, forward(): pl.pallas_call(forward_kernel, out_shape=(jax.ShapeDtypeStruct(block, f32...  8.68 us

profile of v4, /device:TPU:1, one launch (start us, length us, event | category | flops | bytes accessed | tf_op | source)
XLA Modules:
  0.0 103.4 jit_solution(5232792067833508442)
XLA Ops:
  0.0 29.1 %gather_all.1 = (bf16[8,2,3,128,128]{4,3,2,1,0:T(8,128)(2,1)}, f32[8,2,16,8,128]{4,3,2,1,0:T(8,128)}, bf16[8,2,16,8,128]{4,3,2,1,0:T(8,128)(2,1)}, s32[16,128]{1,0:T(8,128)}) custom-call(s32[128]{0:T(128)} %home_ref.1, s32[1,32]{1,0:T(1,128)} %bitcast.5, s32[8,16]{1,0:T(8,128)} %slot_ref.1, s32[8,2048]{1,0:T(8,128)} %row_ref.1, s32[8,2048]{1,0:T(8,128)} %col_ref.1, ...), custom_call_target="tpu_custom_call" | custom-call | tf_op jit(solution)/shard_map/gather_all/pallas_call | solution.py:292
  29.1 8.7 %forward.1 = (f32[8,8,16,128]{3,2,1,0:T(8,128)}, f32[8,2,16,8,128]{4,3,2,1,0:T(8,128)}) custom-call(s32[16,128]{1,0:T(8,128)} %get-tuple-element.13.list_ref, bf16[16,384,128]{2,1,0:T(8,128)(2,1)} %bitcast.4, f32[8,2,16,8,128]{4,3,2,1,0:T(8,128)} %get-tuple-element.14.f_ref, bf16[8,2,16,8,128]{4,3,2,1,0:T(8,128)(2,1)} %get-tuple-element.15.w_ref), custom_call_target="tpu_custom_call" | custom-call | tf_op jit(solution)/shard_map/forward/pallas_call | solution.py:405
  37.8 27.3 %filter.1.filt_ref = f32[8,8,16,128]{3,2,1,0:T(8,128)} custom-call(f32[8,8,16,128]{3,2,1,0:T(8,128)} %get-tuple-element.18.part_ref, f32[8,1025]{1,0:T(8,128)} %noise_ref.1), custom_call_target="tpu_custom_call" | custom-call | tf_op jit(solution)/shard_map/filter/pallas_call | solution.py:603
  65.1 9.3 %backward.1 = f32[16,384,128]{2,1,0:T(8,128)} custom-call(s32[16,128]{1,0:T(8,128)} %get-tuple-element.13.list_ref, f32[8,2,16,8,128]{4,3,2,1,0:T(8,128)} %get-tuple-element.14.f_ref, bf16[8,2,16,8,128]{4,3,2,1,0:T(8,128)(2,1)} %get-tuple-element.15.w_ref, f32[8,2,16,8,128]{4,3,2,1,0:T(8,128)} %get-tuple-element.17.cs_ref, f32[8,8,16,128]{3,2,1,0:T(8,128)} %filter.1.filt_ref), custom_call_target="tpu_custom_call" | custom-call | tf_op jit(solution)/shard_map/backward/pallas_call | solution.py:462
  74.4 27.4 %collect.1 = (f32[2,3,32,128]{3,2,1,0:T(8,128)}, f32[2,3,32,128]{3,2,1,0:T(8,128)}) custom-call(f32[8,2,3,2,2,32,128]{6,5,4,3,2,1,0:T(8,128)} %bitcast.3), custom_call_target="tpu_custom_call" | custom-call | tf_op jit(solution)/shard_map/collect/pallas_call | solution.py:724
  101.8 1.6 %add.3 = f32[2,3,32,128]{3,2,1,0:T(8,128)} add(f32[2,3,32,128]{3,2,1,0:T(8,128)} %get-tuple-element.19, f32[2,3,32,128]{3,2,1,0:T(8,128)} %get-tuple-element.20) | non-fusion elementwise | flops 24576 | bytes 294912 | tf_op jit(solution)/shard_map/add | solution.py:758

commit v5 on v4

--- a/solution.py
+++ b/solution.py
@@ -60,38 +60,53 @@
 
 
 def run_order(pos_ref, order_ref, y, x):
-    f32, i32 = jnp.float32, jnp.int32
-    lanes = lax.broadcasted_iota(i32, (RUNS, LANE), 1)
-    offset = lax.broadcasted_iota(i32, (RUNS, LANE), 0)
+    f32, bf, i32 = jnp.float32, jnp.bfloat16, jnp.int32
+
+    def iota(shape, dim):
+        return lax.broadcasted_iota(i32, shape, dim)
+
+    def whole(mask):
+        return jnp.where(mask, 1.0, 0.0).astype(bf)
+
+    def dot(left, right):
+        return jnp.dot(left, right, preferred_element_type=f32)
+
+    lanes, offset = iota((RUNS, LANE), 1), iota((RUNS, LANE), 0)
     spot = jnp.zeros((DET, LANE), f32)
     for slot in range(NB):
-        placed = (lanes == offset + slot * RUNS).astype(f32).astype(jnp.bfloat16)
-        spot += jnp.dot(pos_ref[slot].astype(f32).astype(jnp.bfloat16), placed, preferred_element_type=f32)
+        spot += dot(pos_ref[slot].astype(f32).astype(bf), whole(lanes == offset + slot * RUNS))
     pos = spot.astype(i32)
     here = (pos // (TILE_DEV * NX * NZ) == y) & ((pos // TILE_DEV) % NX == x)
     tile = ((pos // (TILE_DEV * NX)) % NZ) * TILE_DEV + pos % TILE_DEV
-    run = lax.broadcasted_iota(i32, (DET, LANE), 0) * LANE + lax.broadcasted_iota(i32, (DET, LANE), 1)
-    key = (jnp.where(here, tile, TILE_DEV * NZ) * ALL_RUNS + run).astype(f32)
-    entry_t = (tile * ALL_RUNS + run).astype(f32).T
-    key_t = key.T
-    square = (LANE, LANE)
-    ranks = []
+    kinds, square = (2 * TILE_DEV * NZ, LANE), (LANE, LANE)
+    kind = jnp.where(here, tile, TILE_DEV * NZ)
+    tile = tile.astype(f32)
+    before, every = whole(iota(square, 0) < iota(square, 1)), jnp.ones(square, bf)
+    marks, prior, total = [], [], jnp.zeros(kinds, f32)
     for d in range(DET):
-        mine = jnp.broadcast_to(key[d : d + 1], square)
-        less = jnp.zeros(square, f32)
-        for e in range(DET):
-            less += jnp.where(jnp.broadcast_to(key_t[:, e : e + 1], square) < mine, 1.0, 0.0)
-        ranks.append(jnp.sum(less, axis=0, keepdims=True))
-    rank_t = jnp.concatenate(ranks, axis=0).T
-    place = lax.broadcasted_iota(i32, square, 1).astype(f32)
+        mark = whole(jnp.broadcast_to(kind[d : d + 1], kinds) == iota(kinds, 0))
+        marks.append(mark.astype(f32))
+        prior.append(dot(mark, before) + total)
+        total += dot(mark, every)
+    lower = whole(iota((kinds[0], kinds[0]), 1) < iota((kinds[0], kinds[0]), 0))
+    coarse = jnp.floor(total * (1.0 / 32.0))
+    base = 32.0 * dot(lower, coarse.astype(bf)) + dot(lower, (total - 32.0 * coarse).astype(bf))
+    high_rows, low_rows = iota((DET, LANE), 0).astype(f32), iota(square, 0).astype(f32)
+    lane = iota((DET, LANE), 1).astype(f32)
+    found = jnp.zeros((3 * DET, LANE), f32)
     for d in range(DET):
-        found = jnp.zeros(square, f32)
-        for e in range(DET):
-            at = jnp.broadcast_to(rank_t[:, e : e + 1], square) - (d * LANE)
-            found += jnp.where(at == place, jnp.broadcast_to(entry_t[:, e : e + 1], square), 0.0)
-        order_ref[d : d + 1, :] = jnp.sum(found, axis=0, keepdims=True).astype(i32)
-    count = jnp.sum(jnp.sum(here.astype(f32), axis=1, keepdims=True), axis=0, keepdims=True)
-    order_ref[DET:, :] = jnp.broadcast_to(count, (DET, LANE)).astype(i32)
+        rank = jnp.sum(marks[d] * (prior[d] + base), axis=0, keepdims=True)
+        high = jnp.floor(rank * (1.0 / LANE))
+        low = rank - LANE * high
+        at = jnp.broadcast_to(high, (DET, LANE)) == high_rows
+        values = (jnp.broadcast_to(tile[d : d + 1], (DET, LANE)), jnp.full((DET, LANE), float(d), f32), lane)
+        left = jnp.concatenate([jnp.where(at, v, 0.0) for v in values], axis=0).astype(bf)
+        right = whole(jnp.broadcast_to(low, square) == low_rows)
+        found += lax.dot_general(left, right, (((1,), (1,)), ((), ())), preferred_element_type=f32)
+    entry = found[:DET] * ALL_RUNS + found[DET : 2 * DET] * LANE + found[2 * DET :]
+    order_ref[:DET, :] = entry.astype(i32)
+    others = total[TILE_DEV * NZ : TILE_DEV * NZ + 1]
+    order_ref[DET:, :] = jnp.broadcast_to(ALL_RUNS - others, (DET, LANE)).astype(i32)
 
 
 def pack(home_ref, piece_ref, slot_ref, row_ref, col_ref, low_ref, high_ref, angle_ref, f_own, w_own, p_own):
@@ -628,23 +643,26 @@
 
 CHUNKS = [(t, p) for t in range(TILE_DEV) for p in range(3)]
 HALF_Z = NZ // 2
+WIRE = jnp.bfloat16
 OFFSETS = [4, 3, -3, 2, -2, 1, -1, 0]
 
 
 def collect_kernel(
-    acc_ref, out_ref, rest_ref, own, land_core, land, land_hi, total,
-    own_sem, core_send, core_recv, ring_send, ring_recv, hi_send, hi_recv,
+    acc_ref, out_ref, own, land_core, packet, land, land_last, land_own,
+    own_sem, core_send, core_recv, ring_send, ring_recv, last_send, last_recv, hi_send, hi_recv,
 ):
+    f32 = jnp.float32
     det, tm, y, z, x = place()
     core, hi = det % 2, det // 2
     partner, across = core_of(det), hi_of(det)
-    neighbours = ((det, tm_of(y, (z + 1) % NZ, x)), (det, tm_of(y, (z + NZ - 1) % NZ, x)))
+    right, left = tm_of(y, (z + 1) % NZ, x), tm_of(y, (z + NZ - 1) % NZ, x)
+    neighbours = ((det, right), (det, left))
     loads = []
     for k, offset in enumerate(OFFSETS):
         copy = pltpu.make_async_copy(acc_ref.at[(z + offset + NZ) % NZ, :, :, :, core], own.at[k], own_sem.at[k])
         copy.start()
         loads.append(copy)
-    greet([(partner, tm), (across, tm), *neighbours])
+    greet([(partner, tm), (across, tm), *neighbours, (across, right), (across, left)])
     started = []
 
     def start(copy):
@@ -664,9 +682,22 @@
         sign = 1 if direction == 0 else -1
         k = OFFSETS.index(sign * (HALF_Z - step)) if step else 0
         return remote(
-            own.at[k, t, p], land.at[direction, step, t, p],
+            packet.at[k, t, p], land.at[direction, step, t, p],
             ring_send.at[direction, step, c], ring_recv.at[direction, step, c], neighbours[direction],
         )
+
+    def last_hop(direction, c, crossing):
+        t, p = CHUNKS[c]
+        k = OFFSETS.index(1 if direction == 0 else -1)
+        goal = (right, left)[direction]
+        return remote(
+            packet.at[k, t, p, 1 - hi if crossing else hi], land_last.at[crossing, direction, t, p],
+            last_send.at[crossing, direction, c], last_recv.at[crossing, direction, c],
+            (across if crossing else det, goal),
+        )
+
+    def own_copy(t):
+        return remote(packet.at[len(OFFSETS) - 1, t, :, 1 - hi], land_own.at[t], hi_send.at[t], hi_recv.at[t], (across, tm))
 
     def swapped(k):
         loads[k].wait()
@@ -676,10 +707,11 @@
     for direction in (0, 1):
         for c, (t, p) in enumerate(CHUNKS):
             if t == direction:
-                own[0, t, p] = own[0, t, p] + land_core[0, t, p]
+                packet[0, t, p] = (own[0, t, p] + land_core[0, t, p]).astype(WIRE)
     for p in range(3):
         for direction in (0, 1):
             start(ring(direction, 0, direction * 3 + p))
+    last = len(OFFSETS) - 1
     for step in range(1, HALF_Z):
         keys = [OFFSETS.index(HALF_Z - step), OFFSETS.index(step - HALF_Z)]
         for k in keys:
@@ -692,27 +724,29 @@
                 value = own[k, t, p] + land_core[k, t, p]
                 if step > 1 or t == direction:
                     ring(direction, step - 1, c).wait_recv()
-                    value = value + land[direction, step - 1, t, p]
-                own[k, t, p] = value
-                start(ring(direction, step, c))
-    last = len(OFFSETS) - 1
-    swapped(last)
-
-    def across_copy(c):
-        t, p = CHUNKS[c]
-        return remote(total.at[t, p, 1 - hi], land_hi.at[t, p], hi_send.at[c], hi_recv.at[c], (across, tm))
-
+                    value = value + land[direction, step - 1, t, p].astype(f32)
+                packet[k, t, p] = value.astype(WIRE)
+                if step < HALF_Z - 1:
+                    start(ring(direction, step, c))
+                else:
+                    start(last_hop(direction, c, 1))
+                    start(last_hop(direction, c, 0))
+        if step == 1:
+            swapped(last)
+            for t in range(TILE_DEV):
+                value = own[last, t] + land_core[last, t]
+                packet[last, t] = value.astype(WIRE)
+                start(own_copy(t))
+                own[last, t] = value
+    for t in range(TILE_DEV):
+        own_copy(t).wait_recv()
     for c, (t, p) in enumerate(CHUNKS):
-        value = own[last, t, p] + land_core[last, t, p]
-        for direction in (0, 1):
-            ring(direction, HALF_Z - 1, c).wait_recv()
-            value = value + land[direction, HALF_Z - 1, t, p]
-        total[t, p] = value
-        start(across_copy(c))
-        out_ref[t, p] = total[t, p, hi]
-    for c, (t, p) in enumerate(CHUNKS):
-        across_copy(c).wait_recv()
-        rest_ref[t, p] = land_hi[t, p]
+        value = own[last, t, p, hi] + land_own[t, p].astype(f32)
+        for crossing in (0, 1):
+            for direction in (0, 1):
+                last_hop(direction, c, crossing).wait_recv()
+                value = value + land_last[crossing, direction, t, p].astype(f32)
+        out_ref[t, p] = value
     for copy in started:
         copy.wait_send()
 
@@ -723,22 +757,25 @@
     quarter = (TILE_DEV, 3, STRIP, PIX)
     return pl.pallas_call(
         collect_kernel,
-        out_shape=(jax.ShapeDtypeStruct(quarter, f32),) * 2,
+        out_shape=jax.ShapeDtypeStruct(quarter, f32),
         in_specs=[ANY],
-        out_specs=(VM, VM),
+        out_specs=VM,
         scratch_shapes=[
             pltpu.VMEM((NZ, *half), f32),
             pltpu.VMEM((NZ, *half), f32),
-            pltpu.VMEM((2, HALF_Z, *half), f32),
-            pltpu.VMEM(quarter, f32),
-            pltpu.VMEM(half, f32),
+            pltpu.VMEM((NZ, *half), WIRE),
+            pltpu.VMEM((2, HALF_Z - 1, *half), WIRE),
+            pltpu.VMEM((2, 2, *quarter), WIRE),
+            pltpu.VMEM(quarter, WIRE),
             DMA((NZ,)),
             DMA((NZ,)),
             DMA((NZ,)),
-            DMA((2, HALF_Z, 6)),
-            DMA((2, HALF_Z, 6)),
-            DMA((6,)),
-            DMA((6,)),
+            DMA((2, HALF_Z - 1, 6)),
+            DMA((2, HALF_Z - 1, 6)),
+            DMA((2, 2, 6)),
+            DMA((2, 2, 6)),
+            DMA((2,)),
+            DMA((2,)),
         ],
         compiler_params=pltpu.CompilerParams(collective_id=2, has_side_effects=True),
         name="collect",
@@ -754,8 +791,7 @@
     partial, turns = forward(order, tiles.reshape(TILE_DEV * NZ, 3 * PIX, PIX), all_floats, all_fracs)
     filtered = filtered_of(partial, noise_coef)
     acc = backward(order, all_floats, all_fracs, turns, filtered)
-    near, rest = collect(acc)
-    return near + rest
+    return collect(acc)
 
 
 def solution(mesh):

time: 104 us -> 97.9 us (0.941)
  Pallas kernels: 102 us -> 95.8 us
  other arithmetic: 1.6 us -> 0 us
  local copies, waits for them, and re-layouts: 0 us -> 1.54 us
    pallas_call x1, Pallas kernels: 27.4 us -> 22 us  [collect(): pl.pallas_call(collect_kernel, out_shape=jax.ShapeDtypeStruct(quarter, f3...]
    add x1 -> x0, other arithmetic: 1.6 us -> none  [body(): return near + rest]
    unnamed x0 -> x1, local copies, waits for them, and re-layouts: none -> 1.54 us
where the time goes in v5:
time: 97.9 us; the launch traced here: 97.3 us
  Pallas kernels  95.8 us (98%)
  local copies, waits for them, and re-layouts  1.54 us (2%)
    pallas_call x1, Pallas kernels, gather_all(): pl.pallas_call(gather_kernel, out_shape=(jax.ShapeDtypeStruct((NZ, TILE_D...  29 us
    pallas_call x1, Pallas kernels, filtered_of(): pl.pallas_call(filter_kernel, out_shape=jax.ShapeDtypeStruct((NB, *block)...  26.8 us
    pallas_call x1, Pallas kernels, collect(): pl.pallas_call(collect_kernel, out_shape=jax.ShapeDtypeStruct(quarter, f3...  22 us
    pallas_call x1, Pallas kernels, backward(): pl.pallas_call(backward_kernel, out_shape=jax.ShapeDtypeStruct((TILE_DEV...  9.25 us
    pallas_call x1, Pallas kernels, forward(): pl.pallas_call(forward_kernel, out_shape=(jax.ShapeDtypeStruct(block, f32...  8.69 us

profile of v5, /device:TPU:1, one launch (start us, length us, event | category | flops | bytes accessed | tf_op | source)
XLA Modules:
  0.0 97.3 jit_solution(13666018374765418139)
XLA Ops:
  0.0 29.0 %gather_all.1 = (bf16[8,2,3,128,128]{4,3,2,1,0:T(8,128)(2,1)}, f32[8,2,16,8,128]{4,3,2,1,0:T(8,128)}, bf16[8,2,16,8,128]{4,3,2,1,0:T(8,128)(2,1)}, s32[16,128]{1,0:T(8,128)}) custom-call(s32[128]{0:T(128)} %home_ref.1, s32[1,32]{1,0:T(1,128)} %bitcast.5, s32[8,16]{1,0:T(8,128)} %slot_ref.1, s32[8,2048]{1,0:T(8,128)} %row_ref.1, s32[8,2048]{1,0:T(8,128)} %col_ref.1, ...), custom_call_target="tpu_custom_call" | custom-call | tf_op jit(solution)/shard_map/gather_all/pallas_call | solution.py:307
  29.0 8.7 %forward.1 = (f32[8,8,16,128]{3,2,1,0:T(8,128)}, f32[8,2,16,8,128]{4,3,2,1,0:T(8,128)}) custom-call(s32[16,128]{1,0:T(8,128)} %get-tuple-element.11.list_ref, bf16[16,384,128]{2,1,0:T(8,128)(2,1)} %bitcast.4, f32[8,2,16,8,128]{4,3,2,1,0:T(8,128)} %get-tuple-element.12.f_ref, bf16[8,2,16,8,128]{4,3,2,1,0:T(8,128)(2,1)} %get-tuple-element.13.w_ref), custom_call_target="tpu_custom_call" | custom-call | tf_op jit(solution)/shard_map/forward/pallas_call | solution.py:420
  37.7 26.8 %filter.1.filt_ref = f32[8,8,16,128]{3,2,1,0:T(8,128)} custom-call(f32[8,8,16,128]{3,2,1,0:T(8,128)} %get-tuple-element.16.part_ref, f32[8,1025]{1,0:T(8,128)} %noise_ref.1), custom_call_target="tpu_custom_call" | custom-call | tf_op jit(solution)/shard_map/filter/pallas_call | solution.py:618
  64.5 9.3 %backward.1 = f32[16,384,128]{2,1,0:T(8,128)} custom-call(s32[16,128]{1,0:T(8,128)} %get-tuple-element.11.list_ref, f32[8,2,16,8,128]{4,3,2,1,0:T(8,128)} %get-tuple-element.12.f_ref, bf16[8,2,16,8,128]{4,3,2,1,0:T(8,128)(2,1)} %get-tuple-element.13.w_ref, f32[8,2,16,8,128]{4,3,2,1,0:T(8,128)} %get-tuple-element.15.cs_ref, f32[8,8,16,128]{3,2,1,0:T(8,128)} %filter.1.filt_ref), custom_call_target="tpu_custom_call" | custom-call | tf_op jit(solution)/shard_map/backward/pallas_call | solution.py:477
  73.8 22.0 %collect.1 = f32[2,3,32,128]{3,2,1,0:T(8,128)} custom-call(f32[8,2,3,2,2,32,128]{6,5,4,3,2,1,0:T(8,128)} %bitcast.3), custom_call_target="tpu_custom_call" | custom-call | tf_op jit(solution)/shard_map/collect/pallas_call | solution.py:758
  95.8 1.5 %copy.12 = f32[2,3,32,128]{3,2,1,0:T(8,128)} copy(f32[2,3,32,128]{3,2,1,0:T(8,128)} %collect.1) | data formatting | bytes 196608

commit v6 on v5

--- a/solution.py
+++ b/solution.py
@@ -126,6 +126,7 @@
 def gather_kernel(
     home_ref, piece_ref, slot_ref, row_ref, col_ref, low_ref, high_ref, angle_ref, q_ref,
     tiles_ref, fo_ref, wo_ref, order_ref,
+    slot_own, row_own, col_own, low_own, high_own, angle_own,
     q_own, f_own, w_own, p_own, pos_all, load_sem, store_sem,
     pos_send, pos_recv, block_send, block_recv, strip_send, strip_recv, core_send, core_recv, hi_send, hi_recv,
 ):
@@ -150,14 +151,12 @@
         return f_own.at[part] if part < 2 else w_own
 
     mine = y * NX + x
-    load = pltpu.make_async_copy(q_ref, q_own, load_sem)
-    load.start()
-    greeted = [along(d, j) for d in (0, 1) for j in (1, 2)] + [(partner, tm), (across, tm)] + far
-    barrier = pltpu.get_barrier_semaphore()
-    for peer in greeted:
-        pl.semaphore_signal(barrier, inc=1, device_id=peer, device_id_type=MESH)
-    pack(home_ref, piece_ref, slot_ref, row_ref, col_ref, low_ref, high_ref, angle_ref, f_own, w_own, p_own)
-    pl.semaphore_wait(barrier, len(greeted))
+    given = (slot_ref, row_ref, col_ref, low_ref, high_ref, angle_ref, q_ref)
+    held = (slot_own, row_own, col_own, low_own, high_own, angle_own, q_own)
+    loads = [pltpu.make_async_copy(src, dst, load_sem.at[i]) for i, (src, dst) in enumerate(zip(given, held))]
+    for copy in loads:
+        copy.start()
+    greet([along(d, j) for d in (0, 1) for j in (1, 2)] + [(partner, tm), (across, tm)] + far)
 
     started = []
 
@@ -166,8 +165,6 @@
         started.append(copy)
 
     start(remote(q_ref, strip(z, det), hi_send, hi_recv, (across, tm)))
-    for k, peer in enumerate(far):
-        start(remote(p_own, pos_all.at[mine], pos_send.at[k], pos_recv.at[k], peer))
 
     def send_block(link, slot, part, peer, own=False):
         start(
@@ -229,11 +226,15 @@
         to_partner(half, 0, z)
 
     first_strips(0)
+    for copy in loads:
+        copy.wait()
+    pack(home_ref, piece_ref, slot_own, row_own, col_own, low_own, high_own, angle_own, f_own, w_own, p_own)
+    for k, peer in enumerate(far):
+        start(remote(p_own, pos_all.at[mine], pos_send.at[k], pos_recv.at[k], peer))
     for part in range(3):
         send_block(1, mine, part, up, True)
         send_block(2, mine, part, down, True)
         send_block(0, mine, part, side, True)
-    load.wait()
     stores = []
     for i, (src, dst) in enumerate(
         ((q_own, strip(z, det)), (f_own, fo_ref.at[mine]), (w_own, wo_ref.at[mine]), (p_own, pos_all.at[mine]))
@@ -312,15 +313,16 @@
             jax.ShapeDtypeStruct((NB, *samples), bf),
             jax.ShapeDtypeStruct((2 * DET, LANE), i32),
         ),
-        in_specs=[SM, SM] + [VM] * 6 + [ANY],
+        in_specs=[SM, SM] + [ANY] * 7,
         out_specs=(ANY, ANY, ANY, VM),
         scratch_shapes=[
+            *(pltpu.VMEM(v.shape, v.dtype) for v in (run_slot, hit_row, hit_col, frac_row, frac_col, angle)),
             pltpu.VMEM(quarter.shape, bf),
             pltpu.VMEM(samples, f32),
             pltpu.VMEM(samples, bf),
             pltpu.VMEM((DET, RUNS), i32),
             pltpu.VMEM((NB, DET, RUNS), i32),
-            DMA,
+            DMA((7,)),
             DMA((4,)),
             DMA((NB,)),
             DMA((NB,)),
@@ -375,8 +377,28 @@
     return jnp.concatenate(parts, axis=0)
 
 
-def forward_kernel(list_ref, tiles_ref, f_ref, w_ref, sig_ref, cs_ref, hit_ref, frac_ref):
+def forward_kernel(
+    list_ref, tile_hbm, f_hbm, w_hbm, sig_ref, cs_hbm, hit_ref, frac_ref, cs_ref, tiles_ref, f_ref, w_ref,
+    tile_sem, f_sem, w_sem, cs_sem,
+):
+    def f_copy(z):
+        return pltpu.make_async_copy(f_hbm.at[z], f_ref.at[z], f_sem.at[z])
+
+    def w_copy(z):
+        return pltpu.make_async_copy(w_hbm.at[z], w_ref.at[z], w_sem.at[z])
+
+    def cs_copy(z):
+        return pltpu.make_async_copy(cs_ref.at[z], cs_hbm.at[z], cs_sem.at[z])
+
+    for z in range(NB):
+        f_copy(z).start()
+        w_copy(z).start()
+    tile_copy = pltpu.make_async_copy(tile_hbm, tiles_ref, tile_sem)
+    tile_copy.start()
+
     def prepare(z, _):
+        f_copy(z).wait()
+        w_copy(z).wait()
         code = f_ref[z, 0]
         row = jnp.floor(code * (1.0 / PIX))
         hit_ref[z, 0] = row
@@ -384,12 +406,14 @@
         sin, cos = sin_cos(2.0 * f_ref[z, 1])
         cs_ref[z, 0] = cos
         cs_ref[z, 1] = sin
+        cs_copy(z).start()
         frac_ref[z, 0] = w_ref[z, 0].astype(jnp.float32)
         frac_ref[z, 1] = w_ref[z, 1].astype(jnp.float32)
         sig_ref[z] = jnp.zeros_like(sig_ref[z])
         return 0
 
     lax.fori_loop(0, NB, prepare, 0)
+    tile_copy.wait()
     count = list_ref[DET, 0]
     rows = lax.broadcasted_iota(jnp.int32, (PIX, LANE), 0).astype(jnp.float32).astype(jnp.bfloat16)
 
@@ -411,6 +435,8 @@
         return 0
 
     lax.fori_loop(0, (count + UNROLL - 1) // UNROLL, body, 0)
+    for z in range(NB):
+        cs_copy(z).wait()
 
 
 def forward(order, tiles, floats, fracs):
@@ -420,16 +446,54 @@
     return pl.pallas_call(
         forward_kernel,
         out_shape=(jax.ShapeDtypeStruct(block, f32), jax.ShapeDtypeStruct(pair, f32)),
-        in_specs=[SM, VM, VM, VM],
-        out_specs=(VM, VM),
-        scratch_shapes=[pltpu.VMEM(pair, f32), pltpu.VMEM(pair, f32)],
+        in_specs=[SM, ANY, ANY, ANY],
+        out_specs=(VM, ANY),
+        scratch_shapes=[
+            pltpu.VMEM(pair, f32),
+            pltpu.VMEM(pair, f32),
+            pltpu.VMEM(pair, f32),
+            pltpu.VMEM(tiles.shape, tiles.dtype),
+            pltpu.VMEM(pair, f32),
+            pltpu.VMEM(pair, fracs.dtype),
+            DMA,
+            DMA((NB,)),
+            DMA((NB,)),
+            DMA((NB,)),
+        ],
         name="forward",
     )(order, tiles, floats, fracs)
 
 
-def backward_kernel(list_ref, f_ref, w_ref, cs_ref, filt_ref, acc_ref, hit_ref, frac_ref):
+def backward_kernel(
+    list_ref, f_hbm, w_hbm, cs_hbm, filt_hbm, acc_ref, hit_ref, frac_ref, f_ref, w_ref, cs_ref, filt_ref,
+    f_sem, w_sem, late_sem,
+):
+    def f_copy(z):
+        return pltpu.make_async_copy(f_hbm.at[z, 0], f_ref.at[z], f_sem.at[z])
+
+    def w_copy(z):
+        return pltpu.make_async_copy(w_hbm.at[z], w_ref.at[z], w_sem.at[z])
+
+    late = [
+        pltpu.make_async_copy(cs_hbm, cs_ref, late_sem.at[0]),
+        pltpu.make_async_copy(filt_hbm, filt_ref, late_sem.at[1]),
+    ]
+    for z in range(NB):
+        f_copy(z).start()
+        w_copy(z).start()
+    for copy in late:
+        copy.start()
+
+    def clear(t, _):
+        acc_ref[t] = jnp.zeros_like(acc_ref[t])
+        return 0
+
+    lax.fori_loop(0, TILE_DEV * NZ, clear, 0)
+
     def prepare(z, _):
-        code = f_ref[z, 0]
+        f_copy(z).wait()
+        w_copy(z).wait()
+        code = f_ref[z]
         row = jnp.floor(code * (1.0 / PIX))
         hit_ref[z, 0] = row
         hit_ref[z, 1] = code - row * PIX
@@ -438,12 +502,8 @@
         return 0
 
     lax.fori_loop(0, NB, prepare, 0)
-
-    def clear(t, _):
-        acc_ref[t] = jnp.zeros_like(acc_ref[t])
-        return 0
-
-    lax.fori_loop(0, TILE_DEV * NZ, clear, 0)
+    for copy in late:
+        copy.wait()
     count = list_ref[DET, 0]
     rows = lax.broadcasted_iota(jnp.int32, (PIX, LANE), 0).astype(jnp.float32).astype(jnp.bfloat16)
 
@@ -477,9 +537,19 @@
     return pl.pallas_call(
         backward_kernel,
         out_shape=jax.ShapeDtypeStruct((TILE_DEV * NZ, 3 * PIX, PIX), f32),
-        in_specs=[SM, VM, VM, VM, VM],
+        in_specs=[SM, ANY, ANY, ANY, ANY],
         out_specs=VM,
-        scratch_shapes=[pltpu.VMEM(pair, f32), pltpu.VMEM(pair, f32)],
+        scratch_shapes=[
+            pltpu.VMEM(pair, f32),
+            pltpu.VMEM(pair, f32),
+            pltpu.VMEM((NB, RUNS, DET, LANE), f32),
+            pltpu.VMEM(pair, fracs.dtype),
+            pltpu.VMEM(pair, f32),
+            pltpu.VMEM(filtered.shape, f32),
+            DMA((NB,)),
+            DMA((NB,)),
+            DMA((2,)),
+        ],
         name="backward",
     )(order, floats, fracs, turns, filtered)
 
@@ -580,28 +650,34 @@
         copy.start()
         own_copies.append(copy)
 
-    for d in range(DET):
-        line_all = jnp.concatenate(
-            [
-                jnp.where(first, 0.0, ext[d, :REACH]),
-                ext[d, REACH : REACH + RUNS],
-                jnp.where(last, 0.0, ext[d, REACH + RUNS :]),
-            ],
-            axis=0,
-        )
-        result = jnp.zeros((RUNS, LANE), jnp.float32)
+    for c in range(DET // SENT):
+        dets = range(c * SENT, (c + 1) * SENT)
+        lines = [
+            jnp.concatenate(
+                [
+                    jnp.where(first, 0.0, ext[d, :REACH]),
+                    ext[d, REACH : REACH + RUNS],
+                    jnp.where(last, 0.0, ext[d, REACH + RUNS :]),
+                ],
+                axis=0,
+            )
+            for d in dets
+        ]
+        full = [jnp.zeros((2 * RUNS, LANE), jnp.float32) for d in dets]
+        fine = [jnp.zeros((RUNS, LANE), jnp.float32) for d in dets]
         for m in range(2 * REACH + 1):
-            window = line_all[m : m + RUNS]
-            high = window.astype(jnp.bfloat16)
-            low = (window - high.astype(jnp.float32)).astype(jnp.bfloat16)
-            stack = jnp.concatenate([high, low], axis=0)
             q = REACH - m
-            for index, crossed in [(q, False)] if q > 0 else [(-q, True)] if q < 0 else [(0, False), (REACH + 1, True)]:
-                both = product(stack, t_hi[d, index], crossed)
-                result += both[:RUNS] + both[RUNS:] + product(high, t_lo[d, index], crossed)
-        filt[d] = result
-        if d % SENT == SENT - 1:
-            send_back(d // SENT)
+            for i, d in enumerate(dets):
+                window = lines[i][m : m + RUNS]
+                high = window.astype(jnp.bfloat16)
+                low = (window - high.astype(jnp.float32)).astype(jnp.bfloat16)
+                stack = jnp.concatenate([high, low], axis=0)
+                for index, crossed in [(q, False)] if q > 0 else [(-q, True)] if q < 0 else [(0, False), (REACH + 1, True)]:
+                    full[i] += product(stack, t_hi[d, index], crossed)
+                    fine[i] += product(high, t_lo[d, index], crossed)
+        for i, d in enumerate(dets):
+            filt[d] = full[i][:RUNS] + full[i][RUNS:] + fine[i]
+        send_back(c)
     for copy in own_copies:
         copy.wait()
     for c in range(DET // SENT):
@@ -648,8 +724,8 @@
 
 
 def collect_kernel(
-    acc_ref, out_ref, own, land_core, packet, land, land_last, land_own,
-    own_sem, core_send, core_recv, ring_send, ring_recv, last_send, last_recv, hi_send, hi_recv,
+    acc_ref, sum_ref, land_last, land_own, own, land_core, packet, land,
+    own_sem, sum_sem, core_send, core_recv, ring_send, ring_recv, last_send, last_recv, hi_send, hi_recv,
 ):
     f32 = jnp.float32
     det, tm, y, z, x = place()
@@ -738,15 +814,15 @@
                 packet[last, t] = value.astype(WIRE)
                 start(own_copy(t))
                 own[last, t] = value
+            keep = pltpu.make_async_copy(own.at[last, :, :, hi], sum_ref, sum_sem)
+            keep.start()
     for t in range(TILE_DEV):
         own_copy(t).wait_recv()
-    for c, (t, p) in enumerate(CHUNKS):
-        value = own[last, t, p, hi] + land_own[t, p].astype(f32)
+    for c in range(len(CHUNKS)):
         for crossing in (0, 1):
             for direction in (0, 1):
                 last_hop(direction, c, crossing).wait_recv()
-                value = value + land_last[crossing, direction, t, p].astype(f32)
-        out_ref[t, p] = value
+    keep.wait()
     for copy in started:
         copy.wait_send()
 
@@ -757,17 +833,20 @@
     quarter = (TILE_DEV, 3, STRIP, PIX)
     return pl.pallas_call(
         collect_kernel,
-        out_shape=jax.ShapeDtypeStruct(quarter, f32),
+        out_shape=(
+            jax.ShapeDtypeStruct(quarter, f32),
+            jax.ShapeDtypeStruct((2, 2, *quarter), WIRE),
+            jax.ShapeDtypeStruct(quarter, WIRE),
+        ),
         in_specs=[ANY],
-        out_specs=VM,
+        out_specs=(ANY, ANY, ANY),
         scratch_shapes=[
             pltpu.VMEM((NZ, *half), f32),
             pltpu.VMEM((NZ, *half), f32),
             pltpu.VMEM((NZ, *half), WIRE),
             pltpu.VMEM((2, HALF_Z - 1, *half), WIRE),
-            pltpu.VMEM((2, 2, *quarter), WIRE),
-            pltpu.VMEM(quarter, WIRE),
             DMA((NZ,)),
+            DMA,
             DMA((NZ,)),
             DMA((NZ,)),
             DMA((2, HALF_Z - 1, 6)),
@@ -791,7 +870,10 @@
     partial, turns = forward(order, tiles.reshape(TILE_DEV * NZ, 3 * PIX, PIX), all_floats, all_fracs)
     filtered = filtered_of(partial, noise_coef)
     acc = backward(order, all_floats, all_fracs, turns, filtered)
-    return collect(acc)
+    kept, landed, crossed = collect(acc)
+    f32 = jnp.float32
+    straight = landed[0, 0].astype(f32) + landed[0, 1].astype(f32)
+    return kept + crossed.astype(f32) + straight + landed[1, 0].astype(f32) + landed[1, 1].astype(f32)
 
 
 def solution(mesh):

time: 97.9 us -> 97.6 us (level)
  other arithmetic: 0 us -> 1.64 us
  local copies, waits for them, and re-layouts: 1.54 us -> 0 us
    add x0 -> x1, other arithmetic: none -> 1.64 us  [body(): kept + crossed.astype(f32) + straight + landed[1, 0].astype(f32)]
    unnamed x1 -> x0, local copies, waits for them, and re-layouts: 1.54 us -> none
where the time goes in v6:
time: 97.6 us; the launch traced here: 97.5 us
  Pallas kernels  95.8 us (98%)
  other arithmetic  1.64 us (2%)
    pallas_call x1, Pallas kernels, gather_all(): pl.pallas_call(gather_kernel, out_shape=(jax.ShapeDtypeStruct((NZ, TILE_D...  28.8 us
    pallas_call x1, Pallas kernels, filtered_of(): pl.pallas_call(filter_kernel, out_shape=jax.ShapeDtypeStruct((NB, *block)...  26 us
    pallas_call x1, Pallas kernels, collect(): pl.pallas_call(collect_kernel, out_shape=(jax.ShapeDtypeStruct(quarter, f...  22.6 us
    pallas_call x1, Pallas kernels, backward(): pl.pallas_call(backward_kernel, out_shape=jax.ShapeDtypeStruct((TILE_DEV...  9.75 us
    pallas_call x1, Pallas kernels, forward(): pl.pallas_call(forward_kernel, out_shape=(jax.ShapeDtypeStruct(block, f32...  8.66 us

profile of v6, /device:TPU:1, one launch (start us, length us, event | category | flops | bytes accessed | tf_op | source)
XLA Modules:
  0.0 97.5 jit_solution(8316461541522542065)
XLA Ops:
  0.0 28.8 %gather_all.1 = (bf16[8,2,3,128,128]{4,3,2,1,0:T(8,128)(2,1)}, f32[8,2,16,8,128]{4,3,2,1,0:T(8,128)}, bf16[8,2,16,8,128]{4,3,2,1,0:T(8,128)(2,1)}, s32[16,128]{1,0:T(8,128)}) custom-call(s32[128]{0:T(128)} %home_ref.1, s32[1,32]{1,0:T(1,128)} %bitcast.15, s32[8,16]{1,0:T(8,128)} %slot_ref.1, s32[8,2048]{1,0:T(8,128)} %row_ref.1, s32[8,2048]{1,0:T(8,128)} %col_ref.1, ...), custom_call_target="tpu_custom_call" | custom-call | tf_op jit(solution)/shard_map/gather_all/pallas_call | solution.py:308
  28.8 8.7 %forward.1 = (f32[8,8,16,128]{3,2,1,0:T(8,128)}, f32[8,2,16,8,128]{4,3,2,1,0:T(8,128)}) custom-call(s32[16,128]{1,0:T(8,128)} %get-tuple-element.14.list_ref, bf16[16,384,128]{2,1,0:T(8,128)(2,1)} %bitcast.14, f32[8,2,16,8,128]{4,3,2,1,0:T(8,128)} %get-tuple-element.15.f_hbm, bf16[8,2,16,8,128]{4,3,2,1,0:T(8,128)(2,1)} %get-tuple-element.16.w_hbm), custom_call_target="tpu_custom_call" | custom-call | tf_op jit(solution)/shard_map/forward/pallas_call | solution.py:446
  37.4 26.0 %filter.1.filt_hbm = f32[8,8,16,128]{3,2,1,0:T(8,128)} custom-call(f32[8,8,16,128]{3,2,1,0:T(8,128)} %get-tuple-element.19.part_ref, f32[8,1025]{1,0:T(8,128)} %noise_ref.1), custom_call_target="tpu_custom_call" | custom-call | tf_op jit(solution)/shard_map/filter/pallas_call | solution.py:694
  63.4 9.8 %backward.1 = f32[16,384,128]{2,1,0:T(8,128)} custom-call(s32[16,128]{1,0:T(8,128)} %get-tuple-element.14.list_ref, f32[8,2,16,8,128]{4,3,2,1,0:T(8,128)} %get-tuple-element.15.f_hbm, bf16[8,2,16,8,128]{4,3,2,1,0:T(8,128)(2,1)} %get-tuple-element.16.w_hbm, f32[8,2,16,8,128]{4,3,2,1,0:T(8,128)} %get-tuple-element.18.cs_hbm, f32[8,8,16,128]{3,2,1,0:T(8,128)} %filter.1.filt_hbm), custom_call_target="tpu_custom_call" | custom-call | tf_op jit(solution)/shard_map/backward/pallas_call | solution.py:537
  73.2 22.6 %collect.1 = (f32[2,3,32,128]{3,2,1,0:T(8,128)}, bf16[2,2,2,3,32,128]{5,4,3,2,1,0:T(8,128)(2,1)}, bf16[2,3,32,128]{3,2,1,0:T(8,128)(2,1)}) custom-call(f32[8,2,3,2,2,32,128]{6,5,4,3,2,1,0:T(8,128)} %bitcast.13), custom_call_target="tpu_custom_call" | custom-call | tf_op jit(solution)/shard_map/collect/pallas_call | solution.py:834
  95.9 1.6 %convert_add_fusion = f32[2,3,32,128]{3,2,1,0:T(8,128)} fusion(f32[2,3,32,128]{3,2,1,0:T(8,128)} %get-tuple-element.20, bf16[2,3,32,128]{3,2,1,0:T(8,128)(2,1)} %get-tuple-element.21, bf16[2,2,2,3,32,128]{5,4,3,2,1,0:T(8,128)(2,1)} %get-tuple-element.22), kind=kLoop, calls=%fused_computation | loop fusion | flops 245760 | bytes 442368 | tf_op jit(solution)/shard_map/add | solution.py:876

commit v7 on v5

--- a/solution.py
+++ b/solution.py
@@ -7,6 +7,7 @@
 from jax.experimental.pallas import tpu as pltpu
 from jax.sharding import PartitionSpec as P
 
+GRANT = 24 << 20
 MESH = pl.DeviceIdType.MESH
 NY, NZ, NX = 4, 8, 2
 NB = NY * NX
@@ -333,7 +334,7 @@
             DMA,
             DMA,
         ],
-        compiler_params=pltpu.CompilerParams(collective_id=0, has_side_effects=True),
+        compiler_params=pltpu.CompilerParams(collective_id=0, has_side_effects=True, vmem_limit_bytes=GRANT),
         name="gather_all",
     )(tile_home, piece_list, run_slot, hit_row, hit_col, frac_row, frac_col, angle, quarter)
 
@@ -423,6 +424,7 @@
         in_specs=[SM, VM, VM, VM],
         out_specs=(VM, VM),
         scratch_shapes=[pltpu.VMEM(pair, f32), pltpu.VMEM(pair, f32)],
+        compiler_params=pltpu.CompilerParams(vmem_limit_bytes=GRANT),
         name="forward",
     )(order, tiles, floats, fracs)
 
@@ -480,6 +482,7 @@
         in_specs=[SM, VM, VM, VM, VM],
         out_specs=VM,
         scratch_shapes=[pltpu.VMEM(pair, f32), pltpu.VMEM(pair, f32)],
+        compiler_params=pltpu.CompilerParams(vmem_limit_bytes=GRANT),
         name="backward",
     )(order, floats, fracs, turns, filtered)
 
@@ -636,7 +639,7 @@
             DMA((NB, DET // SENT)),
             DMA((NB, DET // SENT)),
         ],
-        compiler_params=pltpu.CompilerParams(collective_id=1, has_side_effects=True),
+        compiler_params=pltpu.CompilerParams(collective_id=1, has_side_effects=True, vmem_limit_bytes=GRANT),
         name="filter",
     )(partial, noise_coef)
 
@@ -777,7 +780,7 @@
             DMA((2,)),
             DMA((2,)),
         ],
-        compiler_params=pltpu.CompilerParams(collective_id=2, has_side_effects=True),
+        compiler_params=pltpu.CompilerParams(collective_id=2, has_side_effects=True, vmem_limit_bytes=GRANT),
         name="collect",
     )(acc.reshape(NZ, TILE_DEV, 3, 2, 2, STRIP, PIX))
 

time: 97.9 us -> 96.2 us (0.983)
  Pallas kernels: 95.8 us -> 87.9 us
  local copies, waits for them, and re-layouts: 1.54 us -> 7.47 us
    unnamed x1 -> x21, local copies, waits for them, and re-layouts: 1.54 us -> 7.47 us
    pallas_call x1, Pallas kernels: 9.25 us -> 5.78 us  [backward(): pl.pallas_call(backward_kernel, out_shape=jax.ShapeDtypeStruct((TILE_DEV...]
    pallas_call x1, Pallas kernels: 8.69 us -> 5.87 us  [forward(): pl.pallas_call(forward_kernel, out_shape=(jax.ShapeDtypeStruct(block, f32...]
    pallas_call x1, Pallas kernels: 29 us -> 26.7 us  [gather_all(): pl.pallas_call(gather_kernel, out_shape=(jax.ShapeDtypeStruct((NZ, TILE_D...]
    pallas_call x1, Pallas kernels: 22 us -> 23.4 us  [collect(): pl.pallas_call(collect_kernel, out_shape=jax.ShapeDtypeStruct(quarter, f3...]
where the time goes in v7:
time: 96.2 us; the launch traced here: 95.5 us
  Pallas kernels  87.9 us (91%)
  local copies, waits for them, and re-layouts  7.47 us (8%)
    pallas_call x1, Pallas kernels, gather_all(): pl.pallas_call(gather_kernel, out_shape=(jax.ShapeDtypeStruct((NZ, TILE_D...  26.7 us
    pallas_call x1, Pallas kernels, filtered_of(): pl.pallas_call(filter_kernel, out_shape=jax.ShapeDtypeStruct((NB, *block)...  26.1 us
    pallas_call x1, Pallas kernels, collect(): pl.pallas_call(collect_kernel, out_shape=jax.ShapeDtypeStruct(quarter, f3...  23.4 us
    unnamed x21, local copies, waits for them, and re-layouts  7.47 us
    pallas_call x1, Pallas kernels, forward(): pl.pallas_call(forward_kernel, out_shape=(jax.ShapeDtypeStruct(block, f32...  5.87 us
    pallas_call x1, Pallas kernels, backward(): pl.pallas_call(backward_kernel, out_shape=jax.ShapeDtypeStruct((TILE_DEV...  5.78 us

profile of v7, /device:TPU:1, one launch (start us, length us, event | category | flops | bytes accessed | tf_op | source)
XLA Modules:
  0.0 95.5 jit_solution(17013908055894351919)
XLA Ops:
  0.0 0.0 copy-start
  0.0 0.8 copy-done
  0.8 0.0 copy-start.1
  0.8 0.8 copy-done.1
  1.7 0.0 copy-start.2
  1.7 0.8 copy-done.2
  2.5 0.0 copy-start.3
  2.5 0.8 copy-done.3
  3.3 0.0 copy-start.5
  3.3 0.8 copy-done.5
  4.1 0.0 copy-start.6
  4.1 0.8 copy-done.6
  4.8 0.0 copy-start.7
  4.8 0.7 copy-done.7
  5.5 0.0 copy-start.8
  5.5 0.7 copy-done.8
  6.2 0.0 copy-start.9
  6.2 0.7 copy-done.9
  6.8 0.0 copy-start.4
  6.8 26.7 %gather_all.1 = (bf16[8,2,3,128,128]{4,3,2,1,0:T(8,128)(2,1)S(1)}, f32[8,2,16,8,128]{4,3,2,1,0:T(8,128)S(1)}, bf16[8,2,16,8,128]{4,3,2,1,0:T(8,128)(2,1)S(1)}, s32[16,128]{1,0:T(8,128)S(1)}) custom-call(s32[128]{0:T(128)S(1)} %copy-done.8, s32[1,32]{1,0:T(1,128)S(1)} %bitcast.5, s32[8,16]{1,0:T(8,128)S(1)} %copy-done.7, s32[8,2048]{1,0:T(8,128)S(1)} %copy-done, ...), custom_call_target="tpu_custom_call" | custom-call | tf_op jit(solution)/shard_map/gather_all/pallas_call | solution.py:308
  33.6 5.9 %forward.1 = (f32[8,8,16,128]{3,2,1,0:T(8,128)S(1)}, f32[8,2,16,8,128]{4,3,2,1,0:T(8,128)S(1)}) custom-call(s32[16,128]{1,0:T(8,128)S(1)} %get-tuple-element.11.list_ref, bf16[16,384,128]{2,1,0:T(8,128)(2,1)S(1)} %bitcast.4, f32[8,2,16,8,128]{4,3,2,1,0:T(8,128)S(1)} %get-tuple-element.12.f_ref, bf16[8,2,16,8,128]{4,3,2,1,0:T(8,128)(2,1)S(1)} %get-tuple-element.13.w_ref), custom_call_target="tpu_custom_call" | custom-call | tf_op jit(solution)/shard_map/forward/pallas_call | solution.py:421
  39.4 0.0 copy-done.4
  39.4 26.1 %filter.1.filt_ref = f32[8,8,16,128]{3,2,1,0:T(8,128)S(1)} custom-call(f32[8,8,16,128]{3,2,1,0:T(8,128)S(1)} %get-tuple-element.16.part_ref, f32[8,1025]{1,0:T(8,128)S(1)} %copy-done.4), custom_call_target="tpu_custom_call" | custom-call | tf_op jit(solution)/shard_map/filter/pallas_call | solution.py:621
  65.6 5.8 %backward.1 = f32[16,384,128]{2,1,0:T(8,128)S(1)} custom-call(s32[16,128]{1,0:T(8,128)S(1)} %get-tuple-element.11.list_ref, f32[8,2,16,8,128]{4,3,2,1,0:T(8,128)S(1)} %get-tuple-element.12.f_ref, bf16[8,2,16,8,128]{4,3,2,1,0:T(8,128)(2,1)S(1)} %get-tuple-element.13.w_ref, f32[8,2,16,8,128]{4,3,2,1,0:T(8,128)S(1)} %get-tuple-element.15.cs_ref, ...), custom_call_target="tpu_custom_call" | custom-call | tf_op jit(solution)/shard_map/backward/pallas_call | solution.py:479
  71.4 23.4 %collect.1 = f32[2,3,32,128]{3,2,1,0:T(8,128)S(1)} custom-call(f32[8,2,3,2,2,32,128]{6,5,4,3,2,1,0:T(8,128)S(1)} %bitcast.3), custom_call_target="tpu_custom_call" | custom-call | tf_op jit(solution)/shard_map/collect/pallas_call | solution.py:761
  94.8 0.6 copy.12
Async XLA Ops:
  0.0 0.8 copy-start
  0.8 0.8 copy-start.1
  1.7 0.8 copy-start.2
  2.5 0.8 copy-start.3
  3.3 0.8 copy-start.5
  4.1 0.8 copy-start.6
  4.8 0.7 copy-start.7
  5.5 0.7 copy-start.8
  6.2 0.7 copy-start.9
  6.8 32.6 %copy-start.4 = (f32[8,1025]{1,0:T(8,128)S(1)}, f32[8,1025]{1,0:T(8,128)}, u32[]{:S(2)}) copy-start(f32[8,1025]{1,0:T(8,128)} %noise_ref.1) | copy-start | bytes 98404

commit v8 on v7

--- a/solution.py
+++ b/solution.py
@@ -14,6 +14,7 @@
 DET, RUNS, LANE = 8, 16, 128
 PIX = 128
 STRIP = 32
+N_STRIP = 4
 LISTED = 32
 TILE_DEV = 2
 REACH = 8
@@ -72,10 +73,10 @@
     def dot(left, right):
         return jnp.dot(left, right, preferred_element_type=f32)
 
-    lanes, offset = iota((RUNS, LANE), 1), iota((RUNS, LANE), 0)
+    lanes, offset = iota((LANE, LANE), 1), iota((LANE, LANE), 0)
     spot = jnp.zeros((DET, LANE), f32)
     for slot in range(NB):
-        spot += dot(pos_ref[slot].astype(f32).astype(bf), whole(lanes == offset + slot * RUNS))
+        spot += dot(pos_ref[slot].astype(bf), whole((offset < RUNS) & (lanes == offset + slot * RUNS)))
     pos = spot.astype(i32)
     here = (pos // (TILE_DEV * NX * NZ) == y) & ((pos // TILE_DEV) % NX == x)
     tile = ((pos // (TILE_DEV * NX)) % NZ) * TILE_DEV + pos % TILE_DEV
@@ -110,24 +111,42 @@
     order_ref[DET:, :] = jnp.broadcast_to(ALL_RUNS - others, (DET, LANE)).astype(i32)
 
 
-def pack(home_ref, piece_ref, slot_ref, row_ref, col_ref, low_ref, high_ref, angle_ref, f_own, w_own, p_own):
+def pack_kernel(
+    home_ref, piece_ref, slot_ref, row_ref, col_ref, low_ref, high_ref, angle_ref, q_ref, float_ref, half_ref
+):
     for r in range(RUNS):
         at = slice(r * LANE, (r + 1) * LANE)
-        f_own[0, r] = (row_ref[:, at] * PIX + col_ref[:, at]).astype(jnp.float32)
-        f_own[1, r] = angle_ref[:, at]
-        w_own[0, r] = low_ref[:, at]
-        w_own[1, r] = high_ref[:, at]
+        for part, value in enumerate(((row_ref[:, at] * PIX + col_ref[:, at]).astype(jnp.float32), angle_ref[:, at])):
+            float_ref[part * PIECE_RUNS + r * DET : part * PIECE_RUNS + (r + 1) * DET] = value
+        for part, source in enumerate((low_ref, high_ref)):
+            half_ref[part * PIECE_RUNS + r * DET : part * PIECE_RUNS + (r + 1) * DET] = source[:, at]
     slots = slot_ref[...]
-    position = jnp.zeros_like(slots)
+    position = jnp.zeros(slots.shape, jnp.float32)
     for s in range(LISTED):
-        position = jnp.where(slots == s, home_ref[piece_ref[0, s]], position)
-    p_own[...] = position
+        position = jnp.where(slots == s, home_ref[piece_ref[0, s]].astype(jnp.float32), position)
+    float_ref[2 * PIECE_RUNS :] = jnp.concatenate(
+        [position, jnp.zeros((DET, LANE - RUNS), jnp.float32)], axis=1
+    )
+    half_ref[2 * PIECE_RUNS :] = q_ref[...]
+
+
+def packed(tile_home, piece_list, run_slot, hit_row, hit_col, frac_row, frac_col, angle, quarter):
+    return pl.pallas_call(
+        pack_kernel,
+        out_shape=(
+            jax.ShapeDtypeStruct((2 * PIECE_RUNS + DET, LANE), jnp.float32),
+            jax.ShapeDtypeStruct((2 * PIECE_RUNS + quarter.shape[0], LANE), jnp.bfloat16),
+        ),
+        in_specs=[SM, SM] + [VM] * 7,
+        out_specs=(VM,) * 2,
+        name="pack",
+    )(tile_home, piece_list, run_slot, hit_row, hit_col, frac_row, frac_col, angle, quarter)
 
 
 def gather_kernel(
-    home_ref, piece_ref, slot_ref, row_ref, col_ref, low_ref, high_ref, angle_ref, q_ref,
+    float_ref, half_ref,
     tiles_ref, fo_ref, wo_ref, order_ref,
-    q_own, f_own, w_own, p_own, pos_all, load_sem, store_sem,
+    pos_all, store_sem,
     pos_send, pos_recv, block_send, block_recv, strip_send, strip_recv, core_send, core_recv, hi_send, hi_recv,
 ):
     det, tm, y, z, x = place()
@@ -141,24 +160,21 @@
     def along(direction, jump):
         return (det, tm_of(y, (z + jump) % NZ if direction == 0 else (z + NZ - jump) % NZ, x))
 
+    f_ref, p_ref = float_ref.at[pl.ds(0, 2 * PIECE_RUNS)], float_ref.at[pl.ds(2 * PIECE_RUNS, DET)]
+    w_ref = half_ref.at[pl.ds(0, 2 * PIECE_RUNS)]
+    q_ref = half_ref.at[pl.ds(2 * PIECE_RUNS, TILE_DEV * 3 * STRIP)]
+
     def strip(slot, d):
-        return tiles_ref.at[slot, :, :, pl.ds(d * STRIP, STRIP), :]
+        return tiles_ref.at[slot, d]
 
     def block(slot, part):
-        return fo_ref.at[slot, part] if part < 2 else wo_ref.at[slot]
+        return fo_ref.at[slot, pl.ds(part * PIECE_RUNS, PIECE_RUNS)] if part < 2 else wo_ref.at[slot]
 
     def own_block(part):
-        return f_own.at[part] if part < 2 else w_own
+        return float_ref.at[pl.ds(part * PIECE_RUNS, PIECE_RUNS)] if part < 2 else w_ref
 
     mine = y * NX + x
-    load = pltpu.make_async_copy(q_ref, q_own, load_sem)
-    load.start()
-    greeted = [along(d, j) for d in (0, 1) for j in (1, 2)] + [(partner, tm), (across, tm)] + far
-    barrier = pltpu.get_barrier_semaphore()
-    for peer in greeted:
-        pl.semaphore_signal(barrier, inc=1, device_id=peer, device_id_type=MESH)
-    pack(home_ref, piece_ref, slot_ref, row_ref, col_ref, low_ref, high_ref, angle_ref, f_own, w_own, p_own)
-    pl.semaphore_wait(barrier, len(greeted))
+    greet([along(d, j) for d in (0, 1) for j in (1, 2)] + [(partner, tm), (across, tm)] + far)
 
     started = []
 
@@ -167,8 +183,6 @@
         started.append(copy)
 
     start(remote(q_ref, strip(z, det), hi_send, hi_recv, (across, tm)))
-    for k, peer in enumerate(far):
-        start(remote(p_own, pos_all.at[mine], pos_send.at[k], pos_recv.at[k], peer))
 
     def send_block(link, slot, part, peer, own=False):
         start(
@@ -230,14 +244,15 @@
         to_partner(half, 0, z)
 
     first_strips(0)
+    for k, peer in enumerate(far):
+        start(remote(p_ref, pos_all.at[mine], pos_send.at[k], pos_recv.at[k], peer))
     for part in range(3):
         send_block(1, mine, part, up, True)
         send_block(2, mine, part, down, True)
         send_block(0, mine, part, side, True)
-    load.wait()
     stores = []
     for i, (src, dst) in enumerate(
-        ((q_own, strip(z, det)), (f_own, fo_ref.at[mine]), (w_own, wo_ref.at[mine]), (p_own, pos_all.at[mine]))
+        ((q_ref, strip(z, det)), (f_ref, fo_ref.at[mine]), (w_ref, wo_ref.at[mine]), (p_ref, pos_all.at[mine]))
     ):
         copy = pltpu.make_async_copy(src, dst, store_sem.at[i])
         copy.start()
@@ -278,7 +293,7 @@
 
     stores[3].wait()
     for k, peer in enumerate(far):
-        remote(p_own, pos_all.at[mine], pos_send.at[k], pos_recv.at[k], peer).wait_recv()
+        remote(p_ref, pos_all.at[mine], pos_send.at[k], pos_recv.at[k], peer).wait_recv()
     run_order(pos_all, order_ref, y, x)
 
     take_strip(1, 3)
@@ -302,26 +317,21 @@
         copy.wait_send()
 
 
-def gather_all(tile_home, piece_list, run_slot, hit_row, hit_col, frac_row, frac_col, angle, quarter):
+def gather_all(floats, halves):
     bf, f32, i32 = jnp.bfloat16, jnp.float32, jnp.int32
-    samples = (2, RUNS, DET, LANE)
+    samples = (2 * PIECE_RUNS, LANE)
     return pl.pallas_call(
         gather_kernel,
         out_shape=(
-            jax.ShapeDtypeStruct((NZ, TILE_DEV, 3, PIX, PIX), bf),
+            jax.ShapeDtypeStruct((NZ, N_STRIP, TILE_DEV * 3 * STRIP, PIX), bf),
             jax.ShapeDtypeStruct((NB, *samples), f32),
             jax.ShapeDtypeStruct((NB, *samples), bf),
             jax.ShapeDtypeStruct((2 * DET, LANE), i32),
         ),
-        in_specs=[SM, SM] + [VM] * 6 + [ANY],
+        in_specs=[ANY] * 2,
         out_specs=(ANY, ANY, ANY, VM),
         scratch_shapes=[
-            pltpu.VMEM(quarter.shape, bf),
-            pltpu.VMEM(samples, f32),
-            pltpu.VMEM(samples, bf),
-            pltpu.VMEM((DET, RUNS), i32),
-            pltpu.VMEM((NB, DET, RUNS), i32),
-            DMA,
+            pltpu.VMEM((NB, DET, LANE), f32),
             DMA((4,)),
             DMA((NB,)),
             DMA((NB,)),
@@ -336,7 +346,7 @@
         ],
         compiler_params=pltpu.CompilerParams(collective_id=0, has_side_effects=True, vmem_limit_bytes=GRANT),
         name="gather_all",
-    )(tile_home, piece_list, run_slot, hit_row, hit_col, frac_row, frac_col, angle, quarter)
+    )(floats, halves)
 
 
 def sin_cos(v):
@@ -378,15 +388,15 @@
 
 def forward_kernel(list_ref, tiles_ref, f_ref, w_ref, sig_ref, cs_ref, hit_ref, frac_ref):
     def prepare(z, _):
-        code = f_ref[z, 0]
+        code = f_ref[z, :PIECE_RUNS].reshape(RUNS, DET, LANE)
         row = jnp.floor(code * (1.0 / PIX))
         hit_ref[z, 0] = row
         hit_ref[z, 1] = code - row * PIX
-        sin, cos = sin_cos(2.0 * f_ref[z, 1])
+        sin, cos = sin_cos(2.0 * f_ref[z, PIECE_RUNS:].reshape(RUNS, DET, LANE))
         cs_ref[z, 0] = cos
         cs_ref[z, 1] = sin
-        frac_ref[z, 0] = w_ref[z, 0].astype(jnp.float32)
-        frac_ref[z, 1] = w_ref[z, 1].astype(jnp.float32)
+        fracs = w_ref[z].astype(jnp.float32)
+        frac_ref[z] = fracs.reshape(2, RUNS, DET, LANE)
         sig_ref[z] = jnp.zeros_like(sig_ref[z])
         return 0
 
@@ -396,19 +406,24 @@
 
     def body(step, _):
         for u in range(UNROLL):
-            k = step * UNROLL + u
-            tile, z, d, r = run_of(list_ref[k >> 7, k & (LANE - 1)])
+            n = step * UNROLL + u
+            tile, z, d, r = run_of(list_ref[n >> 7, n & (LANE - 1)])
             at = (r, pl.ds(d, 1), slice(None))
             col_high = frac_ref[z, 1, *at]
             row_high = frac_ref[z, 0, *at]
             col_weight = spread(hit_ref[z, 1, *at], low_of(col_high), col_high, rows)
             row_weight = spread(hit_ref[z, 0, *at], low_of(row_high), row_high, rows).astype(jnp.float32)
-            partial = jnp.dot(tiles_ref[tile], col_weight, preferred_element_type=jnp.float32)
-            value = [
-                jnp.sum(partial[p * PIX : (p + 1) * PIX] * row_weight, axis=0, keepdims=True) for p in range(3)
-            ]
+            rows_of_tile = jnp.concatenate([tiles_ref[tile // TILE_DEV, k, tile % TILE_DEV] for k in range(N_STRIP)], axis=0)
+            partial = jnp.dot(rows_of_tile, col_weight, preferred_element_type=jnp.float32)
+            value = []
+            for p in range(3):
+                terms = [
+                    partial[(k * 3 + p) * STRIP : (k * 3 + p + 1) * STRIP] * row_weight[k * STRIP : (k + 1) * STRIP]
+                    for k in range(N_STRIP)
+                ]
+                value.append(jnp.sum(sum(terms[1:], terms[0]), axis=0, keepdims=True))
             total = value[0] + cs_ref[z, 0, *at] * value[1] + cs_ref[z, 1, *at] * value[2]
-            sig_ref[z, d, pl.ds(r, 1), :] = jnp.where(k < count, total, 0.0)
+            sig_ref[z, d, pl.ds(r, 1), :] = jnp.where(n < count, total, 0.0)
         return 0
 
     lax.fori_loop(0, (count + UNROLL - 1) // UNROLL, body, 0)
@@ -431,12 +446,12 @@
 
 def backward_kernel(list_ref, f_ref, w_ref, cs_ref, filt_ref, acc_ref, hit_ref, frac_ref):
     def prepare(z, _):
-        code = f_ref[z, 0]
+        code = f_ref[z, :PIECE_RUNS].reshape(RUNS, DET, LANE)
         row = jnp.floor(code * (1.0 / PIX))
         hit_ref[z, 0] = row
         hit_ref[z, 1] = code - row * PIX
-        frac_ref[z, 0] = w_ref[z, 0].astype(jnp.float32)
-        frac_ref[z, 1] = w_ref[z, 1].astype(jnp.float32)
+        fracs = w_ref[z].astype(jnp.float32)
+        frac_ref[z] = fracs.reshape(2, RUNS, DET, LANE)
         return 0
 
     lax.fori_loop(0, NB, prepare, 0)
@@ -524,7 +539,7 @@
 
 def filter_kernel(
     part_ref, noise_ref, out_ref, land, ext, filt, lags, t_hi, t_lo,
-    own_sem, store_sem, send, recv, halo_send, halo_recv, back_send, back_recv,
+    store_sem, send, recv, halo_send, halo_recv, back_send, back_recv,
 ):
     det, tm, y, z, x = place()
     total_tm = NY * NZ * NX
@@ -537,16 +552,13 @@
 
     peers = [(det, tm_of((y + dy) % NY, z, (x + dx) % NX)) for dy, dx in PEERS]
     greet(peers + [(det, later), (det, prior)])
-    own = pltpu.make_async_copy(part_ref.at[mine], land.at[NB - 1], own_sem)
-    own.start()
     sends = []
     for k, peer in enumerate(peers):
         copy = remote(part_ref.at[slot(k, 1)], land.at[k], send.at[k], recv.at[k], peer)
         copy.start()
         sends.append(copy)
     toeplitz(noise_ref, lags, t_hi, t_lo)
-    own.wait()
-    total = land[NB - 1]
+    total = part_ref[mine]
     for k in range(NB - 1):
         sends[k].wait_recv()
         total = total + land[k]
@@ -583,28 +595,34 @@
         copy.start()
         own_copies.append(copy)
 
-    for d in range(DET):
-        line_all = jnp.concatenate(
-            [
-                jnp.where(first, 0.0, ext[d, :REACH]),
-                ext[d, REACH : REACH + RUNS],
-                jnp.where(last, 0.0, ext[d, REACH + RUNS :]),
-            ],
-            axis=0,
-        )
-        result = jnp.zeros((RUNS, LANE), jnp.float32)
+    for c in range(DET // SENT):
+        dets = range(c * SENT, (c + 1) * SENT)
+        lines = [
+            jnp.concatenate(
+                [
+                    jnp.where(first, 0.0, ext[d, :REACH]),
+                    ext[d, REACH : REACH + RUNS],
+                    jnp.where(last, 0.0, ext[d, REACH + RUNS :]),
+                ],
+                axis=0,
+            )
+            for d in dets
+        ]
+        full = [jnp.zeros((2 * RUNS, LANE), jnp.float32) for d in dets]
+        fine = [jnp.zeros((RUNS, LANE), jnp.float32) for d in dets]
         for m in range(2 * REACH + 1):
-            window = line_all[m : m + RUNS]
-            high = window.astype(jnp.bfloat16)
-            low = (window - high.astype(jnp.float32)).astype(jnp.bfloat16)
-            stack = jnp.concatenate([high, low], axis=0)
             q = REACH - m
-            for index, crossed in [(q, False)] if q > 0 else [(-q, True)] if q < 0 else [(0, False), (REACH + 1, True)]:
-                both = product(stack, t_hi[d, index], crossed)
-                result += both[:RUNS] + both[RUNS:] + product(high, t_lo[d, index], crossed)
-        filt[d] = result
-        if d % SENT == SENT - 1:
-            send_back(d // SENT)
+            for i, d in enumerate(dets):
+                window = lines[i][m : m + RUNS]
+                high = window.astype(jnp.bfloat16)
+                low = (window - high.astype(jnp.float32)).astype(jnp.bfloat16)
+                stack = jnp.concatenate([high, low], axis=0)
+                for index, crossed in [(q, False)] if q > 0 else [(-q, True)] if q < 0 else [(0, False), (REACH + 1, True)]:
+                    full[i] += product(stack, t_hi[d, index], crossed)
+                    fine[i] += product(high, t_lo[d, index], crossed)
+        for i, d in enumerate(dets):
+            filt[d] = full[i][:RUNS] + full[i][RUNS:] + fine[i]
+        send_back(c)
     for copy in own_copies:
         copy.wait()
     for c in range(DET // SENT):
@@ -621,16 +639,15 @@
     return pl.pallas_call(
         filter_kernel,
         out_shape=jax.ShapeDtypeStruct((NB, *block), f32),
-        in_specs=[ANY, VM],
+        in_specs=[VM, VM],
         out_specs=ANY,
         scratch_shapes=[
-            pltpu.VMEM((NB, *block), f32),
+            pltpu.VMEM((NB - 1, *block), f32),
             pltpu.VMEM((DET, RUNS + 2 * REACH, LANE), f32),
             pltpu.VMEM(block, f32),
             pltpu.VMEM((REACH + 1, DET, LANE), f32),
             pltpu.VMEM(matrices, bf),
             pltpu.VMEM(matrices, bf),
-            DMA,
             DMA((DET // SENT,)),
             DMA((NB,)),
             DMA((NB,)),
@@ -651,8 +668,8 @@
 
 
 def collect_kernel(
-    acc_ref, out_ref, own, land_core, packet, land, land_last, land_own,
-    own_sem, core_send, core_recv, ring_send, ring_recv, last_send, last_recv, hi_send, hi_recv,
+    acc_ref, out_ref, land_core, packet, land, land_last, land_own,
+    core_send, core_recv, ring_send, ring_recv, last_send, last_recv, hi_send, hi_recv,
 ):
     f32 = jnp.float32
     det, tm, y, z, x = place()
@@ -660,11 +677,6 @@
     partner, across = core_of(det), hi_of(det)
     right, left = tm_of(y, (z + 1) % NZ, x), tm_of(y, (z + NZ - 1) % NZ, x)
     neighbours = ((det, right), (det, left))
-    loads = []
-    for k, offset in enumerate(OFFSETS):
-        copy = pltpu.make_async_copy(acc_ref.at[(z + offset + NZ) % NZ, :, :, :, core], own.at[k], own_sem.at[k])
-        copy.start()
-        loads.append(copy)
     greet([(partner, tm), (across, tm), *neighbours, (across, right), (across, left)])
     started = []
 
@@ -702,15 +714,17 @@
     def own_copy(t):
         return remote(packet.at[len(OFFSETS) - 1, t, :, 1 - hi], land_own.at[t], hi_send.at[t], hi_recv.at[t], (across, tm))
 
+    def own(k, t, p):
+        return acc_ref[(z + OFFSETS[k] + NZ) % NZ, t, p, :, core]
+
     def swapped(k):
-        loads[k].wait()
         remote(acc_ref.at[0, :, :, :, 0], land_core.at[k], core_send.at[k], core_recv.at[k], (partner, tm)).wait_recv()
 
     swapped(0)
     for direction in (0, 1):
         for c, (t, p) in enumerate(CHUNKS):
             if t == direction:
-                packet[0, t, p] = (own[0, t, p] + land_core[0, t, p]).astype(WIRE)
+                packet[0, t, p] = (own(0, t, p) + land_core[0, t, p]).astype(WIRE)
     for p in range(3):
         for direction in (0, 1):
             start(ring(direction, 0, direction * 3 + p))
@@ -724,7 +738,7 @@
                 c = (i + 3 * (1 - direction)) % len(CHUNKS) if step == 1 else i
                 t, p = CHUNKS[c]
                 k = keys[direction]
-                value = own[k, t, p] + land_core[k, t, p]
+                value = own(k, t, p) + land_core[k, t, p]
                 if step > 1 or t == direction:
                     ring(direction, step - 1, c).wait_recv()
                     value = value + land[direction, step - 1, t, p].astype(f32)
@@ -737,14 +751,15 @@
         if step == 1:
             swapped(last)
             for t in range(TILE_DEV):
-                value = own[last, t] + land_core[last, t]
-                packet[last, t] = value.astype(WIRE)
+                for p in range(3):
+                    value = own(last, t, p) + land_core[last, t, p]
+                    packet[last, t, p] = value.astype(WIRE)
+                    land_core[last, t, p] = value
                 start(own_copy(t))
-                own[last, t] = value
     for t in range(TILE_DEV):
         own_copy(t).wait_recv()
     for c, (t, p) in enumerate(CHUNKS):
-        value = own[last, t, p, hi] + land_own[t, p].astype(f32)
+        value = land_core[last, t, p, hi] + land_own[t, p].astype(f32)
         for crossing in (0, 1):
             for direction in (0, 1):
                 last_hop(direction, c, crossing).wait_recv()
@@ -761,16 +776,14 @@
     return pl.pallas_call(
         collect_kernel,
         out_shape=jax.ShapeDtypeStruct(quarter, f32),
-        in_specs=[ANY],
+        in_specs=[VM],
         out_specs=VM,
         scratch_shapes=[
-            pltpu.VMEM((NZ, *half), f32),
             pltpu.VMEM((NZ, *half), f32),
             pltpu.VMEM((NZ, *half), WIRE),
             pltpu.VMEM((2, HALF_Z - 1, *half), WIRE),
             pltpu.VMEM((2, 2, *quarter), WIRE),
             pltpu.VMEM(quarter, WIRE),
-            DMA((NZ,)),
             DMA((NZ,)),
             DMA((NZ,)),
             DMA((2, HALF_Z - 1, 6)),
@@ -788,10 +801,14 @@
 def body(
     sky_map, tile_home, piece_tiles, run_slot, hit_row, hit_col, frac_row, frac_col, angle, noise_coef
 ):
-    tiles, all_floats, all_fracs, order = gather_all(
-        tile_home, piece_tiles.reshape(1, LISTED), run_slot, hit_row, hit_col, frac_row, frac_col, angle, sky_map
+    floats, halves = packed(
+        tile_home, piece_tiles.reshape(1, LISTED), run_slot, hit_row, hit_col, frac_row, frac_col, angle,
+        sky_map.reshape(TILE_DEV * 3 * STRIP, PIX),
     )
-    partial, turns = forward(order, tiles.reshape(TILE_DEV * NZ, 3 * PIX, PIX), all_floats, all_fracs)
+    tiles, all_floats, all_fracs, order = gather_all(floats, halves)
+    partial, turns = forward(
+        order, tiles.reshape(NZ, N_STRIP, TILE_DEV, 3 * STRIP, PIX), all_floats, all_fracs
+    )
     filtered = filtered_of(partial, noise_coef)
     acc = backward(order, all_floats, all_fracs, turns, filtered)
     return collect(acc)

time: 96.2 us -> 90 us (0.936)
  local copies, waits for them, and re-layouts: 7.47 us -> 2.45 us
    unnamed x21 -> x7, local copies, waits for them, and re-layouts: 7.47 us -> 2.45 us
    pallas_call x1, Pallas kernels: 26.1 us -> 23.5 us  [filtered_of(): pl.pallas_call(filter_kernel, out_shape=jax.ShapeDtypeStruct((NB, *block)...]
    pallas_call x1, Pallas kernels: 23.4 us -> 21 us  [collect(): pl.pallas_call(collect_kernel, out_shape=jax.ShapeDtypeStruct(quarter, f3...]
    pallas_call x1, Pallas kernels: 5.78 us -> 7.8 us  [backward(): pl.pallas_call(backward_kernel, out_shape=jax.ShapeDtypeStruct((TILE_DEV...]
    pallas_call x1, Pallas kernels: 5.87 us -> 7.6 us  [forward(): pl.pallas_call(forward_kernel, out_shape=(jax.ShapeDtypeStruct(block, f32...]
    pallas_call x1 -> x2, Pallas kernels: 26.7 us -> 27.6 us  [the longest x1 26 us: gather_all(): pl.pallas_call(gather_kernel, out_shape=(jax.ShapeDtypeStruct((NZ, N_STRI...]
where the time goes in v8:
time: 90 us
  Pallas kernels  87.5 us (97%)
  local copies, waits for them, and re-layouts  2.45 us (3%)
    pallas_call x1, Pallas kernels, gather_all(): pl.pallas_call(gather_kernel, out_shape=(jax.ShapeDtypeStruct((NZ, N_STRI...  26 us
    pallas_call x1, Pallas kernels, filtered_of(): pl.pallas_call(filter_kernel, out_shape=jax.ShapeDtypeStruct((NB, *block)...  23.5 us
    pallas_call x1, Pallas kernels, collect(): pl.pallas_call(collect_kernel, out_shape=jax.ShapeDtypeStruct(quarter, f3...  21 us
    pallas_call x1, Pallas kernels, backward(): pl.pallas_call(backward_kernel, out_shape=jax.ShapeDtypeStruct((TILE_DEV...  7.8 us
    pallas_call x1, Pallas kernels, forward(): pl.pallas_call(forward_kernel, out_shape=(jax.ShapeDtypeStruct(block, f32...  7.6 us
    unnamed x7, local copies, waits for them, and re-layouts  2.45 us

profile of v8, /device:TPU:1, one launch (start us, length us, event | category | flops | bytes accessed | tf_op | source)
XLA Modules:
  0.0 90.0 jit_solution(7760430053816437222)
XLA Ops:
  0.0 0.0 copy-start.2
  0.0 1.7 %pack.1 = (f32[264,128]{1,0:T(8,128)}, bf16[448,128]{1,0:T(8,128)(2,1)}) custom-call(s32[128]{0:T(128)} %home_ref.1, s32[1,32]{1,0:T(1,128)} %bitcast.7, s32[8,16]{1,0:T(8,128)} %slot_ref.1, s32[8,2048]{1,0:T(8,128)} %row_ref.1, s32[8,2048]{1,0:T(8,128)} %col_ref.1, bf16[8,2048]{1,0:T(8,128)(2,1)} %low_ref.1, bf16[8,2048]{1,0:T(8,128)(2,1)} %high_ref.1, ...), custom_call_target="tpu_custom_call" | custom-call | tf_op jit(solution)/shard_map/pack/pallas_call | solution.py:134
  1.7 0.0 copy-start
  1.7 0.9 %copy-done = f32[264,128]{1,0:T(8,128)S(1)} copy-done((f32[264,128]{1,0:T(8,128)S(1)}, f32[264,128]{1,0:T(8,128)}, u32[]{:S(2)}) %copy-start) | copy-done | bytes 135192
  2.6 0.0 copy-start.1
  2.6 0.9 copy-done.1
  3.5 26.0 %gather_all.1 = (bf16[8,4,192,128]{3,2,1,0:T(8,128)(2,1)S(1)}, f32[8,256,128]{2,1,0:T(8,128)S(1)}, bf16[8,256,128]{2,1,0:T(8,128)(2,1)S(1)}, s32[16,128]{1,0:T(8,128)S(1)}) custom-call(f32[264,128]{1,0:T(8,128)S(1)} %copy-done, bf16[448,128]{1,0:T(8,128)(2,1)S(1)} %copy-done.1), custom_call_target="tpu_custom_call" | custom-call | tf_op jit(solution)/shard_map/gather_all/pallas_call | solution.py:323
  29.5 7.6 %forward.1 = (f32[8,8,16,128]{3,2,1,0:T(8,128)S(1)}, f32[8,2,16,8,128]{4,3,2,1,0:T(8,128)S(1)}) custom-call(s32[16,128]{1,0:T(8,128)S(1)} %get-tuple-element.15.list_ref, bf16[8,4,2,96,128]{4,3,2,1,0:T(8,128)(2,1)S(1)} %bitcast.5, f32[8,256,128]{2,1,0:T(8,128)S(1)} %get-tuple-element.16.f_ref, bf16[8,256,128]{2,1,0:T(8,128)(2,1)S(1)} %get-tuple-element.17.w_ref), custom_call_target="tpu_custom_call" | custom-call | tf_op jit(solution)/shard_map/forward/pallas_call | solution.py:436
  37.1 0.0 copy-done.2
  37.1 23.5 %filter.1.filt_ref = f32[8,8,16,128]{3,2,1,0:T(8,128)S(1)} custom-call(f32[8,8,16,128]{3,2,1,0:T(8,128)S(1)} %get-tuple-element.20.part_ref, f32[8,1025]{1,0:T(8,128)S(1)} %copy-done.2), custom_call_target="tpu_custom_call" | custom-call | tf_op jit(solution)/shard_map/filter/pallas_call | solution.py:639
  60.6 7.8 %backward.1 = f32[16,384,128]{2,1,0:T(8,128)S(1)} custom-call(s32[16,128]{1,0:T(8,128)S(1)} %get-tuple-element.15.list_ref, f32[8,256,128]{2,1,0:T(8,128)S(1)} %get-tuple-element.16.f_ref, bf16[8,256,128]{2,1,0:T(8,128)(2,1)S(1)} %get-tuple-element.17.w_ref, f32[8,2,16,8,128]{4,3,2,1,0:T(8,128)S(1)} %get-tuple-element.19.cs_ref, ...), custom_call_target="tpu_custom_call" | custom-call | tf_op jit(solution)/shard_map/backward/pallas_call | solution.py:494
  68.4 21.0 %collect.1 = f32[2,3,32,128]{3,2,1,0:T(8,128)S(1)} custom-call(f32[8,2,3,2,2,32,128]{6,5,4,3,2,1,0:T(8,128)S(1)} %bitcast.4), custom_call_target="tpu_custom_call" | custom-call | tf_op jit(solution)/shard_map/collect/pallas_call | solution.py:776
  89.3 0.6 copy.12
Async XLA Ops:
  0.0 37.1 %copy-start.2 = (f32[8,1025]{1,0:T(8,128)S(1)}, f32[8,1025]{1,0:T(8,128)}, u32[]{:S(2)}) copy-start(f32[8,1025]{1,0:T(8,128)} %noise_ref.1) | copy-start | bytes 98404
  1.7 0.9 %copy-start = (f32[264,128]{1,0:T(8,128)S(1)}, f32[264,128]{1,0:T(8,128)}, u32[]{:S(2)}) copy-start(f32[264,128]{1,0:T(8,128)} %get-tuple-element.13.float_ref) | copy-start | bytes 405508
  2.6 0.9 copy-start.1

commit v9 on v8

--- a/solution.py
+++ b/solution.py
@@ -268,8 +268,11 @@
                 send_block(5, slot_of[1], part, up)
             if link == 2 and part == 1:
                 send_block(5, slot_of[2], part, down)
+            if link == 1 and part == 2:
+                send_block(3, slot_of[1], part, side)
             if link == 0:
-                send_block(3, slot_of[0], part, up)
+                if part != 2:
+                    send_block(3, slot_of[0], part, up)
                 send_block(4, slot_of[0], part, down)
 
     def opposite(part):
@@ -553,27 +556,42 @@
     peers = [(det, tm_of((y + dy) % NY, z, (x + dx) % NX)) for dy, dx in PEERS]
     greet(peers + [(det, later), (det, prior)])
     sends = []
-    for k, peer in enumerate(peers):
-        copy = remote(part_ref.at[slot(k, 1)], land.at[k], send.at[k], recv.at[k], peer)
-        copy.start()
-        sends.append(copy)
+
+    def part_copy(c, k):
+        rows = pl.ds(c * SENT, SENT)
+        return remote(part_ref.at[slot(k, 1), rows], land.at[k, rows], send.at[k, c], recv.at[k, c], peers[k])
+
+    def halo_copies(c):
+        rows = pl.ds(c * SENT, SENT)
+        return (
+            remote(
+                ext.at[rows, pl.ds(REACH, REACH), :], ext.at[rows, pl.ds(REACH + RUNS, REACH), :],
+                halo_send.at[0, c], halo_recv.at[0, c], (det, prior),
+            ),
+            remote(
+                ext.at[rows, pl.ds(RUNS, REACH), :], ext.at[rows, pl.ds(0, REACH), :],
+                halo_send.at[1, c], halo_recv.at[1, c], (det, later),
+            ),
+        )
+
+    for c in range(DET // SENT):
+        for k in range(NB - 1):
+            copy = part_copy(c, k)
+            copy.start()
+            sends.append(copy)
     toeplitz(noise_ref, lags, t_hi, t_lo)
-    total = part_ref[mine]
-    for k in range(NB - 1):
-        sends[k].wait_recv()
-        total = total + land[k]
-    ext[:, REACH : REACH + RUNS, :] = total
-    to_prior = remote(
-        ext.at[:, pl.ds(REACH, REACH), :], ext.at[:, pl.ds(REACH + RUNS, REACH), :],
-        halo_send.at[0], halo_recv.at[0], (det, prior),
-    )
-    to_later = remote(
-        ext.at[:, pl.ds(RUNS, REACH), :], ext.at[:, pl.ds(0, REACH), :], halo_send.at[1], halo_recv.at[1], (det, later)
-    )
-    to_prior.start()
-    to_later.start()
-    to_prior.wait_recv()
-    to_later.wait_recv()
+
+    def gathered(c):
+        rows = slice(c * SENT, (c + 1) * SENT)
+        total = part_ref[mine, rows]
+        for k in range(NB - 1):
+            part_copy(c, k).wait_recv()
+            total = total + land[k, rows]
+        ext[rows, REACH : REACH + RUNS, :] = total
+        for copy in halo_copies(c):
+            copy.start()
+            sends.append(copy)
+
     first, last = tm == 0, tm == total_tm - 1
 
     def product(left, right, crossed):
@@ -595,7 +613,9 @@
         copy.start()
         own_copies.append(copy)
 
-    for c in range(DET // SENT):
+    def filtered(c):
+        for copy in halo_copies(c):
+            copy.wait_recv()
         dets = range(c * SENT, (c + 1) * SENT)
         lines = [
             jnp.concatenate(
@@ -623,12 +643,20 @@
         for i, d in enumerate(dets):
             filt[d] = full[i][:RUNS] + full[i][RUNS:] + fine[i]
         send_back(c)
+
+    chunks = DET // SENT
+    gathered(0)
+    gathered(1)
+    for c in range(chunks):
+        filtered(c)
+        if c + 2 < chunks:
+            gathered(c + 2)
     for copy in own_copies:
         copy.wait()
     for c in range(DET // SENT):
         for k, peer in enumerate(peers):
             back_copy(c, k, slot(k, -1)).wait_recv()
-    for copy in sends + back + [to_prior, to_later]:
+    for copy in sends + back:
         copy.wait_send()
 
 
@@ -649,10 +677,10 @@
             pltpu.VMEM(matrices, bf),
             pltpu.VMEM(matrices, bf),
             DMA((DET // SENT,)),
-            DMA((NB,)),
-            DMA((NB,)),
-            DMA((2,)),
-            DMA((2,)),
+            DMA((NB, DET // SENT)),
+            DMA((NB, DET // SENT)),
+            DMA((2, DET // SENT)),
+            DMA((2, DET // SENT)),
             DMA((NB, DET // SENT)),
             DMA((NB, DET // SENT)),
         ],

time: 90 us -> 91.2 us (1.013); the launches traced: 90 us -> 90 us
    pallas_call x1, Pallas kernels: 23.5 us -> 21.9 us  [filtered_of(): pl.pallas_call(filter_kernel, out_shape=jax.ShapeDtypeStruct((NB, *block)...]
where the time goes in v9:
time: 91.2 us; the launch traced here: 90 us
  Pallas kernels  87.5 us (96%)
  local copies, waits for them, and re-layouts  2.45 us (3%)
    pallas_call x1, Pallas kernels, gather_all(): pl.pallas_call(gather_kernel, out_shape=(jax.ShapeDtypeStruct((NZ, N_STRI...  26 us
    pallas_call x1, Pallas kernels, filtered_of(): pl.pallas_call(filter_kernel, out_shape=jax.ShapeDtypeStruct((NB, *block)...  21.9 us
    pallas_call x1, Pallas kernels, collect(): pl.pallas_call(collect_kernel, out_shape=jax.ShapeDtypeStruct(quarter, f3...  21.3 us
    pallas_call x1, Pallas kernels, backward(): pl.pallas_call(backward_kernel, out_shape=jax.ShapeDtypeStruct((TILE_DEV...  8.45 us
    pallas_call x1, Pallas kernels, forward(): pl.pallas_call(forward_kernel, out_shape=(jax.ShapeDtypeStruct(block, f32...  8.25 us
    unnamed x7, local copies, waits for them, and re-layouts  2.45 us

profile of v9, /device:TPU:1, one launch (start us, length us, event | category | flops | bytes accessed | tf_op | source)
XLA Modules:
  0.0 90.0 jit_solution(1143300755108697140)
XLA Ops:
  0.0 0.0 copy-start.2
  0.0 1.7 %pack.1 = (f32[264,128]{1,0:T(8,128)}, bf16[448,128]{1,0:T(8,128)(2,1)}) custom-call(s32[128]{0:T(128)} %home_ref.1, s32[1,32]{1,0:T(1,128)} %bitcast.7, s32[8,16]{1,0:T(8,128)} %slot_ref.1, s32[8,2048]{1,0:T(8,128)} %row_ref.1, s32[8,2048]{1,0:T(8,128)} %col_ref.1, bf16[8,2048]{1,0:T(8,128)(2,1)} %low_ref.1, bf16[8,2048]{1,0:T(8,128)(2,1)} %high_ref.1, ...), custom_call_target="tpu_custom_call" | custom-call | tf_op jit(solution)/shard_map/pack/pallas_call | solution.py:134
  1.7 0.0 copy-start
  1.7 0.9 %copy-done = f32[264,128]{1,0:T(8,128)S(1)} copy-done((f32[264,128]{1,0:T(8,128)S(1)}, f32[264,128]{1,0:T(8,128)}, u32[]{:S(2)}) %copy-start) | copy-done | bytes 135192
  2.6 0.0 copy-start.1
  2.6 0.9 copy-done.1
  3.5 26.0 %gather_all.1 = (bf16[8,4,192,128]{3,2,1,0:T(8,128)(2,1)S(1)}, f32[8,256,128]{2,1,0:T(8,128)S(1)}, bf16[8,256,128]{2,1,0:T(8,128)(2,1)S(1)}, s32[16,128]{1,0:T(8,128)S(1)}) custom-call(f32[264,128]{1,0:T(8,128)S(1)} %copy-done, bf16[448,128]{1,0:T(8,128)(2,1)S(1)} %copy-done.1), custom_call_target="tpu_custom_call" | custom-call | tf_op jit(solution)/shard_map/gather_all/pallas_call | solution.py:326
  29.5 8.3 %forward.1 = (f32[8,8,16,128]{3,2,1,0:T(8,128)S(1)}, f32[8,2,16,8,128]{4,3,2,1,0:T(8,128)S(1)}) custom-call(s32[16,128]{1,0:T(8,128)S(1)} %get-tuple-element.15.list_ref, bf16[8,4,2,96,128]{4,3,2,1,0:T(8,128)(2,1)S(1)} %bitcast.5, f32[8,256,128]{2,1,0:T(8,128)S(1)} %get-tuple-element.16.f_ref, bf16[8,256,128]{2,1,0:T(8,128)(2,1)S(1)} %get-tuple-element.17.w_ref), custom_call_target="tpu_custom_call" | custom-call | tf_op jit(solution)/shard_map/forward/pallas_call | solution.py:439
  37.7 0.0 copy-done.2
  37.7 21.9 %filter.1.filt_ref = f32[8,8,16,128]{3,2,1,0:T(8,128)S(1)} custom-call(f32[8,8,16,128]{3,2,1,0:T(8,128)S(1)} %get-tuple-element.20.part_ref, f32[8,1025]{1,0:T(8,128)S(1)} %copy-done.2), custom_call_target="tpu_custom_call" | custom-call | tf_op jit(solution)/shard_map/filter/pallas_call | solution.py:667
  59.7 8.5 %backward.1 = f32[16,384,128]{2,1,0:T(8,128)S(1)} custom-call(s32[16,128]{1,0:T(8,128)S(1)} %get-tuple-element.15.list_ref, f32[8,256,128]{2,1,0:T(8,128)S(1)} %get-tuple-element.16.f_ref, bf16[8,256,128]{2,1,0:T(8,128)(2,1)S(1)} %get-tuple-element.17.w_ref, f32[8,2,16,8,128]{4,3,2,1,0:T(8,128)S(1)} %get-tuple-element.19.cs_ref, ...), custom_call_target="tpu_custom_call" | custom-call | tf_op jit(solution)/shard_map/backward/pallas_call | solution.py:497
  68.1 21.3 %collect.1 = f32[2,3,32,128]{3,2,1,0:T(8,128)S(1)} custom-call(f32[8,2,3,2,2,32,128]{6,5,4,3,2,1,0:T(8,128)S(1)} %bitcast.4), custom_call_target="tpu_custom_call" | custom-call | tf_op jit(solution)/shard_map/collect/pallas_call | solution.py:804
  89.4 0.6 copy.12
Async XLA Ops:
  0.0 37.7 %copy-start.2 = (f32[8,1025]{1,0:T(8,128)S(1)}, f32[8,1025]{1,0:T(8,128)}, u32[]{:S(2)}) copy-start(f32[8,1025]{1,0:T(8,128)} %noise_ref.1) | copy-start | bytes 98404
  1.7 0.9 %copy-start = (f32[264,128]{1,0:T(8,128)S(1)}, f32[264,128]{1,0:T(8,128)}, u32[]{:S(2)}) copy-start(f32[264,128]{1,0:T(8,128)} %get-tuple-element.13.float_ref) | copy-start | bytes 405508
  2.6 0.9 copy-start.1

commit v10 on v9

--- a/solution.py
+++ b/solution.py
@@ -23,6 +23,7 @@
 SENT = 2
 PIECE_RUNS = DET * RUNS
 ALL_RUNS = NB * PIECE_RUNS
+SAMPLE_ROWS = 6 * PIECE_RUNS
 ANY = pl.BlockSpec(memory_space=pl.ANY)
 VM = pl.BlockSpec(memory_space=pltpu.VMEM)
 SM = pl.BlockSpec(memory_space=pltpu.SMEM)
@@ -74,10 +75,10 @@
         return jnp.dot(left, right, preferred_element_type=f32)
 
     lanes, offset = iota((LANE, LANE), 1), iota((LANE, LANE), 0)
-    spot = jnp.zeros((DET, LANE), f32)
+    spot = jnp.zeros((2 * DET, LANE), f32)
     for slot in range(NB):
-        spot += dot(pos_ref[slot].astype(bf), whole((offset < RUNS) & (lanes == offset + slot * RUNS)))
-    pos = spot.astype(i32)
+        spot += dot(pos_ref[slot], whole((offset < RUNS) & (lanes == offset + slot * RUNS)))
+    pos = spot[:DET].astype(i32)
     here = (pos // (TILE_DEV * NX * NZ) == y) & ((pos // TILE_DEV) % NX == x)
     tile = ((pos // (TILE_DEV * NX)) % NZ) * TILE_DEV + pos % TILE_DEV
     kinds, square = (2 * TILE_DEV * NZ, LANE), (LANE, LANE)
@@ -111,41 +112,38 @@
     order_ref[DET:, :] = jnp.broadcast_to(ALL_RUNS - others, (DET, LANE)).astype(i32)
 
 
-def pack_kernel(
-    home_ref, piece_ref, slot_ref, row_ref, col_ref, low_ref, high_ref, angle_ref, q_ref, float_ref, half_ref
-):
+def pack_kernel(home_ref, piece_ref, slot_ref, row_ref, col_ref, low_ref, high_ref, angle_ref, q_ref, out_ref):
+    f32, bf = jnp.float32, jnp.bfloat16
     for r in range(RUNS):
         at = slice(r * LANE, (r + 1) * LANE)
-        for part, value in enumerate(((row_ref[:, at] * PIX + col_ref[:, at]).astype(jnp.float32), angle_ref[:, at])):
-            float_ref[part * PIECE_RUNS + r * DET : part * PIECE_RUNS + (r + 1) * DET] = value
-        for part, source in enumerate((low_ref, high_ref)):
-            half_ref[part * PIECE_RUNS + r * DET : part * PIECE_RUNS + (r + 1) * DET] = source[:, at]
+        angle = angle_ref[:, at]
+        coarse = angle.astype(bf)
+        fine = (angle - coarse.astype(f32)).astype(bf)
+        row, col = row_ref[:, at].astype(f32).astype(bf), col_ref[:, at].astype(f32).astype(bf)
+        for part, value in enumerate((row, col, coarse, fine, low_ref[:, at], high_ref[:, at])):
+            out_ref[part * PIECE_RUNS + r * DET : part * PIECE_RUNS + (r + 1) * DET] = value
     slots = slot_ref[...]
-    position = jnp.zeros(slots.shape, jnp.float32)
+    position = jnp.zeros(slots.shape, f32)
     for s in range(LISTED):
-        position = jnp.where(slots == s, home_ref[piece_ref[0, s]].astype(jnp.float32), position)
-    float_ref[2 * PIECE_RUNS :] = jnp.concatenate(
-        [position, jnp.zeros((DET, LANE - RUNS), jnp.float32)], axis=1
-    )
-    half_ref[2 * PIECE_RUNS :] = q_ref[...]
+        position = jnp.where(slots == s, home_ref[piece_ref[0, s]].astype(f32), position)
+    wide = jnp.concatenate([position, jnp.zeros((DET, LANE - RUNS), f32)], axis=1)
+    out_ref[SAMPLE_ROWS : SAMPLE_ROWS + 2 * DET] = jnp.concatenate([wide, jnp.zeros_like(wide)], axis=0).astype(bf)
+    out_ref[SAMPLE_ROWS + 2 * DET :] = q_ref[...]
 
 
 def packed(tile_home, piece_list, run_slot, hit_row, hit_col, frac_row, frac_col, angle, quarter):
     return pl.pallas_call(
         pack_kernel,
-        out_shape=(
-            jax.ShapeDtypeStruct((2 * PIECE_RUNS + DET, LANE), jnp.float32),
-            jax.ShapeDtypeStruct((2 * PIECE_RUNS + quarter.shape[0], LANE), jnp.bfloat16),
-        ),
+        out_shape=jax.ShapeDtypeStruct((SAMPLE_ROWS + 2 * DET + quarter.shape[0], LANE), jnp.bfloat16),
         in_specs=[SM, SM] + [VM] * 7,
-        out_specs=(VM,) * 2,
+        out_specs=VM,
         name="pack",
     )(tile_home, piece_list, run_slot, hit_row, hit_col, frac_row, frac_col, angle, quarter)
 
 
 def gather_kernel(
-    float_ref, half_ref,
-    tiles_ref, fo_ref, wo_ref, order_ref,
+    pack_ref,
+    tiles_ref, all_ref, order_ref,
     pos_all, store_sem,
     pos_send, pos_recv, block_send, block_recv, strip_send, strip_recv, core_send, core_recv, hi_send, hi_recv,
 ):
@@ -160,18 +158,17 @@
     def along(direction, jump):
         return (det, tm_of(y, (z + jump) % NZ if direction == 0 else (z + NZ - jump) % NZ, x))
 
-    f_ref, p_ref = float_ref.at[pl.ds(0, 2 * PIECE_RUNS)], float_ref.at[pl.ds(2 * PIECE_RUNS, DET)]
-    w_ref = half_ref.at[pl.ds(0, 2 * PIECE_RUNS)]
-    q_ref = half_ref.at[pl.ds(2 * PIECE_RUNS, TILE_DEV * 3 * STRIP)]
+    samples_ref, p_ref = pack_ref.at[pl.ds(0, SAMPLE_ROWS)], pack_ref.at[pl.ds(SAMPLE_ROWS, 2 * DET)]
+    q_ref = pack_ref.at[pl.ds(SAMPLE_ROWS + 2 * DET, TILE_DEV * 3 * STRIP)]
 
     def strip(slot, d):
         return tiles_ref.at[slot, d]
 
     def block(slot, part):
-        return fo_ref.at[slot, pl.ds(part * PIECE_RUNS, PIECE_RUNS)] if part < 2 else wo_ref.at[slot]
+        return all_ref.at[slot, pl.ds(part * 2 * PIECE_RUNS, 2 * PIECE_RUNS)]
 
     def own_block(part):
-        return float_ref.at[pl.ds(part * PIECE_RUNS, PIECE_RUNS)] if part < 2 else w_ref
+        return pack_ref.at[pl.ds(part * 2 * PIECE_RUNS, 2 * PIECE_RUNS)]
 
     mine = y * NX + x
     greet([along(d, j) for d in (0, 1) for j in (1, 2)] + [(partner, tm), (across, tm)] + far)
@@ -243,16 +240,16 @@
                 send_strip(half, direction, distance)
         to_partner(half, 0, z)
 
-    first_strips(0)
     for k, peer in enumerate(far):
         start(remote(p_ref, pos_all.at[mine], pos_send.at[k], pos_recv.at[k], peer))
+    first_strips(0)
     for part in range(3):
         send_block(1, mine, part, up, True)
         send_block(2, mine, part, down, True)
         send_block(0, mine, part, side, True)
     stores = []
     for i, (src, dst) in enumerate(
-        ((q_ref, strip(z, det)), (f_ref, fo_ref.at[mine]), (w_ref, wo_ref.at[mine]), (p_ref, pos_all.at[mine]))
+        ((q_ref, strip(z, det)), (samples_ref, all_ref.at[mine]), (p_ref, pos_all.at[mine]))
     ):
         copy = pltpu.make_async_copy(src, dst, store_sem.at[i])
         copy.start()
@@ -278,6 +275,11 @@
     def opposite(part):
         wait_block(5, slot_of[5], part)
         send_block(6, slot_of[5], part, side)
+
+    stores[2].wait()
+    for k, peer in enumerate(far):
+        remote(p_ref, pos_all.at[mine], pos_send.at[k], pos_recv.at[k], peer).wait_recv()
+    run_order(pos_all, order_ref, y, x)
 
     near(0)
     remote(q_ref, strip(z, across), hi_send, hi_recv, (across, tm)).wait_recv()
@@ -293,11 +295,6 @@
     take_strip(1, 1)
     take_strip(0, 3)
     take_strip(0, 4)
-
-    stores[3].wait()
-    for k, peer in enumerate(far):
-        remote(p_ref, pos_all.at[mine], pos_send.at[k], pos_recv.at[k], peer).wait_recv()
-    run_order(pos_all, order_ref, y, x)
 
     take_strip(1, 3)
     take_strip(1, 4)
@@ -314,28 +311,26 @@
             remote(
                 q_ref, strip(slot, theirs[half]), core_send.at[half, index], core_recv.at[half, index], (partner, tm)
             ).wait_recv()
-    for copy in stores[:3]:
+    for copy in stores[:2]:
         copy.wait()
     for copy in started:
         copy.wait_send()
 
 
-def gather_all(floats, halves):
-    bf, f32, i32 = jnp.bfloat16, jnp.float32, jnp.int32
-    samples = (2 * PIECE_RUNS, LANE)
+def gather_all(pack):
+    bf, i32 = jnp.bfloat16, jnp.int32
     return pl.pallas_call(
         gather_kernel,
         out_shape=(
             jax.ShapeDtypeStruct((NZ, N_STRIP, TILE_DEV * 3 * STRIP, PIX), bf),
-            jax.ShapeDtypeStruct((NB, *samples), f32),
-            jax.ShapeDtypeStruct((NB, *samples), bf),
+            jax.ShapeDtypeStruct((NB, SAMPLE_ROWS, LANE), bf),
             jax.ShapeDtypeStruct((2 * DET, LANE), i32),
         ),
-        in_specs=[ANY] * 2,
-        out_specs=(ANY, ANY, ANY, VM),
+        in_specs=[ANY],
+        out_specs=(ANY, ANY, VM),
         scratch_shapes=[
-            pltpu.VMEM((NB, DET, LANE), f32),
-            DMA((4,)),
+            pltpu.VMEM((NB, 2 * DET, LANE), bf),
+            DMA((3,)),
             DMA((NB,)),
             DMA((NB,)),
             DMA((7, 3)),
@@ -349,7 +344,7 @@
         ],
         compiler_params=pltpu.CompilerParams(collective_id=0, has_side_effects=True, vmem_limit_bytes=GRANT),
         name="gather_all",
-    )(floats, halves)
+    )(pack)
 
 
 def sin_cos(v):
@@ -389,17 +384,19 @@
     return jnp.concatenate(parts, axis=0)
 
 
-def forward_kernel(list_ref, tiles_ref, f_ref, w_ref, sig_ref, cs_ref, hit_ref, frac_ref):
+def samples_of(all_ref, z, part):
+    rows = slice(part * 2 * PIECE_RUNS, (part + 1) * 2 * PIECE_RUNS)
+    return all_ref[z, rows].astype(jnp.float32).reshape(2, RUNS, DET, LANE)
+
+
+def forward_kernel(list_ref, tiles_ref, all_ref, sig_ref, cs_ref, hit_ref, frac_ref):
     def prepare(z, _):
-        code = f_ref[z, :PIECE_RUNS].reshape(RUNS, DET, LANE)
-        row = jnp.floor(code * (1.0 / PIX))
-        hit_ref[z, 0] = row
-        hit_ref[z, 1] = code - row * PIX
-        sin, cos = sin_cos(2.0 * f_ref[z, PIECE_RUNS:].reshape(RUNS, DET, LANE))
+        hit_ref[z] = samples_of(all_ref, z, 0)
+        halves = samples_of(all_ref, z, 1)
+        sin, cos = sin_cos(2.0 * (halves[0] + halves[1]))
         cs_ref[z, 0] = cos
         cs_ref[z, 1] = sin
-        fracs = w_ref[z].astype(jnp.float32)
-        frac_ref[z] = fracs.reshape(2, RUNS, DET, LANE)
+        frac_ref[z] = samples_of(all_ref, z, 2)
         sig_ref[z] = jnp.zeros_like(sig_ref[z])
         return 0
 
@@ -432,29 +429,25 @@
     lax.fori_loop(0, (count + UNROLL - 1) // UNROLL, body, 0)
 
 
-def forward(order, tiles, floats, fracs):
+def forward(order, tiles, samples):
     f32 = jnp.float32
     block = (NB, DET, RUNS, LANE)
     pair = (NB, 2, RUNS, DET, LANE)
     return pl.pallas_call(
         forward_kernel,
         out_shape=(jax.ShapeDtypeStruct(block, f32), jax.ShapeDtypeStruct(pair, f32)),
-        in_specs=[SM, VM, VM, VM],
+        in_specs=[SM, VM, VM],
         out_specs=(VM, VM),
         scratch_shapes=[pltpu.VMEM(pair, f32), pltpu.VMEM(pair, f32)],
         compiler_params=pltpu.CompilerParams(vmem_limit_bytes=GRANT),
         name="forward",
-    )(order, tiles, floats, fracs)
-
-
-def backward_kernel(list_ref, f_ref, w_ref, cs_ref, filt_ref, acc_ref, hit_ref, frac_ref):
+    )(order, tiles, samples)
+
+
+def backward_kernel(list_ref, all_ref, cs_ref, filt_ref, acc_ref, hit_ref, frac_ref):
     def prepare(z, _):
-        code = f_ref[z, :PIECE_RUNS].reshape(RUNS, DET, LANE)
-        row = jnp.floor(code * (1.0 / PIX))
-        hit_ref[z, 0] = row
-        hit_ref[z, 1] = code - row * PIX
-        fracs = w_ref[z].astype(jnp.float32)
-        frac_ref[z] = fracs.reshape(2, RUNS, DET, LANE)
+        hit_ref[z] = samples_of(all_ref, z, 0)
+        frac_ref[z] = samples_of(all_ref, z, 2)
         return 0
 
     lax.fori_loop(0, NB, prepare, 0)
@@ -491,18 +484,18 @@
     lax.fori_loop(0, (count + UNROLL - 1) // UNROLL, body, 0)
 
 
-def backward(order, floats, fracs, turns, filtered):
+def backward(order, samples, turns, filtered):
     f32 = jnp.float32
     pair = (NB, 2, RUNS, DET, LANE)
     return pl.pallas_call(
         backward_kernel,
         out_shape=jax.ShapeDtypeStruct((TILE_DEV * NZ, 3 * PIX, PIX), f32),
-        in_specs=[SM, VM, VM, VM, VM],
+        in_specs=[SM, VM, VM, VM],
         out_specs=VM,
         scratch_shapes=[pltpu.VMEM(pair, f32), pltpu.VMEM(pair, f32)],
         compiler_params=pltpu.CompilerParams(vmem_limit_bytes=GRANT),
         name="backward",
-    )(order, floats, fracs, turns, filtered)
+    )(order, samples, turns, filtered)
 
 
 def toeplitz(noise_ref, line_ref, hi_ref, lo_ref):
@@ -829,16 +822,16 @@
 def body(
     sky_map, tile_home, piece_tiles, run_slot, hit_row, hit_col, frac_row, frac_col, angle, noise_coef
 ):
-    floats, halves = packed(
+    pack = packed(
         tile_home, piece_tiles.reshape(1, LISTED), run_slot, hit_row, hit_col, frac_row, frac_col, angle,
         sky_map.reshape(TILE_DEV * 3 * STRIP, PIX),
     )
-    tiles, all_floats, all_fracs, order = gather_all(floats, halves)
+    tiles, samples, order = gather_all(pack)
     partial, turns = forward(
-        order, tiles.reshape(NZ, N_STRIP, TILE_DEV, 3 * STRIP, PIX), all_floats, all_fracs
+        order, tiles.reshape(NZ, N_STRIP, TILE_DEV, 3 * STRIP, PIX), samples
     )
     filtered = filtered_of(partial, noise_coef)
-    acc = backward(order, all_floats, all_fracs, turns, filtered)
+    acc = backward(order, samples, turns, filtered)
     return collect(acc)
 
 

time: 91.2 us -> 91.1 us (level); the launches traced: 90 us -> 91 us
  Pallas kernels: 87.5 us -> 89.3 us
    pallas_call x1, Pallas kernels: 21.3 us -> 24.9 us  [collect(): pl.pallas_call(collect_kernel, out_shape=jax.ShapeDtypeStruct(quarter, f3...]
    pallas_call x1, Pallas kernels: 8.45 us -> 6.44 us  [backward(): pl.pallas_call(backward_kernel, out_shape=jax.ShapeDtypeStruct((TILE_DEV...]
    pallas_call x1, Pallas kernels: 8.25 us -> 6.43 us  [forward(): pl.pallas_call(forward_kernel, out_shape=(jax.ShapeDtypeStruct(block, f32...]
    pallas_call x1, Pallas kernels: 21.9 us -> 23.1 us  [filtered_of(): pl.pallas_call(filter_kernel, out_shape=jax.ShapeDtypeStruct((NB, *block)...]
    unnamed x7 -> x5, local copies, waits for them, and re-layouts: 2.45 us -> 1.59 us
where the time goes in v10:
time: 91.1 us; the launch traced here: 91 us
  Pallas kernels  89.3 us (98%)
  local copies, waits for them, and re-layouts  1.59 us (2%)
    pallas_call x1, Pallas kernels, gather_all(): pl.pallas_call(gather_kernel, out_shape=(jax.ShapeDtypeStruct((NZ, N_STRI...  26.7 us
    pallas_call x1, Pallas kernels, collect(): pl.pallas_call(collect_kernel, out_shape=jax.ShapeDtypeStruct(quarter, f3...  24.9 us
    pallas_call x1, Pallas kernels, filtered_of(): pl.pallas_call(filter_kernel, out_shape=jax.ShapeDtypeStruct((NB, *block)...  23.1 us
    pallas_call x1, Pallas kernels, backward(): pl.pallas_call(backward_kernel, out_shape=jax.ShapeDtypeStruct((TILE_DEV...  6.44 us
    pallas_call x1, Pallas kernels, forward(): pl.pallas_call(forward_kernel, out_shape=(jax.ShapeDtypeStruct(block, f32...  6.43 us

profile of v10, /device:TPU:1, one launch (start us, length us, event | category | flops | bytes accessed | tf_op | source)
XLA Modules:
  0.0 91.0 jit_solution(17723533342227919441)
XLA Ops:
  0.0 1.7 %pack.1.pack_ref = bf16[976,128]{1,0:T(8,128)(2,1)} custom-call(s32[128]{0:T(128)} %home_ref.1, s32[1,32]{1,0:T(1,128)} %bitcast.7, s32[8,16]{1,0:T(8,128)} %slot_ref.1, s32[8,2048]{1,0:T(8,128)} %row_ref.1, s32[8,2048]{1,0:T(8,128)} %col_ref.1, bf16[8,2048]{1,0:T(8,128)(2,1)} %low_ref.1, bf16[8,2048]{1,0:T(8,128)(2,1)} %high_ref.1, f32[8,2048]{1,0:T(8,128)} %angle_ref.1, ...), custom_call_target="tpu_custom_call" | custom-call | tf_op jit(solution)/shard_map/pack/pallas_call | solution.py:135
  1.7 0.0 copy-start
  1.7 0.9 %copy-done = bf16[976,128]{1,0:T(8,128)(2,1)S(1)} copy-done((bf16[976,128]{1,0:T(8,128)(2,1)S(1)}, bf16[976,128]{1,0:T(8,128)(2,1)}, u32[]{:S(2)}) %copy-start) | copy-done | bytes 249880
  2.6 26.7 %gather_all.1 = (bf16[8,4,192,128]{3,2,1,0:T(8,128)(2,1)S(1)}, bf16[8,768,128]{2,1,0:T(8,128)(2,1)S(1)}, s32[16,128]{1,0:T(8,128)S(1)}) custom-call(bf16[976,128]{1,0:T(8,128)(2,1)S(1)} %copy-done), custom_call_target="tpu_custom_call" | custom-call | tf_op jit(solution)/shard_map/gather_all/pallas_call | solution.py:322
  29.4 0.0 copy-start.1
  29.4 6.4 %forward.1 = (f32[8,8,16,128]{3,2,1,0:T(8,128)S(1)}, f32[8,2,16,8,128]{4,3,2,1,0:T(8,128)S(1)}) custom-call(s32[16,128]{1,0:T(8,128)S(1)} %get-tuple-element.10.list_ref, bf16[8,4,2,96,128]{4,3,2,1,0:T(8,128)(2,1)S(1)} %bitcast.5, bf16[8,768,128]{2,1,0:T(8,128)(2,1)S(1)} %get-tuple-element.11.all_ref), custom_call_target="tpu_custom_call" | custom-call | tf_op jit(solution)/shard_map/forward/pallas_call | solution.py:436
  35.8 0.0 copy-done.1
  35.8 23.1 %filter.1.filt_ref = f32[8,8,16,128]{3,2,1,0:T(8,128)S(1)} custom-call(f32[8,8,16,128]{3,2,1,0:T(8,128)S(1)} %get-tuple-element.14.part_ref, f32[8,1025]{1,0:T(8,128)S(1)} %copy-done.1), custom_call_target="tpu_custom_call" | custom-call | tf_op jit(solution)/shard_map/filter/pallas_call | solution.py:660
  59.0 6.4 %backward.1 = f32[16,384,128]{2,1,0:T(8,128)S(1)} custom-call(s32[16,128]{1,0:T(8,128)S(1)} %get-tuple-element.10.list_ref, bf16[8,768,128]{2,1,0:T(8,128)(2,1)S(1)} %get-tuple-element.11.all_ref, f32[8,2,16,8,128]{4,3,2,1,0:T(8,128)S(1)} %get-tuple-element.13.cs_ref, f32[8,8,16,128]{3,2,1,0:T(8,128)S(1)} %filter.1.filt_ref), custom_call_target="tpu_custom_call" | custom-call | tf_op jit(solution)/shard_map/backward/pallas_call | solution.py:490
  65.4 24.9 %collect.1 = f32[2,3,32,128]{3,2,1,0:T(8,128)S(1)} custom-call(f32[8,2,3,2,2,32,128]{6,5,4,3,2,1,0:T(8,128)S(1)} %bitcast.4), custom_call_target="tpu_custom_call" | custom-call | tf_op jit(solution)/shard_map/collect/pallas_call | solution.py:797
  90.3 0.6 copy.12
Async XLA Ops:
  1.7 0.9 %copy-start = (bf16[976,128]{1,0:T(8,128)(2,1)S(1)}, bf16[976,128]{1,0:T(8,128)(2,1)}, u32[]{:S(2)}) copy-start(bf16[976,128]{1,0:T(8,128)(2,1)} %pack.1.pack_ref) | copy-start | bytes 749572
  29.4 6.4 %copy-start.1 = (f32[8,1025]{1,0:T(8,128)S(1)}, f32[8,1025]{1,0:T(8,128)}, u32[]{:S(2)}) copy-start(f32[8,1025]{1,0:T(8,128)} %noise_ref.1) | copy-start | bytes 98404

commit v11 on v10

--- a/solution.py
+++ b/solution.py
@@ -20,7 +20,7 @@
 REACH = 8
 UNROLL = 16
 HALF = 16
-SENT = 2
+SENT = 4
 PIECE_RUNS = DET * RUNS
 ALL_RUNS = NB * PIECE_RUNS
 SAMPLE_ROWS = 6 * PIECE_RUNS

time: 91.1 us -> 88.7 us (0.974)
  Pallas kernels: 89.3 us -> 86.3 us
    pallas_call x1, Pallas kernels: 24.9 us -> 22.7 us  [collect(): pl.pallas_call(collect_kernel, out_shape=jax.ShapeDtypeStruct(quarter, f3...]
    pallas_call x1, Pallas kernels: 23.1 us -> 21 us  [filtered_of(): pl.pallas_call(filter_kernel, out_shape=jax.ShapeDtypeStruct((NB, *block)...]
where the time goes in v11:
time: 88.7 us; the launch traced here: 88 us
  Pallas kernels  86.3 us (97%)
  local copies, waits for them, and re-layouts  1.59 us (2%)
    pallas_call x1, Pallas kernels, gather_all(): pl.pallas_call(gather_kernel, out_shape=(jax.ShapeDtypeStruct((NZ, N_STRI...  26.7 us
    pallas_call x1, Pallas kernels, collect(): pl.pallas_call(collect_kernel, out_shape=jax.ShapeDtypeStruct(quarter, f3...  22.7 us
    pallas_call x1, Pallas kernels, filtered_of(): pl.pallas_call(filter_kernel, out_shape=jax.ShapeDtypeStruct((NB, *block)...  21 us
    pallas_call x1, Pallas kernels, backward(): pl.pallas_call(backward_kernel, out_shape=jax.ShapeDtypeStruct((TILE_DEV...  7.11 us
    pallas_call x1, Pallas kernels, forward(): pl.pallas_call(forward_kernel, out_shape=(jax.ShapeDtypeStruct(block, f32...  7.04 us

profile of v11, /device:TPU:1, one launch (start us, length us, event | category | flops | bytes accessed | tf_op | source)
XLA Modules:
  0.0 88.0 jit_solution(5009082284909794445)
XLA Ops:
  0.0 1.7 %pack.1.pack_ref = bf16[976,128]{1,0:T(8,128)(2,1)} custom-call(s32[128]{0:T(128)} %home_ref.1, s32[1,32]{1,0:T(1,128)} %bitcast.7, s32[8,16]{1,0:T(8,128)} %slot_ref.1, s32[8,2048]{1,0:T(8,128)} %row_ref.1, s32[8,2048]{1,0:T(8,128)} %col_ref.1, bf16[8,2048]{1,0:T(8,128)(2,1)} %low_ref.1, bf16[8,2048]{1,0:T(8,128)(2,1)} %high_ref.1, f32[8,2048]{1,0:T(8,128)} %angle_ref.1, ...), custom_call_target="tpu_custom_call" | custom-call | tf_op jit(solution)/shard_map/pack/pallas_call | solution.py:135
  1.7 0.0 copy-start
  1.7 0.9 %copy-done = bf16[976,128]{1,0:T(8,128)(2,1)S(1)} copy-done((bf16[976,128]{1,0:T(8,128)(2,1)S(1)}, bf16[976,128]{1,0:T(8,128)(2,1)}, u32[]{:S(2)}) %copy-start) | copy-done | bytes 249880
  2.6 26.7 %gather_all.1 = (bf16[8,4,192,128]{3,2,1,0:T(8,128)(2,1)S(1)}, bf16[8,768,128]{2,1,0:T(8,128)(2,1)S(1)}, s32[16,128]{1,0:T(8,128)S(1)}) custom-call(bf16[976,128]{1,0:T(8,128)(2,1)S(1)} %copy-done), custom_call_target="tpu_custom_call" | custom-call | tf_op jit(solution)/shard_map/gather_all/pallas_call | solution.py:322
  29.4 0.0 copy-start.1
  29.4 7.0 %forward.1 = (f32[8,8,16,128]{3,2,1,0:T(8,128)S(1)}, f32[8,2,16,8,128]{4,3,2,1,0:T(8,128)S(1)}) custom-call(s32[16,128]{1,0:T(8,128)S(1)} %get-tuple-element.10.list_ref, bf16[8,4,2,96,128]{4,3,2,1,0:T(8,128)(2,1)S(1)} %bitcast.5, bf16[8,768,128]{2,1,0:T(8,128)(2,1)S(1)} %get-tuple-element.11.all_ref), custom_call_target="tpu_custom_call" | custom-call | tf_op jit(solution)/shard_map/forward/pallas_call | solution.py:436
  36.4 0.0 copy-done.1
  36.4 21.0 %filter.1.filt_ref = f32[8,8,16,128]{3,2,1,0:T(8,128)S(1)} custom-call(f32[8,8,16,128]{3,2,1,0:T(8,128)S(1)} %get-tuple-element.14.part_ref, f32[8,1025]{1,0:T(8,128)S(1)} %copy-done.1), custom_call_target="tpu_custom_call" | custom-call | tf_op jit(solution)/shard_map/filter/pallas_call | solution.py:660
  57.5 7.1 %backward.1 = f32[16,384,128]{2,1,0:T(8,128)S(1)} custom-call(s32[16,128]{1,0:T(8,128)S(1)} %get-tuple-element.10.list_ref, bf16[8,768,128]{2,1,0:T(8,128)(2,1)S(1)} %get-tuple-element.11.all_ref, f32[8,2,16,8,128]{4,3,2,1,0:T(8,128)S(1)} %get-tuple-element.13.cs_ref, f32[8,8,16,128]{3,2,1,0:T(8,128)S(1)} %filter.1.filt_ref), custom_call_target="tpu_custom_call" | custom-call | tf_op jit(solution)/shard_map/backward/pallas_call | solution.py:490
  64.6 22.7 %collect.1 = f32[2,3,32,128]{3,2,1,0:T(8,128)S(1)} custom-call(f32[8,2,3,2,2,32,128]{6,5,4,3,2,1,0:T(8,128)S(1)} %bitcast.4), custom_call_target="tpu_custom_call" | custom-call | tf_op jit(solution)/shard_map/collect/pallas_call | solution.py:797
  87.3 0.6 copy.12
Async XLA Ops:
  1.7 0.9 %copy-start = (bf16[976,128]{1,0:T(8,128)(2,1)S(1)}, bf16[976,128]{1,0:T(8,128)(2,1)}, u32[]{:S(2)}) copy-start(bf16[976,128]{1,0:T(8,128)(2,1)} %pack.1.pack_ref) | copy-start | bytes 749572
  29.4 7.1 %copy-start.1 = (f32[8,1025]{1,0:T(8,128)S(1)}, f32[8,1025]{1,0:T(8,128)}, u32[]{:S(2)}) copy-start(f32[8,1025]{1,0:T(8,128)} %noise_ref.1) | copy-start | bytes 98404

commit v12 on v11

--- a/solution.py
+++ b/solution.py
@@ -276,11 +276,6 @@
         wait_block(5, slot_of[5], part)
         send_block(6, slot_of[5], part, side)
 
-    stores[2].wait()
-    for k, peer in enumerate(far):
-        remote(p_ref, pos_all.at[mine], pos_send.at[k], pos_recv.at[k], peer).wait_recv()
-    run_order(pos_all, order_ref, y, x)
-
     near(0)
     remote(q_ref, strip(z, across), hi_send, hi_recv, (across, tm)).wait_recv()
     first_strips(1)
@@ -295,6 +290,11 @@
     take_strip(1, 1)
     take_strip(0, 3)
     take_strip(0, 4)
+
+    stores[2].wait()
+    for k, peer in enumerate(far):
+        remote(p_ref, pos_all.at[mine], pos_send.at[k], pos_recv.at[k], peer).wait_recv()
+    run_order(pos_all, order_ref, y, x)
 
     take_strip(1, 3)
     take_strip(1, 4)

time: 88.7 us -> 87.9 us (level)
    pallas_call x1, Pallas kernels: 22.7 us -> 20.6 us  [collect(): pl.pallas_call(collect_kernel, out_shape=jax.ShapeDtypeStruct(quarter, f3...]
    pallas_call x1, Pallas kernels: 21 us -> 22.2 us  [filtered_of(): pl.pallas_call(filter_kernel, out_shape=jax.ShapeDtypeStruct((NB, *block)...]
where the time goes in v12:
time: 87.9 us; the launch traced here: 87.5 us
  Pallas kernels  85.9 us (98%)
  local copies, waits for them, and re-layouts  1.59 us (2%)
    pallas_call x1, Pallas kernels, gather_all(): pl.pallas_call(gather_kernel, out_shape=(jax.ShapeDtypeStruct((NZ, N_STRI...  25.9 us
    pallas_call x1, Pallas kernels, filtered_of(): pl.pallas_call(filter_kernel, out_shape=jax.ShapeDtypeStruct((NB, *block)...  22.2 us
    pallas_call x1, Pallas kernels, collect(): pl.pallas_call(collect_kernel, out_shape=jax.ShapeDtypeStruct(quarter, f3...  20.6 us
    pallas_call x1, Pallas kernels, backward(): pl.pallas_call(backward_kernel, out_shape=jax.ShapeDtypeStruct((TILE_DEV...  7.77 us
    pallas_call x1, Pallas kernels, forward(): pl.pallas_call(forward_kernel, out_shape=(jax.ShapeDtypeStruct(block, f32...  7.64 us

profile of v12, /device:TPU:1, one launch (start us, length us, event | category | flops | bytes accessed | tf_op | source)
XLA Modules:
  0.0 87.5 jit_solution(4917692066874763568)
XLA Ops:
  0.0 1.7 %pack.1.pack_ref = bf16[976,128]{1,0:T(8,128)(2,1)} custom-call(s32[128]{0:T(128)} %home_ref.1, s32[1,32]{1,0:T(1,128)} %bitcast.7, s32[8,16]{1,0:T(8,128)} %slot_ref.1, s32[8,2048]{1,0:T(8,128)} %row_ref.1, s32[8,2048]{1,0:T(8,128)} %col_ref.1, bf16[8,2048]{1,0:T(8,128)(2,1)} %low_ref.1, bf16[8,2048]{1,0:T(8,128)(2,1)} %high_ref.1, f32[8,2048]{1,0:T(8,128)} %angle_ref.1, ...), custom_call_target="tpu_custom_call" | custom-call | tf_op jit(solution)/shard_map/pack/pallas_call | solution.py:135
  1.7 0.0 copy-start
  1.7 0.9 %copy-done = bf16[976,128]{1,0:T(8,128)(2,1)S(1)} copy-done((bf16[976,128]{1,0:T(8,128)(2,1)S(1)}, bf16[976,128]{1,0:T(8,128)(2,1)}, u32[]{:S(2)}) %copy-start) | copy-done | bytes 249880
  2.6 25.9 %gather_all.1 = (bf16[8,4,192,128]{3,2,1,0:T(8,128)(2,1)S(1)}, bf16[8,768,128]{2,1,0:T(8,128)(2,1)S(1)}, s32[16,128]{1,0:T(8,128)S(1)}) custom-call(bf16[976,128]{1,0:T(8,128)(2,1)S(1)} %copy-done), custom_call_target="tpu_custom_call" | custom-call | tf_op jit(solution)/shard_map/gather_all/pallas_call | solution.py:322
  28.6 0.0 copy-start.1
  28.6 7.6 %forward.1 = (f32[8,8,16,128]{3,2,1,0:T(8,128)S(1)}, f32[8,2,16,8,128]{4,3,2,1,0:T(8,128)S(1)}) custom-call(s32[16,128]{1,0:T(8,128)S(1)} %get-tuple-element.10.list_ref, bf16[8,4,2,96,128]{4,3,2,1,0:T(8,128)(2,1)S(1)} %bitcast.5, bf16[8,768,128]{2,1,0:T(8,128)(2,1)S(1)} %get-tuple-element.11.all_ref), custom_call_target="tpu_custom_call" | custom-call | tf_op jit(solution)/shard_map/forward/pallas_call | solution.py:436
  36.2 0.0 copy-done.1
  36.2 22.2 %filter.1.filt_ref = f32[8,8,16,128]{3,2,1,0:T(8,128)S(1)} custom-call(f32[8,8,16,128]{3,2,1,0:T(8,128)S(1)} %get-tuple-element.14.part_ref, f32[8,1025]{1,0:T(8,128)S(1)} %copy-done.1), custom_call_target="tpu_custom_call" | custom-call | tf_op jit(solution)/shard_map/filter/pallas_call | solution.py:660
  58.5 7.8 %backward.1 = f32[16,384,128]{2,1,0:T(8,128)S(1)} custom-call(s32[16,128]{1,0:T(8,128)S(1)} %get-tuple-element.10.list_ref, bf16[8,768,128]{2,1,0:T(8,128)(2,1)S(1)} %get-tuple-element.11.all_ref, f32[8,2,16,8,128]{4,3,2,1,0:T(8,128)S(1)} %get-tuple-element.13.cs_ref, f32[8,8,16,128]{3,2,1,0:T(8,128)S(1)} %filter.1.filt_ref), custom_call_target="tpu_custom_call" | custom-call | tf_op jit(solution)/shard_map/backward/pallas_call | solution.py:490
  66.3 20.6 %collect.1 = f32[2,3,32,128]{3,2,1,0:T(8,128)S(1)} custom-call(f32[8,2,3,2,2,32,128]{6,5,4,3,2,1,0:T(8,128)S(1)} %bitcast.4), custom_call_target="tpu_custom_call" | custom-call | tf_op jit(solution)/shard_map/collect/pallas_call | solution.py:797
  86.9 0.6 copy.12
Async XLA Ops:
  1.7 0.9 %copy-start = (bf16[976,128]{1,0:T(8,128)(2,1)S(1)}, bf16[976,128]{1,0:T(8,128)(2,1)}, u32[]{:S(2)}) copy-start(bf16[976,128]{1,0:T(8,128)(2,1)} %pack.1.pack_ref) | copy-start | bytes 749572
  28.6 7.7 %copy-start.1 = (f32[8,1025]{1,0:T(8,128)S(1)}, f32[8,1025]{1,0:T(8,128)}, u32[]{:S(2)}) copy-start(f32[8,1025]{1,0:T(8,128)} %noise_ref.1) | copy-start | bytes 98404

commit v13 on v12

--- a/solution.py
+++ b/solution.py
@@ -769,7 +769,7 @@
                 else:
                     start(last_hop(direction, c, 1))
                     start(last_hop(direction, c, 0))
-        if step == 1:
+        if step == HALF_Z - 1:
             swapped(last)
             for t in range(TILE_DEV):
                 for p in range(3):

time: 87.9 us -> 89.3 us (1.016)
  Pallas kernels: 85.9 us -> 87.5 us
    pallas_call x1, Pallas kernels: 22.2 us -> 25.8 us  [filtered_of(): pl.pallas_call(filter_kernel, out_shape=jax.ShapeDtypeStruct((NB, *block)...]
    pallas_call x1, Pallas kernels: 20.6 us -> 23.8 us  [collect(): pl.pallas_call(collect_kernel, out_shape=jax.ShapeDtypeStruct(quarter, f3...]
    pallas_call x1, Pallas kernels: 7.77 us -> 5.11 us  [backward(): pl.pallas_call(backward_kernel, out_shape=jax.ShapeDtypeStruct((TILE_DEV...]
    pallas_call x1, Pallas kernels: 7.64 us -> 5.2 us  [forward(): pl.pallas_call(forward_kernel, out_shape=(jax.ShapeDtypeStruct(block, f32...]
where the time goes in v13:
time: 89.3 us; the launch traced here: 89.2 us
  Pallas kernels  87.5 us (98%)
  local copies, waits for them, and re-layouts  1.59 us (2%)
    pallas_call x1, Pallas kernels, gather_all(): pl.pallas_call(gather_kernel, out_shape=(jax.ShapeDtypeStruct((NZ, N_STRI...  25.9 us
    pallas_call x1, Pallas kernels, filtered_of(): pl.pallas_call(filter_kernel, out_shape=jax.ShapeDtypeStruct((NB, *block)...  25.8 us
    pallas_call x1, Pallas kernels, collect(): pl.pallas_call(collect_kernel, out_shape=jax.ShapeDtypeStruct(quarter, f3...  23.8 us
    pallas_call x1, Pallas kernels, forward(): pl.pallas_call(forward_kernel, out_shape=(jax.ShapeDtypeStruct(block, f32...  5.2 us
    pallas_call x1, Pallas kernels, backward(): pl.pallas_call(backward_kernel, out_shape=jax.ShapeDtypeStruct((TILE_DEV...  5.11 us

profile of v13, /device:TPU:1, one launch (start us, length us, event | category | flops | bytes accessed | tf_op | source)
XLA Modules:
  0.0 89.2 jit_solution(9253464406277067391)
XLA Ops:
  0.0 1.7 %pack.1.pack_ref = bf16[976,128]{1,0:T(8,128)(2,1)} custom-call(s32[128]{0:T(128)} %home_ref.1, s32[1,32]{1,0:T(1,128)} %bitcast.7, s32[8,16]{1,0:T(8,128)} %slot_ref.1, s32[8,2048]{1,0:T(8,128)} %row_ref.1, s32[8,2048]{1,0:T(8,128)} %col_ref.1, bf16[8,2048]{1,0:T(8,128)(2,1)} %low_ref.1, bf16[8,2048]{1,0:T(8,128)(2,1)} %high_ref.1, f32[8,2048]{1,0:T(8,128)} %angle_ref.1, ...), custom_call_target="tpu_custom_call" | custom-call | tf_op jit(solution)/shard_map/pack/pallas_call | solution.py:135
  1.7 0.0 copy-start
  1.7 0.9 %copy-done = bf16[976,128]{1,0:T(8,128)(2,1)S(1)} copy-done((bf16[976,128]{1,0:T(8,128)(2,1)S(1)}, bf16[976,128]{1,0:T(8,128)(2,1)}, u32[]{:S(2)}) %copy-start) | copy-done | bytes 249880
  2.6 25.9 %gather_all.1 = (bf16[8,4,192,128]{3,2,1,0:T(8,128)(2,1)S(1)}, bf16[8,768,128]{2,1,0:T(8,128)(2,1)S(1)}, s32[16,128]{1,0:T(8,128)S(1)}) custom-call(bf16[976,128]{1,0:T(8,128)(2,1)S(1)} %copy-done), custom_call_target="tpu_custom_call" | custom-call | tf_op jit(solution)/shard_map/gather_all/pallas_call | solution.py:322
  28.6 0.0 copy-start.1
  28.6 5.2 %forward.1 = (f32[8,8,16,128]{3,2,1,0:T(8,128)S(1)}, f32[8,2,16,8,128]{4,3,2,1,0:T(8,128)S(1)}) custom-call(s32[16,128]{1,0:T(8,128)S(1)} %get-tuple-element.10.list_ref, bf16[8,4,2,96,128]{4,3,2,1,0:T(8,128)(2,1)S(1)} %bitcast.5, bf16[8,768,128]{2,1,0:T(8,128)(2,1)S(1)} %get-tuple-element.11.all_ref), custom_call_target="tpu_custom_call" | custom-call | tf_op jit(solution)/shard_map/forward/pallas_call | solution.py:436
  33.8 0.0 copy-done.1
  33.8 25.8 %filter.1.filt_ref = f32[8,8,16,128]{3,2,1,0:T(8,128)S(1)} custom-call(f32[8,8,16,128]{3,2,1,0:T(8,128)S(1)} %get-tuple-element.14.part_ref, f32[8,1025]{1,0:T(8,128)S(1)} %copy-done.1), custom_call_target="tpu_custom_call" | custom-call | tf_op jit(solution)/shard_map/filter/pallas_call | solution.py:660
  59.6 5.1 %backward.1 = f32[16,384,128]{2,1,0:T(8,128)S(1)} custom-call(s32[16,128]{1,0:T(8,128)S(1)} %get-tuple-element.10.list_ref, bf16[8,768,128]{2,1,0:T(8,128)(2,1)S(1)} %get-tuple-element.11.all_ref, f32[8,2,16,8,128]{4,3,2,1,0:T(8,128)S(1)} %get-tuple-element.13.cs_ref, f32[8,8,16,128]{3,2,1,0:T(8,128)S(1)} %filter.1.filt_ref), custom_call_target="tpu_custom_call" | custom-call | tf_op jit(solution)/shard_map/backward/pallas_call | solution.py:490
  64.8 23.8 %collect.1 = f32[2,3,32,128]{3,2,1,0:T(8,128)S(1)} custom-call(f32[8,2,3,2,2,32,128]{6,5,4,3,2,1,0:T(8,128)S(1)} %bitcast.4), custom_call_target="tpu_custom_call" | custom-call | tf_op jit(solution)/shard_map/collect/pallas_call | solution.py:797
  88.6 0.6 copy.12
Async XLA Ops:
  1.7 0.9 %copy-start = (bf16[976,128]{1,0:T(8,128)(2,1)S(1)}, bf16[976,128]{1,0:T(8,128)(2,1)}, u32[]{:S(2)}) copy-start(bf16[976,128]{1,0:T(8,128)(2,1)} %pack.1.pack_ref) | copy-start | bytes 749572
  28.6 5.2 %copy-start.1 = (f32[8,1025]{1,0:T(8,128)S(1)}, f32[8,1025]{1,0:T(8,128)}, u32[]{:S(2)}) copy-start(f32[8,1025]{1,0:T(8,128)} %noise_ref.1) | copy-start | bytes 98404
